TPU v7x, 32 devices: a whole 2x2x4 slice. The times are simulated.
32 devices in a mesh: ctx: 4 (over y, x), mp: 8 (over z, core).
Axes of the slice: x: 2, y: 2, z: 4, core: 2. Of those that a mesh axis runs over, the one named last changes fastest.
Arguments:
- tokens: bfloat16 [768, 8192], P('ctx'), may hold values from -120 to 120
- norm_gain: float32 [8192], replicated, may hold values from 0.1 to 1.9
- in_weight: bfloat16 [8192, 3, 8192], P(None, None, 'mp'), may hold values from -0.0625 to 0.0625
- short_filter: float32 [3, 3, 8192], P(None, None, 'mp'), may hold values from -3 to 3
- rates: float32 [16, 8192], P(None, 'mp'), may hold values from 0.00013020834 to 0.020833334
- residues: float32 [16, 8192], P(None, 'mp'), may hold values from -4 to 4
- skip: float32 [8192], P('mp'), may hold values from -4 to 4
- out_weight: bfloat16 [8192, 8192], P('mp'), may hold values from -0.09375 to 0.09375
- segment_ids: int32 [768], replicated, may hold values from 0 to 3, never falling along the last dimension, each value on 1 to 576 neighbouring positions
Outputs:
- mixed: bfloat16 [768, 8192], P('ctx', 'mp')
Inputs may be any that keep to these rules, and one draw needn't show every extreme that they name: `segment_ids`: never falls along the sequence; each document spans 1 to 576 positions.
All inputs are finite; a program needn't handle non-finite values.
Results may differ from a plain program's by a relative error of at most 0.0085.
Values may be sent and summed in bfloat16 or wider, within the bound.
No kernel may reach another device: no remote copies, remote signals or barrier semaphores. Data moves between devices by JAX's collectives and lax.ppermute only.
A program may use at most 192 MiB of HBM per device.

v0:
```python
import functools
import jax
import jax.numpy as jnp
from jax import lax
from jax.experimental import pallas as pl
from jax.experimental.pallas import tpu as pltpu
from jax.sharding import PartitionSpec as P

epsilon = 1e-06
f32 = jnp.float32
bf16 = jnp.bfloat16

PARTS = 8
HEAD = 16
MIB = 1 << 20


def vmem():
    return pl.BlockSpec(memory_space=pltpu.VMEM)


def smem():
    return pl.BlockSpec(memory_space=pltpu.SMEM)


def same_id(ids_ref, a, b):
    def get(t):
        return jnp.where(t < 0, -1, ids_ref[jnp.maximum(t, 0)])

    return (get(a) == get(b)).astype(f32)


def hbm():
    return pl.BlockSpec(memory_space=pltpu.HBM)


def front_kernel(
    geometry, position, ids_ref, tokens_ref, gain_ref, weight_ref, taps_ref, rates_ref, residues_ref, skip_ref,
    query_out, prod_out, block_out, keep_out, visible_out, taps, rates, residues, skip,
    ids, gain, tok, normed, ring, total, proj, head, idcol, near, twice, ending, sem, tok_sem, ring_sem,
):
    T, depth, channels, cb_size, kc_size, slots, poles = geometry
    run = T // PARTS
    kcs, cbs = depth // kc_size, channels // cb_size
    steps = kcs * cbs
    base = pl.multiple_of(position[0] * T, 8)

    def fetch(step):
        cb, kc, slot = step // kcs, step % kcs, step % slots
        return pltpu.make_async_copy(
            weight_ref.at[:, pl.ds(pl.multiple_of(kc * kc_size, kc_size), kc_size),
                          pl.ds(pl.multiple_of(cb * cb_size, cb_size), cb_size)],
            ring.at[slot], ring_sem.at[slot])

    small = [
        pltpu.make_async_copy(a, b, sem.at[i])
        for i, (a, b) in enumerate(
            ((ids_ref, ids), (gain_ref, gain), (taps_ref, taps), (rates_ref, rates), (residues_ref, residues),
             (skip_ref, skip)))
    ]
    small[0].start()
    small[1].start()
    chunk = T // 4
    tok_copies = [
        pltpu.make_async_copy(tokens_ref.at[pl.ds(c * chunk, chunk)], tok.at[pl.ds(c * chunk, chunk)], tok_sem.at[c])
        for c in range(4)
    ]
    for copy in tok_copies:
        copy.start()
    for copy in small[2:]:
        copy.start()
    for s in range(min(slots, steps)):
        fetch(s).start()

    small[0].wait()
    idcol[0:8, :] = jnp.full((8, 128), -1.0, f32)
    for b in range(ids.shape[0]):
        row = ids[b : b + 1, :].astype(f32)
        idcol[8 + b * 128 : 8 + (b + 1) * 128, :] = jnp.broadcast_to(row, (128, 128)).T
    near[...] = idcol[pl.ds(base, T + 8), :]
    here = near[8 : 8 + T, :]
    keep_out[...] = (here == near[7 : 7 + T, :]).astype(f32)
    twice[...] = (here == near[6 : 6 + T, :]).astype(f32)
    ending[...] = (here == near[7 + T : 8 + T, :]).astype(f32)
    before = near[pl.ds(7, PARTS, stride=run), :]
    for i in range(run):
        visible_out[i * 8 : (i + 1) * 8, :] = (near[pl.ds(8 + i, PARTS, stride=run), :] == before).astype(f32)
    for i in range(3):
        proj[i, 0:8, :] = jnp.zeros((8, cb_size), f32)
    head[...] = jnp.zeros(head.shape, f32)
    small[1].wait()

    def norm_rows(g, _):
        part = pl.ds(pl.multiple_of(g * 16, 16), 16)
        x = tok[part, :].astype(f32)
        scale = lax.rsqrt(jnp.sum(x * x, axis=-1, keepdims=True) * (1.0 / depth) + epsilon)
        normed[part, :] = (x * scale * gain[...]).astype(bf16)
        return 0

    for c, copy in enumerate(tok_copies):
        copy.wait()
        lax.fori_loop(c * chunk // 16, (c + 1) * chunk // 16, norm_rows, 0)
    for copy in small[2:]:
        copy.wait()

    def epilogue(cb):
        cols = pl.ds(pl.multiple_of(cb * cb_size, cb_size), cb_size)
        feats = []
        m1 = jnp.concatenate([keep_out[...]] * (cb_size // 128), axis=1)
        m2 = jnp.concatenate([twice[...]] * (cb_size // 128), axis=1)
        for i in range(3):
            p = total[i].astype(bf16).astype(f32)
            proj[i, 8 : 8 + T, :] = p
            tap = [taps[j, i : i + 1, cols] for j in range(3)]
            feats.append(
                tap[0] * p + m1 * (tap[1] * proj[i, 7 : 7 + T, :]) + m2 * (tap[2] * proj[i, 6 : 6 + T, :]))
        query_out[:, cols] = feats[0]
        for i in range(1, 3):
            head[2 * (i - 1) : 2 * i, :] = proj[i, 8:10, :]
        for i in range(3):
            head[4 + 2 * i : 6 + 2 * i, :] = proj[i, 6 + T : 8 + T, :]
        block_out[poles : poles + HEAD, cols] = head[...].astype(bf16)
        product = feats[1] * feats[2]
        back = 7.0 - lax.broadcasted_iota(jnp.int32, (8, 128), 0).astype(f32)
        for lane in range(cb_size // 128):
            tile = cb * (cb_size // 128) + lane
            lanes = pl.ds(pl.multiple_of(tile * 128, 128), 128)
            prod_out[tile] = product[:, lane * 128 : lane * 128 + 128]
            r16 = rates[:, lanes]
            jump = jnp.exp(-8.0 * r16)
            leap = [jnp.broadcast_to(jump[n : n + 1], (8, 128)) for n in range(poles)]

            def eight(g, sums):
                part = pl.ds(pl.multiple_of(g * 8, 8), 8)
                p = prod_out[tile, part, :] * ending[part, :]
                return tuple(sums[n] * leap[n] + p for n in range(poles))

            sums = lax.fori_loop(
                0, T // 8, eight, tuple(jnp.zeros((8, 128), f32) for _ in range(poles)), unroll=4)
            ends = [
                jnp.sum(sums[n] * jnp.exp(-back * r16[n : n + 1]), axis=0, keepdims=True) for n in range(poles)
            ]
            block_out[0:poles, lanes] = jnp.concatenate(ends, axis=0).astype(bf16)

    def step_body(step, _):
        cb, kc, slot = step // kcs, step % kcs, step % slots
        fetch(step).wait()
        lhs = normed[:, pl.ds(pl.multiple_of(kc * kc_size, kc_size), kc_size)]
        for i in range(3):
            part = jnp.dot(lhs, ring[slot, i], preferred_element_type=f32)
            total[i] = jnp.where(kc == 0, part, total[i] + part)

        @pl.when(step + slots < steps)
        def _():
            fetch(step + slots).start()

        @pl.when(kc == kcs - 1)
        def _():
            epilogue(cb)

        return 0

    total[...] = jnp.zeros(total.shape, f32)
    lax.fori_loop(0, steps, step_body, 0)


def front(position, ids2, tokens, gain, weight3, taps, rates, residues, skip):
    T, depth = tokens.shape
    channels, poles = weight3.shape[2], rates.shape[0]
    cb_size, kc_size, slots = 256, 2048, 5
    geometry = (T, depth, channels, cb_size, kc_size, slots, poles)
    kept = [pltpu.VMEM(a.shape, a.dtype) for a in (taps, rates, residues, skip)]
    ids2, tokens, gain, weight3, taps, rates, residues, skip = [
        pltpu.with_memory_space_constraint(a, pltpu.HBM)
        for a in (ids2, tokens, gain, weight3, taps, rates, residues, skip)
    ]
    return pl.pallas_call(
        functools.partial(front_kernel, geometry),
        out_shape=[
            jax.ShapeDtypeStruct((T, channels), f32),
            jax.ShapeDtypeStruct((channels // 128, T, 128), f32),
            jax.ShapeDtypeStruct((poles + HEAD, channels), bf16),
            jax.ShapeDtypeStruct((T, 128), f32),
            jax.ShapeDtypeStruct((T, 128), f32),
        ] + kept,
        in_specs=[smem()] + [hbm()] * 8,
        out_specs=[vmem()] * 9,
        scratch_shapes=[
            pltpu.VMEM(ids2.shape, ids2.dtype),
            pltpu.VMEM(gain.shape, f32),
            pltpu.VMEM((T, depth), bf16),
            pltpu.VMEM((T, depth), bf16),
            pltpu.VMEM((slots, 3, kc_size, cb_size), bf16),
            pltpu.VMEM((3, T, cb_size), f32),
            pltpu.VMEM((3, T + 8, cb_size), f32),
            pltpu.VMEM((HEAD, cb_size), f32),
            pltpu.VMEM((ids2.shape[0] * 128 + 8, 128), f32),
            pltpu.VMEM((T + 8, 128), f32),
            pltpu.VMEM((T, 128), f32),
            pltpu.VMEM((T, 128), f32),
            pltpu.SemaphoreType.DMA((6,)),
            pltpu.SemaphoreType.DMA((4,)),
            pltpu.SemaphoreType.DMA((slots,)),
        ],
        compiler_params=pltpu.CompilerParams(vmem_limit_bytes=28 * MIB),
        name="front",
    )(position, ids2, tokens, gain, weight3, taps, rates, residues, skip)


def expm1(x):
    series = jnp.ones_like(x)
    for k in range(9, 1, -1):
        series = 1.0 + series * x * (1.0 / k)
    return jnp.where(jnp.abs(x) < 0.5, x * series, jnp.exp(x) - 1.0)


def local_kernel(poles, first, prod_ref, keep_ref, rates_ref, residues_ref, skip_ref, _, local_out, state_out, pole_out):
    tiles, T, _ = local_out.shape
    run = T // PARTS
    mine = slice(first * 128, (first + tiles) * 128)
    pole_out[...] = residues_ref[:, mine] * jnp.sqrt(-expm1(-2.0 * rates_ref[:, mine]))

    def tile_body(tile, _):
        lanes = pl.ds(pl.multiple_of((first + tile) * 128, 128), 128)
        d16 = jnp.exp(-rates_ref[:, lanes])
        w16 = pole_out[:, pl.ds(pl.multiple_of(tile * 128, 128), 128)]
        decay = [jnp.broadcast_to(d16[n : n + 1], (8, 128)) for n in range(poles)]
        weight = [jnp.broadcast_to(w16[n : n + 1], (8, 128)) for n in range(poles)]
        skip = skip_ref[0:1, lanes]

        def token(i, states):
            at = pl.ds(i, PARTS, stride=run)
            p, keep = prod_ref[first + tile, at, :], keep_ref[at, :]
            after = [states[n] * decay[n] * keep + p for n in range(poles)]
            local_out[tile, at, :] = tree([skip * p] + [weight[n] * after[n] for n in range(poles)])
            return tuple(after)

        states = lax.fori_loop(0, run, token, tuple(jnp.zeros((8, 128), f32) for _ in range(poles)), unroll=2)
        for n in range(poles):
            state_out[tile, pl.ds(n, PARTS, stride=poles), :] = states[n]
        return 0

    lax.fori_loop(0, tiles, tile_body, 0)


def tree(terms):
    while len(terms) > 1:
        terms = [a + b for a, b in zip(terms[0::2], terms[1::2])] + terms[len(terms) // 2 * 2 :]
    return terms[0]


def local_pass(first, tiles, product, keep, rates, residues, skip, after):
    T, poles = product.shape[1], rates.shape[0]
    return pl.pallas_call(
        functools.partial(local_kernel, poles, first),
        out_shape=(
            jax.ShapeDtypeStruct((tiles, T, 128), f32),
            jax.ShapeDtypeStruct((tiles, PARTS * poles, 128), f32),
            jax.ShapeDtypeStruct((poles, tiles * 128), f32),
        ),
        in_specs=[vmem()] * 5 + [pl.BlockSpec(memory_space=pl.ANY)],
        out_specs=[vmem()] * 3,
        compiler_params=pltpu.CompilerParams(vmem_limit_bytes=4 * MIB),
        cost_estimate=pl.CostEstimate(flops=6 * T * poles * tiles * 128, bytes_accessed=8 * MIB, transcendentals=0),
        name="local_pass",
    )(product, keep, rates, residues, skip, after)


def first_products(first, last, taps, ids_ref, base):
    s01, s0m1 = same_id(ids_ref, base + 1, base), same_id(ids_ref, base, base - 1)
    s0m2, s1m1 = same_id(ids_ref, base, base - 2), same_id(ids_ref, base + 1, base - 1)

    def shift(i):
        near, far = last[i][1:2], last[i][0:1]
        t1, t2 = taps[1][i : i + 1], taps[2][i : i + 1]
        return s0m1 * (t1 * near) + s0m2 * (t2 * far), s1m1 * (t2 * near)

    def plain(i):
        t0, t1 = taps[0][i : i + 1], taps[1][i : i + 1]
        return t0 * first[i][0:1], t0 * first[i][1:2] + s01 * (t1 * first[i][0:1])

    k, v, dk, dv = plain(1), plain(2), shift(1), shift(2)
    delta = [(k[j] + dk[j]) * (v[j] + dv[j]) - k[j] * v[j] for j in range(2)]
    return shift(0), delta


def unpack(block, poles):
    first = [None, block[poles : poles + 2], block[poles + 2 : poles + 4]]
    last = [block[poles + 4 + 2 * i : poles + 6 + 2 * i] for i in range(3)]
    return block[0:poles], first, last


def joined_state(low_state, low_last, up_state, up_first, taps, rates, ids_ref, base, length):
    _, delta = first_products(up_first, low_last, taps, ids_ref, base)
    grown = low_state + delta[0] * jnp.exp(rates) + delta[1] * jnp.exp(2.0 * rates)
    open_ = same_id(ids_ref, base + length - 1, base - 1)
    return up_state + grown * (jnp.exp(-rates * jnp.float32(length)) * open_)


def join_kernel(T, poles, span, position, ids_ref, mine_ref, other_ref, taps_ref, rates_ref, _, out):
    me = position[0]
    is_upper = (me // span) % 2 == 1
    base = (me // (2 * span)) * (2 * span * T) + span * T
    mine, other = mine_ref[...].astype(f32), other_ref[...].astype(f32)
    lower, upper = jnp.where(is_upper, other, mine), jnp.where(is_upper, mine, other)
    taps = [taps_ref[j] for j in range(3)]
    low_state, _, low_last = unpack(lower, poles)
    up_state, up_first, _ = unpack(upper, poles)
    state = joined_state(low_state, low_last, up_state, up_first, taps, rates_ref[...], ids_ref, base, span * T)
    out[0:poles, :] = state.astype(bf16)
    row = lax.broadcasted_iota(jnp.int32, (HEAD, lower.shape[1]), 0)
    out[poles : poles + HEAD, :] = jnp.where(row < 4, lower[poles:], upper[poles:]).astype(bf16)


def join(span, T, position, ids, mine, other, taps, rates, after):
    poles = rates.shape[0]
    return pl.pallas_call(
        functools.partial(join_kernel, T, poles, span),
        out_shape=jax.ShapeDtypeStruct(mine.shape, bf16),
        in_specs=[smem(), smem()] + [vmem()] * 4 + [pl.BlockSpec(memory_space=pl.ANY)],
        out_specs=vmem(),
        compiler_params=pltpu.CompilerParams(vmem_limit_bytes=4 * MIB),
        name="join",
    )(position, ids, mine, other, taps, rates, after)


def gate_kernel(
    T, poles, spans, cuts, position, lane_position, ids_ref, query_ref, block_ref, visible_ref, taps_ref, rates_ref, skip_ref,
    out_ref, *rest,
):
    arrived, rest = rest[: len(spans)], rest[len(spans) :]
    parts, rest = [rest[3 * c : 3 * c + 3] for c in range(cuts)], rest[3 * cuts :]
    (gated_out, send_out, mine_out, carry, full, window, sem) = rest
    run = T // PARTS
    tiles = query_ref.shape[1] // 128
    columns(lane_position[0], 0, out_ref, window, sem).start()
    me = position[0]
    base = me * T
    taps = [taps_ref[j] for j in range(3)]
    rates, skip = rates_ref[...], skip_ref[...]
    weight = jnp.concatenate([pole_ref[...] for _, _, pole_ref in parts], axis=1)
    each = tiles // cuts
    prior = jnp.zeros(block_ref.shape, f32)
    prior_state, prior_first, prior_last = unpack(prior, poles)
    for span, ref in zip(spans, arrived):
        state, first, last = unpack(ref[...].astype(f32), poles)
        upper, held = (me // span) % 2 == 1, me % span
        if span == 1:
            both = state
        else:
            both = joined_state(
                state, last, prior_state, prior_first, taps, rates, ids_ref, (me - held) * T, held * T)
        fresh = upper & (held == 0)
        prior_state = jnp.where(fresh, state, jnp.where(upper, both, prior_state))
        prior_first = [None] + [jnp.where(upper, first[i], prior_first[i]) for i in (1, 2)]
        prior_last = [jnp.where(fresh, last[i], prior_last[i]) for i in range(3)]
    _, first, _ = unpack(block_ref[...].astype(f32), poles)
    q_shift, delta = first_products(first, prior_last, taps, ids_ref, base)
    second = delta[1] * jnp.exp(rates)
    now = prior_state + (delta[0] + second) * jnp.exp(rates)
    fix0 = skip * delta[0] - jnp.sum(weight * second, axis=0, keepdims=True)
    fix1 = skip * delta[1]
    jump = jnp.exp(-rates * float(run))
    for s in range(PARTS):
        part = slice(s * poles, (s + 1) * poles)
        began = weight * now
        for tile in range(tiles):
            carry[tile, part, :] = began[:, tile * 128 : tile * 128 + 128]
        if s < PARTS - 1:
            whole = same_id(ids_ref, base + s * run + run - 1, base + s * run - 1)
            ends = jnp.concatenate([parts[tile // each][1][tile % each, part, :] for tile in range(tiles)], axis=1)
            now = now * (jump * whole) + ends

    def lane_body(cut, inner, _):
        tile = cut * each + inner
        lanes = pl.ds(pl.multiple_of(tile * 128, 128), 128)
        d16 = jnp.exp(-rates_ref[:, lanes])
        decay = [jnp.broadcast_to(d16[n : n + 1], (8, 128)) for n in range(poles)]
        start = tuple(carry[tile, pl.ds(n, PARTS, stride=poles), :] for n in range(poles))

        def token(i, states):
            after = [states[n] * decay[n] for n in range(poles)]
            see = visible_ref[pl.ds(pl.multiple_of(i * 8, 8), 8), :]
            at = pl.ds(i, PARTS, stride=run)
            full[tile, at, :] = parts[cut][0][inner, at, :] + see * tree(list(after))
            return tuple(after)

        lax.fori_loop(0, run, token, start, unroll=4)
        return 0

    for cut in range(cuts):
        lax.fori_loop(0, each, functools.partial(lane_body, cut), 0)
    row = lax.broadcasted_iota(jnp.int32, (16, 128), 0)
    for tile in range(tiles):
        lanes = slice(tile * 128, tile * 128 + 128)
        gated_out[:, lanes] = (query_ref[:, lanes] * full[tile]).astype(bf16)
        top_q, top = query_ref[0:16, lanes], full[tile, 0:16, :]
        top_q = top_q + jnp.where(row == 0, q_shift[0][:, lanes], 0.0) + jnp.where(row == 1, q_shift[1][:, lanes], 0.0)
        top = top + jnp.where(row == 0, fix0[:, lanes], 0.0) + jnp.where(row == 1, fix1[:, lanes], 0.0)
        gated_out[0:16, lanes] = (top_q * top).astype(bf16)
    columns(lane_position[0], 0, out_ref, window, sem).wait()
    share(lane_position[0], gated_out, window, send_out, mine_out)


def target(index, slot):
    chip = index // 2
    low = chip < 2
    if slot < 2:
        return jnp.where(low, 3 - slot, slot)
    if slot == 2:
        return jnp.where(low, 1 - chip, 5 - chip)
    return chip


def columns(index, slot, out_ref, window, sem):
    both = window.shape[1]
    start = pl.multiple_of(target(index, slot) * both, both)
    return pltpu.make_async_copy(out_ref.at[:, pl.ds(start, both)], window, sem)


def share(index, gated_ref, window, send_out, mine_out):
    width = send_out.shape[1]
    tile = 256
    core = index % 2

    for j in range(width // tile):
        at = slice(j * tile, j * tile + tile)
        for out, half in ((send_out, 1 - core), (mine_out, core)):
            cols = pl.ds(pl.multiple_of(half * width + j * tile, tile), tile)
            out[:, at] = jnp.dot(gated_ref[...], window[:, cols], preferred_element_type=f32).astype(out.dtype)


def share_kernel(slots, lane_position, gated_ref, out_ref, *rest):
    outs, (windows, sem) = rest[:-2], rest[-2:]
    copies = [columns(lane_position[0], slot, out_ref, windows.at[k], sem.at[k]) for k, slot in enumerate(slots)]
    for copy in copies:
        copy.start()
    for k, copy in enumerate(copies):
        copy.wait()
        share(lane_position[0], gated_ref, windows.at[k], outs[2 * k], outs[2 * k + 1])


def share_rest(slots, lane_position, gated, out_weight, width):
    T, channels = gated.shape
    return pl.pallas_call(
        functools.partial(share_kernel, slots),
        out_shape=[jax.ShapeDtypeStruct((T, width), d) for _ in slots for d in (bf16, f32)],
        in_specs=[smem(), vmem(), hbm()],
        out_specs=[vmem()] * (2 * len(slots)),
        scratch_shapes=[
            pltpu.VMEM((len(slots), channels, 2 * width), bf16),
            pltpu.SemaphoreType.DMA((len(slots),)),
        ],
        compiler_params=pltpu.CompilerParams(vmem_limit_bytes=20 * MIB),
        cost_estimate=pl.CostEstimate(
            flops=4 * T * channels * width * len(slots), bytes_accessed=4 * channels * width * len(slots), transcendentals=0),
        name="share_rest",
    )(lane_position, gated, out_weight)


def gate(T, spans, arrived, position, lane_position, ids, query, parts, block, visible, taps, rates, skip, out_weight, width):
    poles, channels = rates.shape
    return pl.pallas_call(
        functools.partial(gate_kernel, T, poles, tuple(spans), len(parts)),
        out_shape=[
            jax.ShapeDtypeStruct(query.shape, bf16),
            jax.ShapeDtypeStruct((T, width), bf16),
            jax.ShapeDtypeStruct((T, width), f32),
        ],
        in_specs=[smem()] * 3 + [vmem()] * 6 + [hbm()] + [vmem()] * (len(spans) + 3 * len(parts)),
        out_specs=[vmem()] * 3,
        scratch_shapes=[
            pltpu.VMEM((channels // 128, PARTS * poles, 128), f32),
            pltpu.VMEM((channels // 128, T, 128), f32),
            pltpu.VMEM((channels, 2 * width), bf16),
            pltpu.SemaphoreType.DMA,
        ],
        compiler_params=pltpu.CompilerParams(vmem_limit_bytes=10 * MIB),
        name="gate",
    )(position, lane_position, ids, query, block, visible, taps, rates, skip, out_weight, *arrived,
      *[a for part in parts for a in part])


def total(*terms):
    return functools.reduce(lambda a, b: a + b, [t.astype(f32) for t in terms]).astype(bf16)


def scatter_line(lane_position, gated, send, mine, out_weight, width):
    pair = [(m, m ^ 1) for m in range(8)]

    def along(hops):
        return [(a * 2 + c, b * 2 + c) for a, b in hops for c in range(2)]

    ends = along([(0, 1), (3, 2)])
    middle = along([(1, 2), (2, 1)])
    near = along([(0, 1), (1, 0), (2, 3), (3, 2)])
    sums = [total(mine, lax.ppermute(send, "mp", pair))]
    first = lax.ppermute(sums[0], "mp", ends)
    rest = share_rest((1, 2, 3), lane_position, gated, out_weight, width)
    sums += [total(rest[2 * k + 1], lax.ppermute(rest[2 * k], "mp", pair)) for k in range(3)]
    second = lax.ppermute(sums[1], "mp", ends)
    across = lax.ppermute(total(sums[0], first), "mp", middle)
    across2 = lax.ppermute(total(sums[1], second), "mp", middle)
    last = lax.ppermute(total(sums[2], across), "mp", near)
    return total(sums[3], across2, last)


def shifted(value, axis, steps):
    count = lax.axis_size(axis)
    leading, last = (max(0, -steps), min(count, count - steps))
    return lax.ppermute(value, axis, [(source, source + steps) for source in range(leading, last)])


def project(block, norm_gain, weights):
    floats = block.astype(jnp.float32)
    mean_square = jnp.mean(floats * floats, axis=-1, keepdims=True)
    normed = (floats * lax.rsqrt(mean_square + epsilon) * norm_gain[None, :]).astype(jnp.bfloat16)
    return jnp.dot(normed, weights, preferred_element_type=jnp.float32).astype(jnp.bfloat16)


def general(
    tokens, norm_gain, in_weight, short_filter, rates, residues, skip, out_weight, segment_ids
):
    tok_rows = tokens.shape[0]
    model_width = tokens.shape[1]
    channels = in_weight.shape[2]
    filter_taps = short_filter.shape[0]
    pole_count = rates.shape[0]
    device_index = lax.axis_index("ctx")
    row_offset = device_index * tok_rows
    weights = in_weight.reshape(model_width, 3 * channels)
    projected = project(tokens, norm_gain, weights)
    previous = shifted(projected[tok_rows - (filter_taps - 1) :], "ctx", 1)
    extended = jnp.concatenate([previous, projected], axis=0)
    padded_ids = jnp.concatenate([jnp.full((filter_taps,), -1, jnp.int32), segment_ids], axis=0)
    window = lax.dynamic_slice_in_dim(padded_ids, row_offset, tok_rows + filter_taps, 0)
    local_ids = window[filter_taps:]
    taps_table = short_filter.reshape(filter_taps, 3 * channels)
    featured = jnp.zeros((tok_rows, 3 * channels), jnp.float32)
    for lag_index in range(filter_taps):
        begin = filter_taps - 1 - lag_index
        lagged = extended[begin : begin + tok_rows].astype(jnp.float32)
        matches = window[filter_taps - lag_index : filter_taps - lag_index + tok_rows] == local_ids
        term = taps_table[lag_index][None, :] * lagged
        featured = featured + jnp.where(matches[:, None], term, jnp.zeros_like(term))
    query_part = featured[:, :channels]
    key_part = featured[:, channels : 2 * channels]
    value_part = featured[:, 2 * channels :]
    product = key_part * value_part
    offsets = jnp.arange(tok_rows, dtype=jnp.float32)
    center = float(tok_rows // 2)
    growth = jnp.exp(-(offsets - center)[:, None, None] * rates[None])
    shrinkage = jnp.exp((offsets - center)[:, None, None] * rates[None])
    weighted = (shrinkage * product[:, None, :]).reshape(tok_rows, pole_count * channels)
    visible = (offsets[:, None] >= offsets[None, :]) & (local_ids[:, None] == local_ids[None, :])
    in_block = jnp.dot(visible.astype(jnp.float32), weighted, precision=lax.Precision.HIGHEST)
    in_block = in_block.reshape(tok_rows, pole_count, channels) * growth
    survives = local_ids == window[filter_taps - 1]
    block_factor = jnp.exp(-rates * tok_rows)
    block_end = in_block[tok_rows - 1]
    block_ends = lax.all_gather(block_end[None], "ctx", axis=0, tiled=True)
    shard_count = segment_ids.shape[0] // tok_rows
    last_ids = segment_ids.reshape(shard_count, tok_rows)[:, tok_rows - 1]
    prior_ids = jnp.concatenate([jnp.full((1,), -1, jnp.int32), last_ids[:-1]], axis=0)
    shard_decays = block_factor[None] * (last_ids == prior_ids).astype(jnp.float32)[:, None, None]

    def absorb(running, inputs):
        shard, factor, shard_end = inputs
        advanced = running * factor + shard_end
        return (jnp.where(shard < device_index, advanced, running), None)

    incoming, _ = lax.scan(
        absorb,
        jnp.zeros_like(block_end),
        (jnp.arange(shard_count, dtype=jnp.int32), shard_decays, block_ends),
    )
    carried = incoming[None] * jnp.exp(-(offsets + 1.0)[:, None, None] * rates[None])
    carried = carried * survives.astype(jnp.float32)[:, None, None]
    states = in_block + carried
    pole_weight = residues * jnp.sqrt(-jnp.expm1(-2.0 * rates))
    longconv = jnp.sum(pole_weight[None] * states, axis=1)
    gated = (query_part * (longconv + skip[None, :] * product)).astype(jnp.bfloat16)
    partial_terms = jnp.dot(gated, out_weight, preferred_element_type=jnp.float32)
    return lax.psum_scatter(partial_terms, "mp", scatter_dimension=1, tiled=True).astype(
        jnp.bfloat16
    )


def local(tokens, norm_gain, in_weight, short_filter, rates, residues, skip, out_weight, segment_ids):
    T = tokens.shape[0]
    shards = lax.axis_size("ctx")
    me = lax.axis_index("ctx")
    position = me.astype(jnp.int32)[None]
    lane_position = lax.axis_index("mp").astype(jnp.int32)[None]
    width = out_weight.shape[1] // lax.axis_size("mp")
    weight3 = jnp.transpose(in_weight, (1, 0, 2))
    out_weight = pltpu.with_memory_space_constraint(out_weight, pltpu.HBM)
    query, product, block, keep, visible, taps, rates, residues, skip = front(
        position, segment_ids.reshape(-1, 128), tokens, norm_gain[None], weight3, short_filter, rates, residues, skip[None])
    cuts = shards.bit_length() - 1
    each = product.shape[0] // cuts
    group, spans, arrived, parts = block, [], [], []
    for k in range(cuts):
        span = 1 << k
        other = lax.ppermute(group, "ctx", [(a, a ^ span) for a in range(shards)])
        spans.append(span)
        arrived.append(other)
        parts.append(local_pass(k * each, each, product, keep, rates, residues, skip, group))
        if k < cuts - 1:
            group = join(span, T, position, segment_ids, group, other, taps, rates, parts[k][0])
    gated, send, mine = gate(T, spans, arrived, position, lane_position, segment_ids, query, parts, block, visible, taps, rates,
                             skip, out_weight, width)
    return scatter_line(lane_position, gated, send, mine, out_weight, width)


def solution(mesh):
    placed = (
        P("ctx", None),
        P(),
        P(None, None, "mp"),
        P(None, None, "mp"),
        P(None, "mp"),
        P(None, "mp"),
        P("mp"),
        P("mp", None),
        P(),
    )
    shards, groups = mesh.shape["ctx"], mesh.shape["mp"]

    def body(tokens, norm_gain, in_weight, *rest):
        suits = groups == 8 and shards & (shards - 1) == 0 and shards > 1
        suits = suits and in_weight.shape[2] % 512 == 0 and in_weight.shape[0] % 2048 == 0
        suits = suits and tokens.shape[0] % 64 == 0 and rest[-1].shape[0] % 128 == 0 and rest[1].shape[0] % 8 == 0
        return (local if suits else general)(tokens, norm_gain, in_weight, *rest)

    return jax.shard_map(
        body, mesh=mesh, in_specs=placed, out_specs=P("ctx", "mp"), check_vma=False
    )
```

profile of v0, /device:TPU:0, one launch (start us, length us, event | category | flops | bytes accessed | tf_op | source)
XLA Modules:
  0.0 77.9 jit_solution(17744545614155005213)
XLA Ops:
  0.0 0.0 copy-start
  0.0 20.7 %front.1 = (f32[192,1024]{1,0:T(8,128)S(1)}, f32[8,192,128]{2,1,0:T(8,128)S(1)}, bf16[32,1024]{1,0:T(8,128)(2,1)S(1)}, f32[192,128]{1,0:T(8,128)S(1)}, f32[192,1...) custom-call(s32[1]{0:T(128)} %bitcast.1.position, ...), custom_call_target="tpu_custom_call" | custom-call | tf_op jit(solution)/shard_map/front/pallas_call | solution.py:177
  20.7 3.0 %collective-permute-start = (bf16[32,1024]{1,0:T(8,128)(2,1)S(1)}, bf16[32,1024]{1,0:T(8,128)(2,1)S(1)}, u32[]{:S(2)}, u32[]{:S(2)}) collective-permute-start(bf16[32,1024]{1,0:T(8,128)(2,1)S(1)} %get-tuple-element.30._.mine_ref.block_ref), channel_id=1, source_target_pairs={{0,8},{8,0},{16,24},{24,16},{1,9},{9,1},{17,25},{25,17},{2,10},{10... | collective-permute-start | bytes 196616 | tf_op jit(solution)/shard_map/ppermute | solution.py:605
  23.8 1.8 %local_pass.2 = (f32[4,192,128]{2,1,0:T(8,128)S(1)}, f32[4,128,128]{2,1,0:T(8,128)S(1)}, f32[16,512]{1,0:T(8,128)S(1)}) custom-call(f32[8,192,128]{2,1,0:T(8,128)S(1)} %get-tuple-element.35.prod_ref, f32[192,128]{1,0:T(8,128)S(1)} %get-tuple-element.36.keep_ref, f32[16,1024]{1,0:T(8,128)S(1)} %get-tuple-element.33.rates_ref, ...), custom_call_target="tpu_custom_call" | custom-call | flops 9437184 | bytes 8388608 | tf_op jit(solution)/shard_map/local_pass/pallas_call | solution.py:254
  25.5 0.5 collective-permute-done.other_ref.rest_0_
  26.0 0.0 copy-done
  26.0 0.7 join.1._
  26.7 2.1 %collective-permute-start.1 = (bf16[32,1024]{1,0:T(8,128)(2,1)S(1)}, bf16[32,1024]{1,0:T(8,128)(2,1)S(1)}, u32[]{:S(2)}, u32[]{:S(2)}) collective-permute-start(bf16[32,1024]{1,0:T(8,128)(2,1)S(1)} %join.1._), channel_id=1, source_target_pairs={{0,16},{8,24},{16,0},{24,8},{1,17},{9,25},{17,1},{25,9},{2,18},{10... | collective-permute-start | bytes 196616 | tf_op jit(solution)/shard_map/ppermute | solution.py:605
  28.8 1.8 %local_pass.3 = (f32[4,192,128]{2,1,0:T(8,128)S(1)}, f32[4,128,128]{2,1,0:T(8,128)S(1)}, f32[16,512]{1,0:T(8,128)S(1)}) custom-call(f32[8,192,128]{2,1,0:T(8,128)S(1)} %get-tuple-element.35.prod_ref, f32[192,128]{1,0:T(8,128)S(1)} %get-tuple-element.36.keep_ref, f32[16,1024]{1,0:T(8,128)S(1)} %get-tuple-element.33.rates_ref, ...), custom_call_target="tpu_custom_call" | custom-call | flops 9437184 | bytes 8388608 | tf_op jit(solution)/shard_map/local_pass/pallas_call | solution.py:254
  30.6 0.5 collective-permute-done.1.rest_1_
  31.0 3.8 %gate.1 = (bf16[192,1024]{1,0:T(8,128)(2,1)S(1)}, bf16[192,1024]{1,0:T(8,128)(2,1)S(1)}, f32[192,1024]{1,0:T(8,128)S(1)}) custom-call(s32[1]{0:T(128)} %bitcast.1.position, s32[1]{0:T(128)} %bitcast.lane_position, s32[768]{0:T(1024)S(1)} %copy-done, f32[192,1024]{1,0:T(8,128)S(1)} %get-tuple-element.29.query_ref, ...), custom_call_target="tpu_custom_call" | custom-call | tf_op jit(solution)/shard_map/gate/pallas_call | solution.py:463
  34.9 0.1 collective-permute-start.7
  34.9 5.7 %share_rest.1 = (bf16[192,1024]{1,0:T(8,128)(2,1)S(1)}, f32[192,1024]{1,0:T(8,128)S(1)}, bf16[192,1024]{1,0:T(8,128)(2,1)S(1)}, f32[192,1024]{1,0:T(8,128)S(1)},...) custom-call(s32[1]{0:T(128)} %bitcast.lane_position, bf16[192,1024]{1,0:T(8,128)(2,1)S(1)} %get-tuple-element.44.gated_ref, ...), custom_call_target="tpu_custom_call" | custom-call | flops 2415919104 | bytes 12582912 | tf_op jit(solution)/shard_map/share_rest/pallas_call | solution.py:445
  40.7 0.6 collective-permute-start.3
  41.3 0.0 collective-permute-done.7
  41.3 0.1 add_convert_fusion.3
  41.3 4.0 %collective-permute-start.8 = (bf16[192,1024]{1,0:T(8,128)(2,1)S(1)}, bf16[192,1024]{1,0:T(8,128)(2,1)S(1)}, u32[]{:S(2)}, u32[]{:S(2)}) collective-permute-start(bf16[192,1024]{1,0:T(8,128)(2,1)S(1)} %add_convert_fusion.3), channel_id=1, source_target_pairs={{0,2},{1,3},{6,4},{7,5},{8,10},{9,11},{14,12},{15,13},{16,18},{17,... | collective-permute-start | bytes 1179656 | tf_op jit(solution)/shard_map/ppermute | solution.py:498
  45.4 0.0 collective-permute-done.3
  45.4 0.1 add_convert_fusion.6
  45.5 1.3 %collective-permute-start.4 = (bf16[192,1024]{1,0:T(8,128)(2,1)S(1)}, bf16[192,1024]{1,0:T(8,128)(2,1)S(1)}, u32[]{:S(2)}, u32[]{:S(2)}) collective-permute-start(bf16[192,1024]{1,0:T(8,128)(2,1)S(1)} %add_convert_fusion.6), channel_id=1, source_target_pairs={{0,2},{1,3},{6,4},{7,5},{8,10},{9,11},{14,12},{15,13},{16,18},{17,... | collective-permute-start | bytes 1179656 | tf_op jit(solution)/shard_map/ppermute | solution.py:501
  46.8 0.1 collective-permute-start.6
  46.9 7.9 %collective-permute-done.8 = bf16[192,1024]{1,0:T(8,128)(2,1)S(1)} collective-permute-done((bf16[192,1024]{1,0:T(8,128)(2,1)S(1)}, bf16[192,1024]{1,0:T(8,128)(2,1)S(1)}, u32[]{:S(2)}, u32[]{:S(2)}) %collective-permute-start.8) | collective-permute-done | bytes 393248 | tf_op jit(solution)/shard_map/ppermute | solution.py:498
  54.8 0.1 add_convert_fusion.2
  55.0 0.7 collective-permute-start.9
  55.7 0.1 collective-permute-start.2
  55.7 6.6 %collective-permute-done.4 = bf16[192,1024]{1,0:T(8,128)(2,1)S(1)} collective-permute-done((bf16[192,1024]{1,0:T(8,128)(2,1)S(1)}, bf16[192,1024]{1,0:T(8,128)(2,1)S(1)}, u32[]{:S(2)}, u32[]{:S(2)}) %collective-permute-start.4) | collective-permute-done | bytes 393248 | tf_op jit(solution)/shard_map/ppermute | solution.py:501
  62.3 0.1 add_convert_fusion.5
  62.5 0.7 collective-permute-start.5
  63.2 0.0 collective-permute-done.6
  63.2 0.0 collective-permute-done.9
  63.2 0.2 add_convert_fusion.1
  63.4 5.5 %collective-permute-start.10 = (bf16[192,1024]{1,0:T(8,128)(2,1)S(1)}, bf16[192,1024]{1,0:T(8,128)(2,1)S(1)}, u32[]{:S(2)}, u32[]{:S(2)}) collective-permute-start(bf16[192,1024]{1,0:T(8,128)(2,1)S(1)} %add_convert_fusion.1), channel_id=1, source_target_pairs={{0,2},{1,3},{2,0},{3,1},{4,6},{5,7},{6,4},{7,5},{8,10},{9,11},{10,... | collective-permute-start | bytes 1179656 | tf_op jit(solution)/shard_map/ppermute | solution.py:504
  68.9 0.0 collective-permute-done.2
  68.9 0.0 collective-permute-done.5
  68.9 8.0 %collective-permute-done.10 = bf16[192,1024]{1,0:T(8,128)(2,1)S(1)} collective-permute-done((bf16[192,1024]{1,0:T(8,128)(2,1)S(1)}, bf16[192,1024]{1,0:T(8,128)(2,1)S(1)}, u32[]{:S(2)}, u32[]{:S(2)}) %collective-permute-start.10) | collective-permute-done | bytes 393248 | tf_op jit(solution)/shard_map/ppermute | solution.py:504
  76.9 1.0 %add_convert_fusion = bf16[192,1024]{1,0:T(8,128)(2,1)} fusion(bf16[192,1024]{1,0:T(8,128)(2,1)S(1)} %collective-permute-done.10, bf16[192,1024]{1,0:T(8,128)(2,1)S(1)} %collective-permute-done.5, f32[192,1024]{1,0:T(8,128)S(1)} %get-tuple-element.45, bf16[192,1024]{1,0:T(8,128)(2,1)S(1)} %collective-permute-done.2), kind=kLoop, calls=%fused_computation | loop fusion | flops 1769472 | bytes 2359296 | tf_op jit(solution)/shard_map/convert_element_type | solution.py:485
Async XLA Ops:
  0.0 26.0 %copy-start = (s32[768]{0:T(1024)S(1)}, s32[768]{0:T(1024)}, u32[]{:S(2)}) copy-start(s32[768]{0:T(1024)} %ids_ref.3) | copy-start | bytes 9220
  20.7 5.3 %collective-permute-start = (bf16[32,1024]{1,0:T(8,128)(2,1)S(1)}, bf16[32,1024]{1,0:T(8,128)(2,1)S(1)}, u32[]{:S(2)}, u32[]{:S(2)}) collective-permute-start(bf16[32,1024]{1,0:T(8,128)(2,1)S(1)} %get-tuple-element.30._.mine_ref.block_ref), channel_id=1, source_target_pairs={{0,8},{8,0},{16,24},{24,16},{1,9},{9,1},{17,25},{25,17},{2,10},{10... | collective-permute-start | bytes 196616 | tf_op jit(solution)/shard_map/ppermute | solution.py:605
  26.7 4.4 %collective-permute-start.1 = (bf16[32,1024]{1,0:T(8,128)(2,1)S(1)}, bf16[32,1024]{1,0:T(8,128)(2,1)S(1)}, u32[]{:S(2)}, u32[]{:S(2)}) collective-permute-start(bf16[32,1024]{1,0:T(8,128)(2,1)S(1)} %join.1._), channel_id=1, source_target_pairs={{0,16},{8,24},{16,0},{24,8},{1,17},{9,25},{17,1},{25,9},{2,18},{10... | collective-permute-start | bytes 196616 | tf_op jit(solution)/shard_map/ppermute | solution.py:605
  34.9 6.4 %collective-permute-start.7 = (bf16[192,1024]{1,0:T(8,128)(2,1)S(1)}, bf16[192,1024]{1,0:T(8,128)(2,1)S(1)}, u32[]{:S(2)}, u32[]{:S(2)}) collective-permute-start(bf16[192,1024]{1,0:T(8,128)(2,1)S(1)} %get-tuple-element.52), channel_id=1, source_target_pairs={{0,1},{1,0},{2,3},{3,2},{4,5},{5,4},{6,7},{7,6},{8,9},{9,8},{10,11... | collective-permute-start | bytes 1179656 | tf_op jit(solution)/shard_map/ppermute | solution.py:497
  40.7 4.7 %collective-permute-start.3 = (bf16[192,1024]{1,0:T(8,128)(2,1)S(1)}, bf16[192,1024]{1,0:T(8,128)(2,1)S(1)}, u32[]{:S(2)}, u32[]{:S(2)}) collective-permute-start(bf16[192,1024]{1,0:T(8,128)(2,1)S(1)} %get-tuple-element.48), channel_id=1, source_target_pairs={{0,1},{1,0},{2,3},{3,2},{4,5},{5,4},{6,7},{7,6},{8,9},{9,8},{10,11... | collective-permute-start | bytes 1179656 | tf_op jit(solution)/shard_map/ppermute | solution.py:500
  41.3 13.5 %collective-permute-start.8 = (bf16[192,1024]{1,0:T(8,128)(2,1)S(1)}, bf16[192,1024]{1,0:T(8,128)(2,1)S(1)}, u32[]{:S(2)}, u32[]{:S(2)}) collective-permute-start(bf16[192,1024]{1,0:T(8,128)(2,1)S(1)} %add_convert_fusion.3), channel_id=1, source_target_pairs={{0,2},{1,3},{6,4},{7,5},{8,10},{9,11},{14,12},{15,13},{16,18},{17,... | collective-permute-start | bytes 1179656 | tf_op jit(solution)/shard_map/ppermute | solution.py:498
  45.5 16.8 %collective-permute-start.4 = (bf16[192,1024]{1,0:T(8,128)(2,1)S(1)}, bf16[192,1024]{1,0:T(8,128)(2,1)S(1)}, u32[]{:S(2)}, u32[]{:S(2)}) collective-permute-start(bf16[192,1024]{1,0:T(8,128)(2,1)S(1)} %add_convert_fusion.6), channel_id=1, source_target_pairs={{0,2},{1,3},{6,4},{7,5},{8,10},{9,11},{14,12},{15,13},{16,18},{17,... | collective-permute-start | bytes 1179656 | tf_op jit(solution)/shard_map/ppermute | solution.py:501
  46.8 16.4 %collective-permute-start.6 = (bf16[192,1024]{1,0:T(8,128)(2,1)S(1)}, bf16[192,1024]{1,0:T(8,128)(2,1)S(1)}, u32[]{:S(2)}, u32[]{:S(2)}) collective-permute-start(bf16[192,1024]{1,0:T(8,128)(2,1)S(1)} %get-tuple-element.50), channel_id=1, source_target_pairs={{0,1},{1,0},{2,3},{3,2},{4,5},{5,4},{6,7},{7,6},{8,9},{9,8},{10,11... | collective-permute-start | bytes 1179656 | tf_op jit(solution)/shard_map/ppermute | solution.py:500
  55.0 8.2 %collective-permute-start.9 = (bf16[192,1024]{1,0:T(8,128)(2,1)S(1)}, bf16[192,1024]{1,0:T(8,128)(2,1)S(1)}, u32[]{:S(2)}, u32[]{:S(2)}) collective-permute-start(bf16[192,1024]{1,0:T(8,128)(2,1)S(1)} %add_convert_fusion.2), channel_id=1, source_target_pairs={{2,4},{3,5},{4,2},{5,3},{10,12},{11,13},{12,10},{13,11},{18,20},{1... | collective-permute-start | bytes 1179656 | tf_op jit(solution)/shard_map/ppermute | solution.py:502
  55.7 13.2 %collective-permute-start.2 = (bf16[192,1024]{1,0:T(8,128)(2,1)S(1)}, bf16[192,1024]{1,0:T(8,128)(2,1)S(1)}, u32[]{:S(2)}, u32[]{:S(2)}) collective-permute-start(bf16[192,1024]{1,0:T(8,128)(2,1)S(1)} %get-tuple-element.46), channel_id=1, source_target_pairs={{0,1},{1,0},{2,3},{3,2},{4,5},{5,4},{6,7},{7,6},{8,9},{9,8},{10,11... | collective-permute-start | bytes 1179656 | tf_op jit(solution)/shard_map/ppermute | solution.py:500
  62.5 6.4 %collective-permute-start.5 = (bf16[192,1024]{1,0:T(8,128)(2,1)S(1)}, bf16[192,1024]{1,0:T(8,128)(2,1)S(1)}, u32[]{:S(2)}, u32[]{:S(2)}) collective-permute-start(bf16[192,1024]{1,0:T(8,128)(2,1)S(1)} %add_convert_fusion.5), channel_id=1, source_target_pairs={{2,4},{3,5},{4,2},{5,3},{10,12},{11,13},{12,10},{13,11},{18,20},{1... | collective-permute-start | bytes 1179656 | tf_op jit(solution)/shard_map/ppermute | solution.py:503
  63.4 13.5 %collective-permute-start.10 = (bf16[192,1024]{1,0:T(8,128)(2,1)S(1)}, bf16[192,1024]{1,0:T(8,128)(2,1)S(1)}, u32[]{:S(2)}, u32[]{:S(2)}) collective-permute-start(bf16[192,1024]{1,0:T(8,128)(2,1)S(1)} %add_convert_fusion.1), channel_id=1, source_target_pairs={{0,2},{1,3},{2,0},{3,1},{4,6},{5,7},{6,4},{7,5},{8,10},{9,11},{10,... | collective-permute-start | bytes 1179656 | tf_op jit(solution)/shard_map/ppermute | solution.py:504
where the time goes:
time: 78.1 us; the launch traced here: 77.9 us
  Pallas kernels  34.5 us (44%)
  waiting for transfers between devices  23.5 us (30%)
  starting transfers between devices  18.1 us (23%)
  other arithmetic  1.64 us (2%)
    pallas_call x1, Pallas kernels, front(): pl.pallas_call(functools.partial(front_kernel, geometry), out_shape=[jax....  20.7 us
    ppermute x1, waiting for transfers between devices, scatter_line(): last = lax.ppermute(total(sums[2], across), 'mp', near)  8.01 us
    ppermute x1, waiting for transfers between devices, scatter_line(): first = lax.ppermute(sums[0], 'mp', ends)  7.94 us
    ppermute x1, waiting for transfers between devices, scatter_line(): second = lax.ppermute(sums[1], 'mp', ends)  6.6 us
    pallas_call x1, Pallas kernels, share_rest(): pl.pallas_call(functools.partial(share_kernel, slots), out_shape=[jax.Sha...  5.74 us
    ppermute x1, starting transfers between devices, scatter_line(): last = lax.ppermute(total(sums[2], across), 'mp', near)  5.51 us
    ppermute x2, starting transfers between devices, local(): other = lax.ppermute(group, 'ctx', [(a, a ^ span) for a in range(shards)])  5.15 us
    ppermute x1, starting transfers between devices, scatter_line(): first = lax.ppermute(sums[0], 'mp', ends)  4 us
  transfers between devices with their start and end apart: 11, of which 5 were waited for; matrix products, arithmetic and copies ran while one was open for 1% of the time, Pallas kernels for 12%

commit v1 on v0

--- a/solution.py
+++ b/solution.py
@@ -214,7 +214,12 @@
     return jnp.where(jnp.abs(x) < 0.5, x * series, jnp.exp(x) - 1.0)
 
 
-def local_kernel(poles, first, prod_ref, keep_ref, rates_ref, residues_ref, skip_ref, _, local_out, state_out, pole_out):
+def local_kernel(
+    poles, first, slot, lane_position, prod_ref, keep_ref, rates_ref, residues_ref, skip_ref, out_ref, _,
+    local_out, state_out, pole_out, window_out, sem,
+):
+    copy = columns(lane_position[0], slot, out_ref, window_out, sem)
+    copy.start()
     tiles, T, _ = local_out.shape
     run = T // PARTS
     mine = slice(first * 128, (first + tiles) * 128)
@@ -241,6 +246,7 @@
         return 0
 
     lax.fori_loop(0, tiles, tile_body, 0)
+    copy.wait()
 
 
 def tree(terms):
@@ -249,21 +255,23 @@
     return terms[0]
 
 
-def local_pass(first, tiles, product, keep, rates, residues, skip, after):
+def local_pass(first, tiles, slot, lane_position, product, keep, rates, residues, skip, out_weight, width, after):
     T, poles = product.shape[1], rates.shape[0]
     return pl.pallas_call(
-        functools.partial(local_kernel, poles, first),
+        functools.partial(local_kernel, poles, first, slot),
         out_shape=(
             jax.ShapeDtypeStruct((tiles, T, 128), f32),
             jax.ShapeDtypeStruct((tiles, PARTS * poles, 128), f32),
             jax.ShapeDtypeStruct((poles, tiles * 128), f32),
+            jax.ShapeDtypeStruct((out_weight.shape[0], 2 * width), bf16),
         ),
-        in_specs=[vmem()] * 5 + [pl.BlockSpec(memory_space=pl.ANY)],
-        out_specs=[vmem()] * 3,
-        compiler_params=pltpu.CompilerParams(vmem_limit_bytes=4 * MIB),
+        in_specs=[smem()] + [vmem()] * 5 + [hbm(), pl.BlockSpec(memory_space=pl.ANY)],
+        out_specs=[vmem()] * 4,
+        scratch_shapes=[pltpu.SemaphoreType.DMA],
+        compiler_params=pltpu.CompilerParams(vmem_limit_bytes=8 * MIB),
         cost_estimate=pl.CostEstimate(flops=6 * T * poles * tiles * 128, bytes_accessed=8 * MIB, transcendentals=0),
         name="local_pass",
-    )(product, keep, rates, residues, skip, after)
+    )(lane_position, product, keep, rates, residues, skip, out_weight, after)
 
 
 def first_products(first, last, taps, ids_ref, base):
@@ -326,14 +334,19 @@
 
 def gate_kernel(
     T, poles, spans, cuts, position, lane_position, ids_ref, query_ref, block_ref, visible_ref, taps_ref, rates_ref, skip_ref,
-    out_ref, *rest,
+    out_ref, window_ref, *rest,
 ):
     arrived, rest = rest[: len(spans)], rest[len(spans) :]
     parts, rest = [rest[3 * c : 3 * c + 3] for c in range(cuts)], rest[3 * cuts :]
-    (gated_out, send_out, mine_out, carry, full, window, sem) = rest
+    gated_out, send_out, mine_out, third_out, fourth_out, carry, full, sem = rest
     run = T // PARTS
     tiles = query_ref.shape[1] // 128
-    columns(lane_position[0], 0, out_ref, window, sem).start()
+    copies = [
+        columns(lane_position[0], slot, out_ref, out, sem.at[k])
+        for k, (slot, out) in enumerate(((2, third_out), (3, fourth_out)))
+    ]
+    for copy in copies:
+        copy.start()
     me = position[0]
     base = me * T
     taps = [taps_ref[j] for j in range(3)]
@@ -398,17 +411,20 @@
         top_q = top_q + jnp.where(row == 0, q_shift[0][:, lanes], 0.0) + jnp.where(row == 1, q_shift[1][:, lanes], 0.0)
         top = top + jnp.where(row == 0, fix0[:, lanes], 0.0) + jnp.where(row == 1, fix1[:, lanes], 0.0)
         gated_out[0:16, lanes] = (top_q * top).astype(bf16)
-    columns(lane_position[0], 0, out_ref, window, sem).wait()
-    share(lane_position[0], gated_out, window, send_out, mine_out)
+    share(lane_position[0], gated_out, window_ref, send_out, mine_out)
+    for copy in copies:
+        copy.wait()
 
 
 def target(index, slot):
     chip = index // 2
-    low = chip < 2
-    if slot < 2:
-        return jnp.where(low, 3 - slot, slot)
+    odd = chip % 2
+    if slot == 0:
+        return 3 - 3 * odd
+    if slot == 1:
+        return 1 + odd
     if slot == 2:
-        return jnp.where(low, 1 - chip, 5 - chip)
+        return (chip + 2) % 4
     return chip
 
 
@@ -430,35 +446,28 @@
             out[:, at] = jnp.dot(gated_ref[...], window[:, cols], preferred_element_type=f32).astype(out.dtype)
 
 
-def share_kernel(slots, lane_position, gated_ref, out_ref, *rest):
-    outs, (windows, sem) = rest[:-2], rest[-2:]
-    copies = [columns(lane_position[0], slot, out_ref, windows.at[k], sem.at[k]) for k, slot in enumerate(slots)]
-    for copy in copies:
-        copy.start()
-    for k, copy in enumerate(copies):
-        copy.wait()
-        share(lane_position[0], gated_ref, windows.at[k], outs[2 * k], outs[2 * k + 1])
-
-
-def share_rest(slots, lane_position, gated, out_weight, width):
+def share_kernel(count, lane_position, gated_ref, *rest):
+    windows, outs = rest[:count], rest[count:]
+    for k, window in enumerate(windows):
+        share(lane_position[0], gated_ref, window, outs[2 * k], outs[2 * k + 1])
+
+
+def shares(lane_position, gated, windows, width):
     T, channels = gated.shape
+    count = len(windows)
     return pl.pallas_call(
-        functools.partial(share_kernel, slots),
-        out_shape=[jax.ShapeDtypeStruct((T, width), d) for _ in slots for d in (bf16, f32)],
-        in_specs=[smem(), vmem(), hbm()],
-        out_specs=[vmem()] * (2 * len(slots)),
-        scratch_shapes=[
-            pltpu.VMEM((len(slots), channels, 2 * width), bf16),
-            pltpu.SemaphoreType.DMA((len(slots),)),
-        ],
-        compiler_params=pltpu.CompilerParams(vmem_limit_bytes=20 * MIB),
+        functools.partial(share_kernel, count),
+        out_shape=[jax.ShapeDtypeStruct((T, width), d) for _ in windows for d in (bf16, f32)],
+        in_specs=[smem(), vmem()] + [vmem()] * count,
+        out_specs=[vmem()] * (2 * count),
+        compiler_params=pltpu.CompilerParams(vmem_limit_bytes=4 * MIB),
         cost_estimate=pl.CostEstimate(
-            flops=4 * T * channels * width * len(slots), bytes_accessed=4 * channels * width * len(slots), transcendentals=0),
-        name="share_rest",
-    )(lane_position, gated, out_weight)
-
-
-def gate(T, spans, arrived, position, lane_position, ids, query, parts, block, visible, taps, rates, skip, out_weight, width):
+            flops=4 * T * channels * width * count, bytes_accessed=4 * channels * width * count, transcendentals=0),
+        name="shares",
+    )(lane_position, gated, *windows)
+
+
+def gate(T, spans, arrived, position, lane_position, ids, query, parts, block, visible, taps, rates, skip, out_weight, window, width):
     poles, channels = rates.shape
     return pl.pallas_call(
         functools.partial(gate_kernel, T, poles, tuple(spans), len(parts)),
@@ -466,18 +475,19 @@
             jax.ShapeDtypeStruct(query.shape, bf16),
             jax.ShapeDtypeStruct((T, width), bf16),
             jax.ShapeDtypeStruct((T, width), f32),
+            jax.ShapeDtypeStruct(window.shape, bf16),
+            jax.ShapeDtypeStruct(window.shape, bf16),
         ],
-        in_specs=[smem()] * 3 + [vmem()] * 6 + [hbm()] + [vmem()] * (len(spans) + 3 * len(parts)),
-        out_specs=[vmem()] * 3,
+        in_specs=[smem()] * 3 + [vmem()] * 6 + [hbm()] + [vmem()] * (1 + len(spans) + 3 * len(parts)),
+        out_specs=[vmem()] * 5,
         scratch_shapes=[
             pltpu.VMEM((channels // 128, PARTS * poles, 128), f32),
             pltpu.VMEM((channels // 128, T, 128), f32),
-            pltpu.VMEM((channels, 2 * width), bf16),
-            pltpu.SemaphoreType.DMA,
+            pltpu.SemaphoreType.DMA((2,)),
         ],
-        compiler_params=pltpu.CompilerParams(vmem_limit_bytes=10 * MIB),
+        compiler_params=pltpu.CompilerParams(vmem_limit_bytes=12 * MIB),
         name="gate",
-    )(position, lane_position, ids, query, block, visible, taps, rates, skip, out_weight, *arrived,
+    )(position, lane_position, ids, query, block, visible, taps, rates, skip, out_weight, window, *arrived,
       *[a for part in parts for a in part])
 
 
@@ -485,24 +495,28 @@
     return functools.reduce(lambda a, b: a + b, [t.astype(f32) for t in terms]).astype(bf16)
 
 
-def scatter_line(lane_position, gated, send, mine, out_weight, width):
+def scatter_line(lane_position, gated, send, mine, windows, width):
+    chip = lax.axis_index("mp") // 2
+    inner = (chip == 1) | (chip == 2)
     pair = [(m, m ^ 1) for m in range(8)]
 
     def along(hops):
         return [(a * 2 + c, b * 2 + c) for a, b in hops for c in range(2)]
 
-    ends = along([(0, 1), (3, 2)])
-    middle = along([(1, 2), (2, 1)])
-    near = along([(0, 1), (1, 0), (2, 3), (3, 2)])
-    sums = [total(mine, lax.ppermute(send, "mp", pair))]
-    first = lax.ppermute(sums[0], "mp", ends)
-    rest = share_rest((1, 2, 3), lane_position, gated, out_weight, width)
-    sums += [total(rest[2 * k + 1], lax.ppermute(rest[2 * k], "mp", pair)) for k in range(3)]
-    second = lax.ppermute(sums[1], "mp", ends)
-    across = lax.ppermute(total(sums[0], first), "mp", middle)
-    across2 = lax.ppermute(total(sums[1], second), "mp", middle)
-    last = lax.ppermute(total(sums[2], across), "mp", near)
-    return total(sums[3], across2, last)
+    def where(mask, x):
+        return jnp.where(mask, x.astype(f32), 0.0)
+
+    far = total(mine, lax.ppermute(send, "mp", pair))
+    from_near = lax.ppermute(far, "mp", along([(0, 1), (1, 0), (2, 3), (3, 2)]))
+    send, mine = shares(lane_position, gated, windows[:1], width)
+    second = total(mine, lax.ppermute(send, "mp", pair))
+    from_middle = lax.ppermute(second, "mp", along([(1, 2), (2, 1)]))
+    from_end = lax.ppermute(second, "mp", along([(0, 1), (3, 2)]))
+    send2, mine2, send3, mine3 = shares(lane_position, gated, windows[1:], width)
+    across = total(mine2, lax.ppermute(send2, "mp", pair), where(inner, from_near))
+    own = total(mine3, lax.ppermute(send3, "mp", pair))
+    from_across = lax.ppermute(across, "mp", along([(0, 2), (1, 3), (2, 0), (3, 1)]))
+    return total(own, where(~inner, from_near), from_middle, from_end, from_across)
 
 
 def shifted(value, axis, steps):
@@ -599,18 +613,21 @@
         position, segment_ids.reshape(-1, 128), tokens, norm_gain[None], weight3, short_filter, rates, residues, skip[None])
     cuts = shards.bit_length() - 1
     each = product.shape[0] // cuts
-    group, spans, arrived, parts = block, [], [], []
+    group, spans, arrived, parts, windows = block, [], [], [], []
     for k in range(cuts):
         span = 1 << k
         other = lax.ppermute(group, "ctx", [(a, a ^ span) for a in range(shards)])
         spans.append(span)
         arrived.append(other)
-        parts.append(local_pass(k * each, each, product, keep, rates, residues, skip, group))
+        *part, window = local_pass(
+            k * each, each, min(k, 1), lane_position, product, keep, rates, residues, skip, out_weight, width, group)
+        parts.append(part)
+        windows.append(window)
         if k < cuts - 1:
-            group = join(span, T, position, segment_ids, group, other, taps, rates, parts[k][0])
-    gated, send, mine = gate(T, spans, arrived, position, lane_position, segment_ids, query, parts, block, visible, taps, rates,
-                             skip, out_weight, width)
-    return scatter_line(lane_position, gated, send, mine, out_weight, width)
+            group = join(span, T, position, segment_ids, group, other, taps, rates, part[0])
+    gated, send, mine, third, fourth = gate(T, spans, arrived, position, lane_position, segment_ids, query, parts, block,
+                                            visible, taps, rates, skip, out_weight, windows[0], width)
+    return scatter_line(lane_position, gated, send, mine, [windows[1], third, fourth], width)
 
 
 def solution(mesh):
@@ -628,7 +645,7 @@
     shards, groups = mesh.shape["ctx"], mesh.shape["mp"]
 
     def body(tokens, norm_gain, in_weight, *rest):
-        suits = groups == 8 and shards & (shards - 1) == 0 and shards > 1
+        suits = groups == 8 and shards & (shards - 1) == 0 and shards > 2
         suits = suits and in_weight.shape[2] % 512 == 0 and in_weight.shape[0] % 2048 == 0
         suits = suits and tokens.shape[0] % 64 == 0 and rest[-1].shape[0] % 128 == 0 and rest[1].shape[0] % 8 == 0
         return (local if suits else general)(tokens, norm_gain, in_weight, *rest)

time: 78.1 us -> 76.1 us (0.974)
  waiting for transfers between devices: 23.5 us -> 19.4 us
  other arithmetic: 1.64 us -> 5.44 us
  Pallas kernels: 34.5 us -> 32.5 us
    convert_element_type x6 -> x4, other arithmetic: 1.64 us -> 5.44 us  [total(): functools.reduce(lambda a, b: a + b, [t.astype(f32) for t in terms])]
    ppermute x9 -> x8, waiting for transfers between devices: 22.6 us -> 19.3 us  [the longest x1 14.1 us: scatter_line(): lax.ppermute(across, 'mp', along([(0, 2), (1, 3), (2, 0), (3, 1)]))]
    pallas_call x3 -> x4, Pallas kernels: 9.3 us -> 7.36 us  [the longest x2 4.42 us: local_pass(): pl.pallas_call(functools.partial(local_kernel, poles, first, slot), out_s...]
    ppermute x2, waiting for transfers between devices: 0.92 us -> 0.05 us  [local(): other = lax.ppermute(group, 'ctx', [(a, a ^ span) for a in range(shards)])]
    ppermute x9 -> x8, starting transfers between devices: 13 us -> 13.3 us  [the longest x1 6.31 us: scatter_line(): from_end = lax.ppermute(second, 'mp', along([(0, 1), (3, 2)]))]
  transfers between devices with their start and end apart: 11 -> 10, of which waited for: 5 -> 3; matrix products, arithmetic and copies ran while one was open for 1% -> 4% of each run, Pallas kernels for 12% -> 10%
where the time goes in v1:
time: 76.1 us; the launch traced here: 75.8 us
  Pallas kernels  32.5 us (43%)
  waiting for transfers between devices  19.4 us (25%)
  starting transfers between devices  18.4 us (24%)
  other arithmetic  5.44 us (7%)
    pallas_call x1, Pallas kernels, front(): pl.pallas_call(functools.partial(front_kernel, geometry), out_shape=[jax....  20.3 us
    ppermute x1, waiting for transfers between devices, scatter_line(): lax.ppermute(across, 'mp', along([(0, 2), (1, 3), (2, 0), (3, 1)]))  14.1 us
    ppermute x1, starting transfers between devices, scatter_line(): from_end = lax.ppermute(second, 'mp', along([(0, 1), (3, 2)]))  6.31 us
    convert_element_type x4, other arithmetic, total(): functools.reduce(lambda a, b: a + b, [t.astype(f32) for t in terms])  5.44 us
    ppermute x2, starting transfers between devices, local(): other = lax.ppermute(group, 'ctx', [(a, a ^ span) for a in range(shards)])  5.14 us
    pallas_call x2, Pallas kernels, local_pass(): pl.pallas_call(functools.partial(local_kernel, poles, first, slot), out_s...  4.42 us
    pallas_call x1, Pallas kernels, gate(): pl.pallas_call(functools.partial(gate_kernel, T, poles, tuple(spans), len...  4.09 us
    ppermute x1, waiting for transfers between devices, scatter_line(): from_end = lax.ppermute(second, 'mp', along([(0, 1), (3, 2)]))  3.47 us
  transfers between devices with their start and end apart: 10, of which 3 were waited for; matrix products, arithmetic and copies ran while one was open for 4% of the time, Pallas kernels for 10%

profile of v1, /device:TPU:0, one launch (start us, length us, event | category | flops | bytes accessed | tf_op | source)
XLA Modules:
  0.0 75.8 jit_solution(12562902336052929259)
XLA Ops:
  0.0 20.3 %front.1 = (f32[192,1024]{1,0:T(8,128)S(1)}, f32[8,192,128]{2,1,0:T(8,128)S(1)}, bf16[32,1024]{1,0:T(8,128)(2,1)S(1)}, f32[192,128]{1,0:T(8,128)S(1)}, f32[192,1...) custom-call(s32[1]{0:T(128)} %bitcast.1.position, ...), custom_call_target="tpu_custom_call" | custom-call | tf_op jit(solution)/shard_map/front/pallas_call | solution.py:177
  20.3 3.0 %collective-permute-start = (bf16[32,1024]{1,0:T(8,128)(2,1)S(1)}, bf16[32,1024]{1,0:T(8,128)(2,1)S(1)}, u32[]{:S(2)}, u32[]{:S(2)}) collective-permute-start(bf16[32,1024]{1,0:T(8,128)(2,1)S(1)} %get-tuple-element.34._.mine_ref.block_ref), channel_id=1, source_target_pairs={{0,8},{8,0},{16,24},{24,16},{1,9},{9,1},{17,25},{25,17},{2,10},{10... | collective-permute-start | bytes 196616 | tf_op jit(solution)/shard_map/ppermute | solution.py:619
  23.4 0.0 copy-start
  23.4 2.2 %local_pass.2 = (f32[4,192,128]{2,1,0:T(8,128)S(1)}, f32[4,128,128]{2,1,0:T(8,128)S(1)}, f32[16,512]{1,0:T(8,128)S(1)}, bf16[1024,2048]{1,0:T(8,128)(2,1)S(1)}) custom-call(s32[1]{0:T(128)} %bitcast.lane_position, f32[8,192,128]{2,1,0:T(8,128)S(1)} %get-tuple-element.39.prod_ref, f32[192,128]{1,0:T(8,128)S(1)} %get-tuple-element.40.keep_ref, ...), custom_call_target="tpu_custom_call" | custom-call | flops 9437184 | bytes 8388608 | tf_op jit(solution)/shard_map/local_pass/pallas_call | solution.py:260
  25.6 0.0 collective-permute-done.other_ref.rest_0_
  25.6 0.0 copy-done
  25.6 0.7 join.1._
  26.3 2.1 %collective-permute-start.1 = (bf16[32,1024]{1,0:T(8,128)(2,1)S(1)}, bf16[32,1024]{1,0:T(8,128)(2,1)S(1)}, u32[]{:S(2)}, u32[]{:S(2)}) collective-permute-start(bf16[32,1024]{1,0:T(8,128)(2,1)S(1)} %join.1._), channel_id=1, source_target_pairs={{0,16},{8,24},{16,0},{24,8},{1,17},{9,25},{17,1},{25,9},{2,18},{10... | collective-permute-start | bytes 196616 | tf_op jit(solution)/shard_map/ppermute | solution.py:619
  28.4 2.2 %local_pass.3 = (f32[4,192,128]{2,1,0:T(8,128)S(1)}, f32[4,128,128]{2,1,0:T(8,128)S(1)}, f32[16,512]{1,0:T(8,128)S(1)}, bf16[1024,2048]{1,0:T(8,128)(2,1)S(1)}) custom-call(s32[1]{0:T(128)} %bitcast.lane_position, f32[8,192,128]{2,1,0:T(8,128)S(1)} %get-tuple-element.39.prod_ref, f32[192,128]{1,0:T(8,128)S(1)} %get-tuple-element.40.keep_ref, ...), custom_call_target="tpu_custom_call" | custom-call | flops 9437184 | bytes 8388608 | tf_op jit(solution)/shard_map/local_pass/pallas_call | solution.py:260
  30.6 0.0 collective-permute-done.1.rest_1_
  30.7 4.1 %gate.1 = (bf16[192,1024]{1,0:T(8,128)(2,1)S(1)}, bf16[192,1024]{1,0:T(8,128)(2,1)S(1)}, f32[192,1024]{1,0:T(8,128)S(1)}, bf16[1024,2048]{1,0:T(8,128)(2,1)S(1)}, bf16[1024,2048]{1,0:T(8,128)(2,1)S(1)}) custom-call(s32[1]{0:T(128)} %bitcast.1.position, s32[1]{0:T(128)} %bitcast.lane_position, s32[768]{0:T(1024)S(1)} %copy-done, ...), custom_call_target="tpu_custom_call" | custom-call | tf_op jit(solution)/shard_map/gate/pallas_call | solution.py:472
  34.8 0.1 collective-permute-start.3
  34.8 1.1 %shares.3 = (bf16[192,1024]{1,0:T(8,128)(2,1)S(1)}, f32[192,1024]{1,0:T(8,128)S(1)}) custom-call(s32[1]{0:T(128)} %bitcast.lane_position, bf16[192,1024]{1,0:T(8,128)(2,1)S(1)} %get-tuple-element.49.gated_ref, bf16[1024,2048]{1,0:T(8,128)(2,1)S(1)} %get-tuple-element.56.rest_0_), custom_call_target="tpu_custom_call" | custom-call | flops 805306368 | bytes 4194304 | tf_op jit(solution)/shard_map/shares/pallas_call | solution.py:458
  35.9 0.5 collective-permute-start.5
  36.5 1.9 %shares.2 = (bf16[192,1024]{1,0:T(8,128)(2,1)S(1)}, f32[192,1024]{1,0:T(8,128)S(1)}, bf16[192,1024]{1,0:T(8,128)(2,1)S(1)}, f32[192,1024]{1,0:T(8,128)S(1)}) custom-call(s32[1]{0:T(128)} %bitcast.lane_position, bf16[192,1024]{1,0:T(8,128)(2,1)S(1)} %get-tuple-element.49.gated_ref, bf16[1024,2048]{1,0:T(8,128)(2,1)S(1)} %get-tuple-element.50.rest_0_, ...), custom_call_target="tpu_custom_call" | custom-call | flops 1610612736 | bytes 8388608 | tf_op jit(solution)/shard_map/shares/pallas_call | solution.py:458
  38.3 0.1 collective-permute-start.8
  38.4 0.0 collective-permute-done.3
  38.4 0.8 %add_convert_fusion.1 = bf16[192,1024]{1,0:T(8,128)(2,1)} fusion(f32[192,1024]{1,0:T(8,128)S(1)} %get-tuple-element.54, bf16[192,1024]{1,0:T(8,128)(2,1)S(1)} %collective-permute-done.3), kind=kLoop, calls=%fused_computation.10 | loop fusion | flops 589824 | bytes 1572864 | tf_op jit(solution)/shard_map/convert_element_type | solution.py:495
  39.3 2.1 %collective-permute-start.4 = (bf16[192,1024]{1,0:T(8,128)(2,1)}, bf16[192,1024]{1,0:T(8,128)(2,1)}, u32[]{:S(2)}, u32[]{:S(2)}) collective-permute-start(bf16[192,1024]{1,0:T(8,128)(2,1)} %add_convert_fusion.1), channel_id=1, source_target_pairs={{0,2},{1,3},{2,0},{3,1},{4,6},{5,7},{6,4},{7,5},{8,10},{9,11},{10,... | collective-permute-start | bytes 1179656 | tf_op jit(solution)/shard_map/ppermute | solution.py:510
  41.4 0.2 collective-permute-start.2
  41.6 0.0 collective-permute-done.5
  41.6 1.1 %add_convert_fusion = bf16[192,1024]{1,0:T(8,128)(2,1)S(1)} fusion(f32[192,1024]{1,0:T(8,128)S(1)} %get-tuple-element.57, bf16[192,1024]{1,0:T(8,128)(2,1)} %collective-permute-done.5), kind=kLoop, calls=%fused_computation.9 | loop fusion | flops 589824 | bytes 1572864 | tf_op jit(solution)/shard_map/convert_element_type | solution.py:495
  42.7 0.7 collective-permute-start.6
  43.4 6.3 %collective-permute-start.7 = (bf16[192,1024]{1,0:T(8,128)(2,1)S(1)}, bf16[192,1024]{1,0:T(8,128)(2,1)S(1)}, u32[]{:S(2)}, u32[]{:S(2)}) collective-permute-start(bf16[192,1024]{1,0:T(8,128)(2,1)S(1)} %add_convert_fusion), channel_id=1, source_target_pairs={{0,2},{1,3},{6,4},{7,5},{8,10},{9,11},{14,12},{15,13},{16,18},{17,... | collective-permute-start | bytes 1179656 | tf_op jit(solution)/shard_map/ppermute | solution.py:514
  49.7 0.0 collective-permute-done.8
  49.7 1.8 %collective-permute-done.4 = bf16[192,1024]{1,0:T(8,128)(2,1)} collective-permute-done((bf16[192,1024]{1,0:T(8,128)(2,1)}, bf16[192,1024]{1,0:T(8,128)(2,1)}, u32[]{:S(2)}, u32[]{:S(2)}) %collective-permute-start.4) | collective-permute-done | bytes 393248 | tf_op jit(solution)/shard_map/ppermute | solution.py:510
  51.4 1.3 %fusion.6 = bf16[192,1024]{1,0:T(8,128)(2,1)S(1)} fusion(bf16[192,1024]{1,0:T(8,128)(2,1)} %collective-permute-done.4, f32[192,1024]{1,0:T(8,128)S(1)} %get-tuple-element.59, bf16[192,1024]{1,0:T(8,128)(2,1)} %collective-permute-done.8, pred[]{:T(512)S(6)} %or.3), kind=kLoop, calls=%fused_computation.8 | loop fusion | flops 1179648 | bytes 1966081 | tf_op jit(solution)/shard_map/convert_element_type | solution.py:495
  52.7 3.3 %collective-permute-start.9 = (bf16[192,1024]{1,0:T(8,128)(2,1)S(1)}, bf16[192,1024]{1,0:T(8,128)(2,1)S(1)}, u32[]{:S(2)}, u32[]{:S(2)}) collective-permute-start(bf16[192,1024]{1,0:T(8,128)(2,1)S(1)} %fusion.6), channel_id=1, source_target_pairs={{0,4},{1,5},{2,6},{3,7},{4,0},{5,1},{6,2},{7,3},{8,12},{9,13},{10,... | collective-permute-start | bytes 1179656 | tf_op jit(solution)/shard_map/ppermute | solution.py:518
  56.0 0.0 collective-permute-done.2
  56.0 0.0 collective-permute-done.6
  56.0 3.5 %collective-permute-done.7 = bf16[192,1024]{1,0:T(8,128)(2,1)S(1)} collective-permute-done((bf16[192,1024]{1,0:T(8,128)(2,1)S(1)}, bf16[192,1024]{1,0:T(8,128)(2,1)S(1)}, u32[]{:S(2)}, u32[]{:S(2)}) %collective-permute-start.7) | collective-permute-done | bytes 393248 | tf_op jit(solution)/shard_map/ppermute | solution.py:514
  59.5 14.1 %collective-permute-done.9 = bf16[192,1024]{1,0:T(8,128)(2,1)S(1)} collective-permute-done((bf16[192,1024]{1,0:T(8,128)(2,1)S(1)}, bf16[192,1024]{1,0:T(8,128)(2,1)S(1)}, u32[]{:S(2)}, u32[]{:S(2)}) %collective-permute-start.9) | collective-permute-done | bytes 393248 | tf_op jit(solution)/shard_map/ppermute | solution.py:518
  73.6 2.2 %fusion.4 = bf16[192,1024]{1,0:T(8,128)(2,1)} fusion(bf16[192,1024]{1,0:T(8,128)(2,1)} %collective-permute-done.4, bf16[192,1024]{1,0:T(8,128)(2,1)S(1)} %collective-permute-done.9, bf16[192,1024]{1,0:T(8,128)(2,1)S(1)} %collective-permute-done.7, bf16[192,1024]{1,0:T(8,128)(2,1)S(1)} %collective-permute-done.6, f32[192,1024]{1,0:T(8,128)S(1)} %get-tuple-element.52, ...), kind=kLoop, calls=%fused_computation.6 | loop fusion | flops 2752512 | bytes 3145729 | tf_op jit(solution)/shard_map/convert_element_type | solution.py:495
Async XLA Ops:
  20.3 5.3 %collective-permute-start = (bf16[32,1024]{1,0:T(8,128)(2,1)S(1)}, bf16[32,1024]{1,0:T(8,128)(2,1)S(1)}, u32[]{:S(2)}, u32[]{:S(2)}) collective-permute-start(bf16[32,1024]{1,0:T(8,128)(2,1)S(1)} %get-tuple-element.34._.mine_ref.block_ref), channel_id=1, source_target_pairs={{0,8},{8,0},{16,24},{24,16},{1,9},{9,1},{17,25},{25,17},{2,10},{10... | collective-permute-start | bytes 196616 | tf_op jit(solution)/shard_map/ppermute | solution.py:619
  23.4 2.2 %copy-start = (s32[768]{0:T(1024)S(1)}, s32[768]{0:T(1024)}, u32[]{:S(2)}) copy-start(s32[768]{0:T(1024)} %ids_ref.3) | copy-start | bytes 9220
  26.3 4.4 %collective-permute-start.1 = (bf16[32,1024]{1,0:T(8,128)(2,1)S(1)}, bf16[32,1024]{1,0:T(8,128)(2,1)S(1)}, u32[]{:S(2)}, u32[]{:S(2)}) collective-permute-start(bf16[32,1024]{1,0:T(8,128)(2,1)S(1)} %join.1._), channel_id=1, source_target_pairs={{0,16},{8,24},{16,0},{24,8},{1,17},{9,25},{17,1},{25,9},{2,18},{10... | collective-permute-start | bytes 196616 | tf_op jit(solution)/shard_map/ppermute | solution.py:619
  34.8 3.7 %collective-permute-start.3 = (bf16[192,1024]{1,0:T(8,128)(2,1)S(1)}, bf16[192,1024]{1,0:T(8,128)(2,1)S(1)}, u32[]{:S(2)}, u32[]{:S(2)}) collective-permute-start(bf16[192,1024]{1,0:T(8,128)(2,1)S(1)} %get-tuple-element.55), channel_id=1, source_target_pairs={{0,1},{1,0},{2,3},{3,2},{4,5},{5,4},{6,7},{7,6},{8,9},{9,8},{10,11... | collective-permute-start | bytes 1179656 | tf_op jit(solution)/shard_map/ppermute | solution.py:509
  35.9 5.7 %collective-permute-start.5 = (bf16[192,1024]{1,0:T(8,128)(2,1)S(1)}, bf16[192,1024]{1,0:T(8,128)(2,1)}, u32[]{:S(2)}, u32[]{:S(2)}) collective-permute-start(bf16[192,1024]{1,0:T(8,128)(2,1)S(1)} %get-tuple-element.58), channel_id=1, source_target_pairs={{0,1},{1,0},{2,3},{3,2},{4,5},{5,4},{6,7},{7,6},{8,9},{9,8},{10,11... | collective-permute-start | bytes 1179656 | tf_op jit(solution)/shard_map/ppermute | solution.py:512
  38.3 11.3 %collective-permute-start.8 = (bf16[192,1024]{1,0:T(8,128)(2,1)S(1)}, bf16[192,1024]{1,0:T(8,128)(2,1)}, u32[]{:S(2)}, u32[]{:S(2)}) collective-permute-start(bf16[192,1024]{1,0:T(8,128)(2,1)S(1)} %get-tuple-element.60), channel_id=1, source_target_pairs={{0,1},{1,0},{2,3},{3,2},{4,5},{5,4},{6,7},{7,6},{8,9},{9,8},{10,11... | collective-permute-start | bytes 1179656 | tf_op jit(solution)/shard_map/ppermute | solution.py:516
  39.3 12.2 %collective-permute-start.4 = (bf16[192,1024]{1,0:T(8,128)(2,1)}, bf16[192,1024]{1,0:T(8,128)(2,1)}, u32[]{:S(2)}, u32[]{:S(2)}) collective-permute-start(bf16[192,1024]{1,0:T(8,128)(2,1)} %add_convert_fusion.1), channel_id=1, source_target_pairs={{0,2},{1,3},{2,0},{3,1},{4,6},{5,7},{6,4},{7,5},{8,10},{9,11},{10,... | collective-permute-start | bytes 1179656 | tf_op jit(solution)/shard_map/ppermute | solution.py:510
  41.4 14.7 %collective-permute-start.2 = (bf16[192,1024]{1,0:T(8,128)(2,1)S(1)}, bf16[192,1024]{1,0:T(8,128)(2,1)}, u32[]{:S(2)}, u32[]{:S(2)}) collective-permute-start(bf16[192,1024]{1,0:T(8,128)(2,1)S(1)} %get-tuple-element.53), channel_id=1, source_target_pairs={{0,1},{1,0},{2,3},{3,2},{4,5},{5,4},{6,7},{7,6},{8,9},{9,8},{10,11... | collective-permute-start | bytes 1179656 | tf_op jit(solution)/shard_map/ppermute | solution.py:517
  42.7 13.4 %collective-permute-start.6 = (bf16[192,1024]{1,0:T(8,128)(2,1)S(1)}, bf16[192,1024]{1,0:T(8,128)(2,1)S(1)}, u32[]{:S(2)}, u32[]{:S(2)}) collective-permute-start(bf16[192,1024]{1,0:T(8,128)(2,1)S(1)} %add_convert_fusion), channel_id=1, source_target_pairs={{2,4},{3,5},{4,2},{5,3},{10,12},{11,13},{12,10},{13,11},{18,20},{1... | collective-permute-start | bytes 1179656 | tf_op jit(solution)/shard_map/ppermute | solution.py:513
  43.4 16.2 %collective-permute-start.7 = (bf16[192,1024]{1,0:T(8,128)(2,1)S(1)}, bf16[192,1024]{1,0:T(8,128)(2,1)S(1)}, u32[]{:S(2)}, u32[]{:S(2)}) collective-permute-start(bf16[192,1024]{1,0:T(8,128)(2,1)S(1)} %add_convert_fusion), channel_id=1, source_target_pairs={{0,2},{1,3},{6,4},{7,5},{8,10},{9,11},{14,12},{15,13},{16,18},{17,... | collective-permute-start | bytes 1179656 | tf_op jit(solution)/shard_map/ppermute | solution.py:514
  52.7 20.9 %collective-permute-start.9 = (bf16[192,1024]{1,0:T(8,128)(2,1)S(1)}, bf16[192,1024]{1,0:T(8,128)(2,1)S(1)}, u32[]{:S(2)}, u32[]{:S(2)}) collective-permute-start(bf16[192,1024]{1,0:T(8,128)(2,1)S(1)} %fusion.6), channel_id=1, source_target_pairs={{0,4},{1,5},{2,6},{3,7},{4,0},{5,1},{6,2},{7,3},{8,12},{9,13},{10,... | collective-permute-start | bytes 1179656 | tf_op jit(solution)/shard_map/ppermute | solution.py:518

commit v2 on v1

--- a/solution.py
+++ b/solution.py
@@ -334,19 +334,13 @@
 
 def gate_kernel(
     T, poles, spans, cuts, position, lane_position, ids_ref, query_ref, block_ref, visible_ref, taps_ref, rates_ref, skip_ref,
-    out_ref, window_ref, *rest,
+    window_ref, *rest,
 ):
     arrived, rest = rest[: len(spans)], rest[len(spans) :]
     parts, rest = [rest[3 * c : 3 * c + 3] for c in range(cuts)], rest[3 * cuts :]
-    gated_out, send_out, mine_out, third_out, fourth_out, carry, full, sem = rest
+    gated_out, send_out, mine_out, carry, full = rest
     run = T // PARTS
     tiles = query_ref.shape[1] // 128
-    copies = [
-        columns(lane_position[0], slot, out_ref, out, sem.at[k])
-        for k, (slot, out) in enumerate(((2, third_out), (3, fourth_out)))
-    ]
-    for copy in copies:
-        copy.start()
     me = position[0]
     base = me * T
     taps = [taps_ref[j] for j in range(3)]
@@ -412,8 +406,6 @@
         top = top + jnp.where(row == 0, fix0[:, lanes], 0.0) + jnp.where(row == 1, fix1[:, lanes], 0.0)
         gated_out[0:16, lanes] = (top_q * top).astype(bf16)
     share(lane_position[0], gated_out, window_ref, send_out, mine_out)
-    for copy in copies:
-        copy.wait()
 
 
 def target(index, slot):
@@ -467,7 +459,33 @@
     )(lane_position, gated, *windows)
 
 
-def gate(T, spans, arrived, position, lane_position, ids, query, parts, block, visible, taps, rates, skip, out_weight, window, width):
+def late_share_kernel(slots, lane_position, gated_ref, out_ref, *rest):
+    outs, (windows, sem) = rest[:-2], rest[-2:]
+    copies = [columns(lane_position[0], slot, out_ref, windows.at[k], sem.at[k]) for k, slot in enumerate(slots)]
+    for copy in copies:
+        copy.start()
+    for k, copy in enumerate(copies):
+        copy.wait()
+        share(lane_position[0], gated_ref, windows.at[k], outs[2 * k], outs[2 * k + 1])
+
+
+def late_shares(slots, lane_position, gated, out_weight, width):
+    T, channels = gated.shape
+    count = len(slots)
+    return pl.pallas_call(
+        functools.partial(late_share_kernel, slots),
+        out_shape=[jax.ShapeDtypeStruct((T, width), d) for _ in slots for d in (bf16, f32)],
+        in_specs=[smem(), vmem(), hbm()],
+        out_specs=[vmem()] * (2 * count),
+        scratch_shapes=[pltpu.VMEM((count, channels, 2 * width), bf16), pltpu.SemaphoreType.DMA((count,))],
+        compiler_params=pltpu.CompilerParams(vmem_limit_bytes=10 * MIB),
+        cost_estimate=pl.CostEstimate(
+            flops=4 * T * channels * width * count, bytes_accessed=4 * channels * width * count, transcendentals=0),
+        name="late_shares",
+    )(lane_position, gated, out_weight)
+
+
+def gate(T, spans, arrived, position, lane_position, ids, query, parts, block, visible, taps, rates, skip, window, width):
     poles, channels = rates.shape
     return pl.pallas_call(
         functools.partial(gate_kernel, T, poles, tuple(spans), len(parts)),
@@ -475,19 +493,16 @@
             jax.ShapeDtypeStruct(query.shape, bf16),
             jax.ShapeDtypeStruct((T, width), bf16),
             jax.ShapeDtypeStruct((T, width), f32),
-            jax.ShapeDtypeStruct(window.shape, bf16),
-            jax.ShapeDtypeStruct(window.shape, bf16),
         ],
-        in_specs=[smem()] * 3 + [vmem()] * 6 + [hbm()] + [vmem()] * (1 + len(spans) + 3 * len(parts)),
-        out_specs=[vmem()] * 5,
+        in_specs=[smem()] * 3 + [vmem()] * (7 + len(spans) + 3 * len(parts)),
+        out_specs=[vmem()] * 3,
         scratch_shapes=[
             pltpu.VMEM((channels // 128, PARTS * poles, 128), f32),
             pltpu.VMEM((channels // 128, T, 128), f32),
-            pltpu.SemaphoreType.DMA((2,)),
         ],
-        compiler_params=pltpu.CompilerParams(vmem_limit_bytes=12 * MIB),
+        compiler_params=pltpu.CompilerParams(vmem_limit_bytes=6 * MIB),
         name="gate",
-    )(position, lane_position, ids, query, block, visible, taps, rates, skip, out_weight, window, *arrived,
+    )(position, lane_position, ids, query, block, visible, taps, rates, skip, window, *arrived,
       *[a for part in parts for a in part])
 
 
@@ -495,7 +510,7 @@
     return functools.reduce(lambda a, b: a + b, [t.astype(f32) for t in terms]).astype(bf16)
 
 
-def scatter_line(lane_position, gated, send, mine, windows, width):
+def scatter_line(lane_position, gated, send, mine, window, out_weight, width):
     chip = lax.axis_index("mp") // 2
     inner = (chip == 1) | (chip == 2)
     pair = [(m, m ^ 1) for m in range(8)]
@@ -506,17 +521,22 @@
     def where(mask, x):
         return jnp.where(mask, x.astype(f32), 0.0)
 
-    far = total(mine, lax.ppermute(send, "mp", pair))
-    from_near = lax.ppermute(far, "mp", along([(0, 1), (1, 0), (2, 3), (3, 2)]))
-    send, mine = shares(lane_position, gated, windows[:1], width)
-    second = total(mine, lax.ppermute(send, "mp", pair))
-    from_middle = lax.ppermute(second, "mp", along([(1, 2), (2, 1)]))
-    from_end = lax.ppermute(second, "mp", along([(0, 1), (3, 2)]))
-    send2, mine2, send3, mine3 = shares(lane_position, gated, windows[1:], width)
-    across = total(mine2, lax.ppermute(send2, "mp", pair), where(inner, from_near))
-    own = total(mine3, lax.ppermute(send3, "mp", pair))
+    def hop(x, hops):
+        return lax.ppermute(x, "mp", hops)
+
+    near = along([(0, 1), (1, 0), (2, 3), (3, 2)])
+    traded = hop(send, pair)
+    far = total(mine, traded)
+    from_near = hop(far, near)
+    send, mine = shares(lane_position, gated, [window], width)
+    second = total(mine, hop(send, pair))
+    from_end = hop(second, near)
+    from_middle = hop(second, along([(1, 2), (2, 1)]))
+    send2, mine2, send3, mine3 = late_shares((2, 3), lane_position, gated, out_weight, width)
+    across = total(mine2, hop(send2, pair), where(inner, from_near))
+    own = total(mine3, hop(send3, pair))
     from_across = lax.ppermute(across, "mp", along([(0, 2), (1, 3), (2, 0), (3, 1)]))
-    return total(own, where(~inner, from_near), from_middle, from_end, from_across)
+    return total(own, jnp.where(inner, from_end.astype(f32), from_near.astype(f32)), from_middle, from_across)
 
 
 def shifted(value, axis, steps):
@@ -625,9 +645,9 @@
         windows.append(window)
         if k < cuts - 1:
             group = join(span, T, position, segment_ids, group, other, taps, rates, part[0])
-    gated, send, mine, third, fourth = gate(T, spans, arrived, position, lane_position, segment_ids, query, parts, block,
-                                            visible, taps, rates, skip, out_weight, windows[0], width)
-    return scatter_line(lane_position, gated, send, mine, [windows[1], third, fourth], width)
+    gated, send, mine = gate(T, spans, arrived, position, lane_position, segment_ids, query, parts, block, visible, taps, rates,
+                             skip, windows[0], width)
+    return scatter_line(lane_position, gated, send, mine, windows[1], out_weight, width)
 
 
 def solution(mesh):

time: 76.1 us -> 78.2 us (1.028)
  waiting for transfers between devices: 19.4 us -> 25.9 us
  starting transfers between devices: 18.4 us -> 12.3 us
  Pallas kernels: 32.5 us -> 34.2 us
    ppermute x7, waiting for transfers between devices: 5.25 us -> 16.4 us  [hop(): return lax.ppermute(x, 'mp', hops)]
    ppermute x7, starting transfers between devices: 9.99 us -> 4.08 us  [hop(): return lax.ppermute(x, 'mp', hops)]
    ppermute x1, waiting for transfers between devices: 14.1 us -> 9.46 us  [scatter_line(): lax.ppermute(across, 'mp', along([(0, 2), (1, 3), (2, 0), (3, 1)]))]
    pallas_call x0 -> x1, Pallas kernels: none -> 4.55 us  [late_shares(): pl.pallas_call(functools.partial(late_share_kernel, slots), out_shape=[ja...]
    pallas_call x2 -> x1, Pallas kernels: 2.94 us -> 1.06 us  [shares(): pl.pallas_call(functools.partial(share_kernel, count), out_shape=[jax.Sha...]
    pallas_call x1, Pallas kernels: 4.09 us -> 3.19 us  [gate(): pl.pallas_call(functools.partial(gate_kernel, T, poles, tuple(spans), len...]
  transfers between devices with their start and end apart: 10 -> 10, of which waited for: 3 -> 3; matrix products, arithmetic and copies ran while one was open for 4% -> 4% of each run, Pallas kernels for 10% -> 13%
where the time goes in v2:
time: 78.2 us; the launch traced here: 77.9 us
  Pallas kernels  34.2 us (44%)
  waiting for transfers between devices  25.9 us (33%)
  starting transfers between devices  12.3 us (16%)
  other arithmetic  5.32 us (7%)
    pallas_call x1, Pallas kernels, front(): pl.pallas_call(functools.partial(front_kernel, geometry), out_shape=[jax....  20.3 us
    ppermute x7, waiting for transfers between devices, hop(): return lax.ppermute(x, 'mp', hops)  16.4 us
    ppermute x1, waiting for transfers between devices, scatter_line(): lax.ppermute(across, 'mp', along([(0, 2), (1, 3), (2, 0), (3, 1)]))  9.46 us
    convert_element_type x4, other arithmetic, total(): functools.reduce(lambda a, b: a + b, [t.astype(f32) for t in terms])  5.32 us
    ppermute x2, starting transfers between devices, local(): other = lax.ppermute(group, 'ctx', [(a, a ^ span) for a in range(shards)])  5.14 us
    pallas_call x1, Pallas kernels, late_shares(): pl.pallas_call(functools.partial(late_share_kernel, slots), out_shape=[ja...  4.55 us
    pallas_call x2, Pallas kernels, local_pass(): pl.pallas_call(functools.partial(local_kernel, poles, first, slot), out_s...  4.42 us
    ppermute x7, starting transfers between devices, hop(): return lax.ppermute(x, 'mp', hops)  4.08 us
  transfers between devices with their start and end apart: 10, of which 3 were waited for; matrix products, arithmetic and copies ran while one was open for 4% of the time, Pallas kernels for 13%

profile of v2, /device:TPU:0, one launch (start us, length us, event | category | flops | bytes accessed | tf_op | source)
XLA Modules:
  0.0 77.9 jit_solution(1446459313218969024)
XLA Ops:
  0.0 20.3 %front.1 = (f32[192,1024]{1,0:T(8,128)S(1)}, f32[8,192,128]{2,1,0:T(8,128)S(1)}, bf16[32,1024]{1,0:T(8,128)(2,1)S(1)}, f32[192,128]{1,0:T(8,128)S(1)}, f32[192,1...) custom-call(s32[1]{0:T(128)} %bitcast.1.position, ...), custom_call_target="tpu_custom_call" | custom-call | tf_op jit(solution)/shard_map/front/pallas_call | solution.py:177
  20.3 3.0 %collective-permute-start = (bf16[32,1024]{1,0:T(8,128)(2,1)S(1)}, bf16[32,1024]{1,0:T(8,128)(2,1)S(1)}, u32[]{:S(2)}, u32[]{:S(2)}) collective-permute-start(bf16[32,1024]{1,0:T(8,128)(2,1)S(1)} %get-tuple-element.32._.mine_ref.block_ref), channel_id=1, source_target_pairs={{0,8},{8,0},{16,24},{24,16},{1,9},{9,1},{17,25},{25,17},{2,10},{10... | collective-permute-start | bytes 196616 | tf_op jit(solution)/shard_map/ppermute | solution.py:639
  23.4 0.0 copy-start
  23.4 2.2 %local_pass.2 = (f32[4,192,128]{2,1,0:T(8,128)S(1)}, f32[4,128,128]{2,1,0:T(8,128)S(1)}, f32[16,512]{1,0:T(8,128)S(1)}, bf16[1024,2048]{1,0:T(8,128)(2,1)S(1)}) custom-call(s32[1]{0:T(128)} %bitcast.lane_position, f32[8,192,128]{2,1,0:T(8,128)S(1)} %get-tuple-element.37.prod_ref, f32[192,128]{1,0:T(8,128)S(1)} %get-tuple-element.38.keep_ref, ...), custom_call_target="tpu_custom_call" | custom-call | flops 9437184 | bytes 8388608 | tf_op jit(solution)/shard_map/local_pass/pallas_call | solution.py:260
  25.6 0.0 collective-permute-done.other_ref.rest_0_
  25.6 0.0 copy-done
  25.6 0.7 join.1._
  26.3 2.1 %collective-permute-start.1 = (bf16[32,1024]{1,0:T(8,128)(2,1)S(1)}, bf16[32,1024]{1,0:T(8,128)(2,1)S(1)}, u32[]{:S(2)}, u32[]{:S(2)}) collective-permute-start(bf16[32,1024]{1,0:T(8,128)(2,1)S(1)} %join.1._), channel_id=1, source_target_pairs={{0,16},{8,24},{16,0},{24,8},{1,17},{9,25},{17,1},{25,9},{2,18},{10... | collective-permute-start | bytes 196616 | tf_op jit(solution)/shard_map/ppermute | solution.py:639
  28.4 2.2 %local_pass.3 = (f32[4,192,128]{2,1,0:T(8,128)S(1)}, f32[4,128,128]{2,1,0:T(8,128)S(1)}, f32[16,512]{1,0:T(8,128)S(1)}, bf16[1024,2048]{1,0:T(8,128)(2,1)S(1)}) custom-call(s32[1]{0:T(128)} %bitcast.lane_position, f32[8,192,128]{2,1,0:T(8,128)S(1)} %get-tuple-element.37.prod_ref, f32[192,128]{1,0:T(8,128)S(1)} %get-tuple-element.38.keep_ref, ...), custom_call_target="tpu_custom_call" | custom-call | flops 9437184 | bytes 8388608 | tf_op jit(solution)/shard_map/local_pass/pallas_call | solution.py:260
  30.6 0.0 collective-permute-done.1.rest_1_
  30.7 3.2 %gate.1 = (bf16[192,1024]{1,0:T(8,128)(2,1)S(1)}, bf16[192,1024]{1,0:T(8,128)(2,1)S(1)}, f32[192,1024]{1,0:T(8,128)S(1)}) custom-call(s32[1]{0:T(128)} %bitcast.1.position, s32[1]{0:T(128)} %bitcast.lane_position, s32[768]{0:T(1024)S(1)} %copy-done, f32[192,1024]{1,0:T(8,128)S(1)} %get-tuple-element.31.query_ref, ...), custom_call_target="tpu_custom_call" | custom-call | tf_op jit(solution)/shard_map/gate/pallas_call | solution.py:490
  33.9 0.1 collective-permute-start.5
  33.9 1.1 %shares.1 = (bf16[192,1024]{1,0:T(8,128)(2,1)S(1)}, f32[192,1024]{1,0:T(8,128)S(1)}) custom-call(s32[1]{0:T(128)} %bitcast.lane_position, bf16[192,1024]{1,0:T(8,128)(2,1)S(1)} %get-tuple-element.47.gated_ref, bf16[1024,2048]{1,0:T(8,128)(2,1)S(1)} %get-tuple-element.50.rest_0_), custom_call_target="tpu_custom_call" | custom-call | flops 805306368 | bytes 4194304 | tf_op jit(solution)/shard_map/shares/pallas_call | solution.py:450
  35.0 4.6 %late_shares.1 = (bf16[192,1024]{1,0:T(8,128)(2,1)S(1)}, f32[192,1024]{1,0:T(8,128)S(1)}, bf16[192,1024]{1,0:T(8,128)(2,1)S(1)}, f32[192,1024]{1,0:T(8,128)S(1)}) custom-call(s32[1]{0:T(128)} %bitcast.lane_position, bf16[192,1024]{1,0:T(8,128)(2,1)S(1)} %get-tuple-element.47.gated_ref, bf16[1024,8192]{1,0:T(8,128)(2,1)} %out_ref.5), custom_call_target="tpu_custom_call" | custom-call | flops 1610612736 | bytes 8388608 | tf_op jit(solution)/shard_map/late_shares/pallas_call | solution.py:475
  39.6 0.6 collective-permute-start.3
  40.1 0.1 collective-permute-start.8
  40.2 0.0 collective-permute-done.5
  40.2 0.8 %add_convert_fusion = bf16[192,1024]{1,0:T(8,128)(2,1)} fusion(f32[192,1024]{1,0:T(8,128)S(1)} %get-tuple-element.53, bf16[192,1024]{1,0:T(8,128)(2,1)S(1)} %collective-permute-done.5), kind=kLoop, calls=%fused_computation.8 | loop fusion | flops 589824 | bytes 1572864 | tf_op jit(solution)/shard_map/convert_element_type | solution.py:510
  41.1 2.1 %collective-permute-start.6 = (bf16[192,1024]{1,0:T(8,128)(2,1)}, bf16[192,1024]{1,0:T(8,128)(2,1)}, u32[]{:S(2)}, u32[]{:S(2)}) collective-permute-start(bf16[192,1024]{1,0:T(8,128)(2,1)} %add_convert_fusion), channel_id=1, source_target_pairs={{0,2},{1,3},{2,0},{3,1},{4,6},{5,7},{6,4},{7,5},{8,10},{9,11},{10,... | collective-permute-start | bytes 1179656 | tf_op jit(solution)/shard_map/ppermute | solution.py:525
  43.1 0.2 collective-permute-start.2
  43.3 0.0 collective-permute-done.3
  43.3 1.1 %add_convert_fusion.1 = bf16[192,1024]{1,0:T(8,128)(2,1)S(1)} fusion(f32[192,1024]{1,0:T(8,128)S(1)} %get-tuple-element.51, bf16[192,1024]{1,0:T(8,128)(2,1)} %collective-permute-done.3), kind=kLoop, calls=%fused_computation.9 | loop fusion | flops 589824 | bytes 1572864 | tf_op jit(solution)/shard_map/convert_element_type | solution.py:510
  44.4 0.5 collective-permute-start.4
  44.8 0.7 collective-permute-start.7
  45.5 0.0 collective-permute-done.8
  45.5 7.9 %collective-permute-done.6 = bf16[192,1024]{1,0:T(8,128)(2,1)} collective-permute-done((bf16[192,1024]{1,0:T(8,128)(2,1)}, bf16[192,1024]{1,0:T(8,128)(2,1)}, u32[]{:S(2)}, u32[]{:S(2)}) %collective-permute-start.6) | collective-permute-done | bytes 393248 | tf_op jit(solution)/shard_map/ppermute | solution.py:525
  53.4 1.3 %fusion.5 = bf16[192,1024]{1,0:T(8,128)(2,1)S(1)} fusion(bf16[192,1024]{1,0:T(8,128)(2,1)} %collective-permute-done.6, f32[192,1024]{1,0:T(8,128)S(1)} %get-tuple-element.55, bf16[192,1024]{1,0:T(8,128)(2,1)} %collective-permute-done.8, pred[]{:T(512)S(6)} %or.3), kind=kLoop, calls=%fused_computation.7 | loop fusion | flops 1179648 | bytes 1966081 | tf_op jit(solution)/shard_map/convert_element_type | solution.py:510
  54.7 3.1 %collective-permute-start.9 = (bf16[192,1024]{1,0:T(8,128)(2,1)S(1)}, bf16[192,1024]{1,0:T(8,128)(2,1)S(1)}, u32[]{:S(2)}, u32[]{:S(2)}) collective-permute-start(bf16[192,1024]{1,0:T(8,128)(2,1)S(1)} %fusion.5), channel_id=1, source_target_pairs={{0,4},{1,5},{2,6},{3,7},{4,0},{5,1},{6,2},{7,3},{8,12},{9,13},{10,... | collective-permute-start | bytes 1179656 | tf_op jit(solution)/shard_map/ppermute | solution.py:538
  57.8 0.0 collective-permute-done.2
  57.8 8.5 %collective-permute-done.4 = bf16[192,1024]{1,0:T(8,128)(2,1)S(1)} collective-permute-done((bf16[192,1024]{1,0:T(8,128)(2,1)S(1)}, bf16[192,1024]{1,0:T(8,128)(2,1)S(1)}, u32[]{:S(2)}, u32[]{:S(2)}) %collective-permute-start.4) | collective-permute-done | bytes 393248 | tf_op jit(solution)/shard_map/ppermute | solution.py:525
  66.3 0.0 collective-permute-done.7
  66.3 9.5 %collective-permute-done.9 = bf16[192,1024]{1,0:T(8,128)(2,1)S(1)} collective-permute-done((bf16[192,1024]{1,0:T(8,128)(2,1)S(1)}, bf16[192,1024]{1,0:T(8,128)(2,1)S(1)}, u32[]{:S(2)}, u32[]{:S(2)}) %collective-permute-start.9) | collective-permute-done | bytes 393248 | tf_op jit(solution)/shard_map/ppermute | solution.py:538
  75.8 2.1 %fusion.3 = bf16[192,1024]{1,0:T(8,128)(2,1)} fusion(bf16[192,1024]{1,0:T(8,128)(2,1)} %collective-permute-done.6, bf16[192,1024]{1,0:T(8,128)(2,1)S(1)} %collective-permute-done.9, bf16[192,1024]{1,0:T(8,128)(2,1)S(1)} %collective-permute-done.7, bf16[192,1024]{1,0:T(8,128)(2,1)S(1)} %collective-permute-done.4, f32[192,1024]{1,0:T(8,128)S(1)} %get-tuple-element.48, ...), kind=kLoop, calls=%fused_computation.5 | loop fusion | flops 2555904 | bytes 3145729 | tf_op jit(solution)/shard_map/convert_element_type | solution.py:510
Async XLA Ops:
  20.3 5.3 %collective-permute-start = (bf16[32,1024]{1,0:T(8,128)(2,1)S(1)}, bf16[32,1024]{1,0:T(8,128)(2,1)S(1)}, u32[]{:S(2)}, u32[]{:S(2)}) collective-permute-start(bf16[32,1024]{1,0:T(8,128)(2,1)S(1)} %get-tuple-element.32._.mine_ref.block_ref), channel_id=1, source_target_pairs={{0,8},{8,0},{16,24},{24,16},{1,9},{9,1},{17,25},{25,17},{2,10},{10... | collective-permute-start | bytes 196616 | tf_op jit(solution)/shard_map/ppermute | solution.py:639
  23.4 2.2 %copy-start = (s32[768]{0:T(1024)S(1)}, s32[768]{0:T(1024)}, u32[]{:S(2)}) copy-start(s32[768]{0:T(1024)} %ids_ref.3) | copy-start | bytes 9220
  26.3 4.4 %collective-permute-start.1 = (bf16[32,1024]{1,0:T(8,128)(2,1)S(1)}, bf16[32,1024]{1,0:T(8,128)(2,1)S(1)}, u32[]{:S(2)}, u32[]{:S(2)}) collective-permute-start(bf16[32,1024]{1,0:T(8,128)(2,1)S(1)} %join.1._), channel_id=1, source_target_pairs={{0,16},{8,24},{16,0},{24,8},{1,17},{9,25},{17,1},{25,9},{2,18},{10... | collective-permute-start | bytes 196616 | tf_op jit(solution)/shard_map/ppermute | solution.py:639
  33.9 6.3 %collective-permute-start.5 = (bf16[192,1024]{1,0:T(8,128)(2,1)S(1)}, bf16[192,1024]{1,0:T(8,128)(2,1)S(1)}, u32[]{:S(2)}, u32[]{:S(2)}) collective-permute-start(bf16[192,1024]{1,0:T(8,128)(2,1)S(1)} %get-tuple-element.54), channel_id=1, source_target_pairs={{0,1},{1,0},{2,3},{3,2},{4,5},{5,4},{6,7},{7,6},{8,9},{9,8},{10,11... | collective-permute-start | bytes 1179656 | tf_op jit(solution)/shard_map/ppermute | solution.py:525
  39.6 3.7 %collective-permute-start.3 = (bf16[192,1024]{1,0:T(8,128)(2,1)S(1)}, bf16[192,1024]{1,0:T(8,128)(2,1)}, u32[]{:S(2)}, u32[]{:S(2)}) collective-permute-start(bf16[192,1024]{1,0:T(8,128)(2,1)S(1)} %get-tuple-element.52), channel_id=1, source_target_pairs={{0,1},{1,0},{2,3},{3,2},{4,5},{5,4},{6,7},{7,6},{8,9},{9,8},{10,11... | collective-permute-start | bytes 1179656 | tf_op jit(solution)/shard_map/ppermute | solution.py:525
  40.1 5.4 %collective-permute-start.8 = (bf16[192,1024]{1,0:T(8,128)(2,1)S(1)}, bf16[192,1024]{1,0:T(8,128)(2,1)}, u32[]{:S(2)}, u32[]{:S(2)}) collective-permute-start(bf16[192,1024]{1,0:T(8,128)(2,1)S(1)} %get-tuple-element.56), channel_id=1, source_target_pairs={{0,1},{1,0},{2,3},{3,2},{4,5},{5,4},{6,7},{7,6},{8,9},{9,8},{10,11... | collective-permute-start | bytes 1179656 | tf_op jit(solution)/shard_map/ppermute | solution.py:525
  41.1 12.4 %collective-permute-start.6 = (bf16[192,1024]{1,0:T(8,128)(2,1)}, bf16[192,1024]{1,0:T(8,128)(2,1)}, u32[]{:S(2)}, u32[]{:S(2)}) collective-permute-start(bf16[192,1024]{1,0:T(8,128)(2,1)} %add_convert_fusion), channel_id=1, source_target_pairs={{0,2},{1,3},{2,0},{3,1},{4,6},{5,7},{6,4},{7,5},{8,10},{9,11},{10,... | collective-permute-start | bytes 1179656 | tf_op jit(solution)/shard_map/ppermute | solution.py:525
  43.1 14.7 %collective-permute-start.2 = (bf16[192,1024]{1,0:T(8,128)(2,1)S(1)}, bf16[192,1024]{1,0:T(8,128)(2,1)S(1)}, u32[]{:S(2)}, u32[]{:S(2)}) collective-permute-start(bf16[192,1024]{1,0:T(8,128)(2,1)S(1)} %get-tuple-element.49), channel_id=1, source_target_pairs={{0,1},{1,0},{2,3},{3,2},{4,5},{5,4},{6,7},{7,6},{8,9},{9,8},{10,11... | collective-permute-start | bytes 1179656 | tf_op jit(solution)/shard_map/ppermute | solution.py:525
  44.4 21.9 %collective-permute-start.4 = (bf16[192,1024]{1,0:T(8,128)(2,1)S(1)}, bf16[192,1024]{1,0:T(8,128)(2,1)S(1)}, u32[]{:S(2)}, u32[]{:S(2)}) collective-permute-start(bf16[192,1024]{1,0:T(8,128)(2,1)S(1)} %add_convert_fusion.1), channel_id=1, source_target_pairs={{0,2},{1,3},{2,0},{3,1},{4,6},{5,7},{6,4},{7,5},{8,10},{9,11},{10,... | collective-permute-start | bytes 1179656 | tf_op jit(solution)/shard_map/ppermute | solution.py:525
  44.8 21.5 %collective-permute-start.7 = (bf16[192,1024]{1,0:T(8,128)(2,1)S(1)}, bf16[192,1024]{1,0:T(8,128)(2,1)S(1)}, u32[]{:S(2)}, u32[]{:S(2)}) collective-permute-start(bf16[192,1024]{1,0:T(8,128)(2,1)S(1)} %add_convert_fusion.1), channel_id=1, source_target_pairs={{2,4},{3,5},{4,2},{5,3},{10,12},{11,13},{12,10},{13,11},{18,20},{1... | collective-permute-start | bytes 1179656 | tf_op jit(solution)/shard_map/ppermute | solution.py:525
  54.7 21.1 %collective-permute-start.9 = (bf16[192,1024]{1,0:T(8,128)(2,1)S(1)}, bf16[192,1024]{1,0:T(8,128)(2,1)S(1)}, u32[]{:S(2)}, u32[]{:S(2)}) collective-permute-start(bf16[192,1024]{1,0:T(8,128)(2,1)S(1)} %fusion.5), channel_id=1, source_target_pairs={{0,4},{1,5},{2,6},{3,7},{4,0},{5,1},{6,2},{7,3},{8,12},{9,13},{10,... | collective-permute-start | bytes 1179656 | tf_op jit(solution)/shard_map/ppermute | solution.py:538

commit v3 on v2

--- a/solution.py
+++ b/solution.py
@@ -510,33 +510,51 @@
     return functools.reduce(lambda a, b: a + b, [t.astype(f32) for t in terms]).astype(bf16)
 
 
+def merge_kernel(count, has_inner, lane_position, *rest):
+    terms, picks, out = rest[:count], rest[count:-1], rest[-1]
+    value = terms[0][...].astype(f32)
+    for term in terms[1:]:
+        value = value + term[...].astype(f32)
+    chip = lane_position[0] // 2
+    inner = (chip == 1) | (chip == 2)
+    for pick, wanted in zip(picks, (inner, jnp.logical_not(inner)) if has_inner else (jnp.logical_not(inner),)):
+        value = value + jnp.where(wanted, pick[...].astype(f32), 0.0)
+    out[...] = value.astype(out.dtype)
+
+
+def merge(lane_position, dtype, terms, inner=None, outer=None):
+    picks = [a for a in (inner, outer) if a is not None]
+    terms = [pltpu.with_memory_space_constraint(a, pltpu.VMEM) for a in (*terms, *picks)]
+    return pl.pallas_call(
+        functools.partial(merge_kernel, len(terms) - len(picks), inner is not None),
+        out_shape=jax.ShapeDtypeStruct(terms[0].shape, dtype),
+        in_specs=[smem()] + [vmem()] * len(terms),
+        out_specs=vmem(),
+        compiler_params=pltpu.CompilerParams(vmem_limit_bytes=3 * MIB),
+        name="merge",
+    )(lane_position, *terms)
+
+
 def scatter_line(lane_position, gated, send, mine, window, out_weight, width):
-    chip = lax.axis_index("mp") // 2
-    inner = (chip == 1) | (chip == 2)
     pair = [(m, m ^ 1) for m in range(8)]
 
     def along(hops):
         return [(a * 2 + c, b * 2 + c) for a, b in hops for c in range(2)]
 
-    def where(mask, x):
-        return jnp.where(mask, x.astype(f32), 0.0)
-
-    def hop(x, hops):
-        return lax.ppermute(x, "mp", hops)
-
     near = along([(0, 1), (1, 0), (2, 3), (3, 2)])
-    traded = hop(send, pair)
-    far = total(mine, traded)
-    from_near = hop(far, near)
+    traded = lax.ppermute(send, "mp", pair)
+    far = merge(lane_position, bf16, (mine, traded))
+    from_near = lax.ppermute(far, "mp", near)
     send, mine = shares(lane_position, gated, [window], width)
-    second = total(mine, hop(send, pair))
-    from_end = hop(second, near)
-    from_middle = hop(second, along([(1, 2), (2, 1)]))
+    second = merge(lane_position, bf16, (mine, lax.ppermute(send, "mp", pair)))
+    from_middle = lax.ppermute(second, "mp", along([(1, 2), (2, 1)]))
+    from_end = lax.ppermute(second, "mp", near)
     send2, mine2, send3, mine3 = late_shares((2, 3), lane_position, gated, out_weight, width)
-    across = total(mine2, hop(send2, pair), where(inner, from_near))
-    own = total(mine3, hop(send3, pair))
+    mine2 = merge(lane_position, f32, (mine2, lax.ppermute(send2, "mp", pair)))
+    across = merge(lane_position, bf16, (mine2,), inner=from_near)
     from_across = lax.ppermute(across, "mp", along([(0, 2), (1, 3), (2, 0), (3, 1)]))
-    return total(own, jnp.where(inner, from_end.astype(f32), from_near.astype(f32)), from_middle, from_across)
+    own = merge(lane_position, f32, (mine3, lax.ppermute(send3, "mp", pair), from_middle), inner=from_end, outer=from_near)
+    return total(own, from_across)
 
 
 def shifted(value, axis, steps):

time: 78.2 us -> 75.1 us (0.960)
  other arithmetic: 5.32 us -> 0.84 us
  waiting for transfers between devices: 25.9 us -> 26.8 us
    convert_element_type x4 -> x1, other arithmetic: 5.32 us -> 0.84 us  [total(): functools.reduce(lambda a, b: a + b, [t.astype(f32) for t in terms])]
    ppermute x7, waiting for transfers between devices: 16.4 us -> 19.2 us  [the longest x1 10.7 us: scatter_line(): from_end = lax.ppermute(second, 'mp', near)]
    ppermute x1, waiting for transfers between devices: 9.46 us -> 7.56 us  [scatter_line(): lax.ppermute(across, 'mp', along([(0, 2), (1, 3), (2, 0), (3, 1)]))]
  transfers between devices with their start and end apart: 10 -> 10, of which waited for: 3 -> 3; matrix products, arithmetic and copies ran while one was open for 4% -> 0% of each run, Pallas kernels for 13% -> 14%
where the time goes in v3:
time: 75.1 us; the launch traced here: 75 us
  Pallas kernels  34.8 us (46%)
  waiting for transfers between devices  26.8 us (36%)
  starting transfers between devices  12.4 us (17%)
  other arithmetic  0.84 us (1%)
    pallas_call x1, Pallas kernels, front(): pl.pallas_call(functools.partial(front_kernel, geometry), out_shape=[jax....  20.3 us
    ppermute x1, waiting for transfers between devices, scatter_line(): from_end = lax.ppermute(second, 'mp', near)  10.7 us
    ppermute x1, waiting for transfers between devices, scatter_line(): from_near = lax.ppermute(far, 'mp', near)  8.46 us
    ppermute x1, waiting for transfers between devices, scatter_line(): lax.ppermute(across, 'mp', along([(0, 2), (1, 3), (2, 0), (3, 1)]))  7.56 us
    ppermute x2, starting transfers between devices, local(): other = lax.ppermute(group, 'ctx', [(a, a ^ span) for a in range(shards)])  5.14 us
    pallas_call x1, Pallas kernels, late_shares(): pl.pallas_call(functools.partial(late_share_kernel, slots), out_shape=[ja...  4.53 us
    pallas_call x2, Pallas kernels, local_pass(): pl.pallas_call(functools.partial(local_kernel, poles, first, slot), out_s...  4.42 us
    pallas_call x1, Pallas kernels, gate(): pl.pallas_call(functools.partial(gate_kernel, T, poles, tuple(spans), len...  3.19 us
  transfers between devices with their start and end apart: 10, of which 3 were waited for; matrix products, arithmetic and copies ran while one was open for 0% of the time, Pallas kernels for 14%

profile of v3, /device:TPU:0, one launch (start us, length us, event | category | flops | bytes accessed | tf_op | source)
XLA Modules:
  0.0 75.0 jit_solution(7865314718697548200)
XLA Ops:
  0.0 20.3 %front.1 = (f32[192,1024]{1,0:T(8,128)S(1)}, f32[8,192,128]{2,1,0:T(8,128)S(1)}, bf16[32,1024]{1,0:T(8,128)(2,1)S(1)}, f32[192,128]{1,0:T(8,128)S(1)}, f32[192,1...) custom-call(s32[1]{0:T(128)} %bitcast.1.position, ...), custom_call_target="tpu_custom_call" | custom-call | tf_op jit(solution)/shard_map/front/pallas_call | solution.py:177
  20.3 3.0 %collective-permute-start = (bf16[32,1024]{1,0:T(8,128)(2,1)S(1)}, bf16[32,1024]{1,0:T(8,128)(2,1)S(1)}, u32[]{:S(2)}, u32[]{:S(2)}) collective-permute-start(bf16[32,1024]{1,0:T(8,128)(2,1)S(1)} %get-tuple-element.32._.mine_ref.block_ref), channel_id=1, source_target_pairs={{0,8},{8,0},{16,24},{24,16},{1,9},{9,1},{17,25},{25,17},{2,10},{10... | collective-permute-start | bytes 196616 | tf_op jit(solution)/shard_map/ppermute | solution.py:657
  23.4 0.0 copy-start
  23.4 2.2 %local_pass.2 = (f32[4,192,128]{2,1,0:T(8,128)S(1)}, f32[4,128,128]{2,1,0:T(8,128)S(1)}, f32[16,512]{1,0:T(8,128)S(1)}, bf16[1024,2048]{1,0:T(8,128)(2,1)S(1)}) custom-call(s32[1]{0:T(128)} %bitcast.lane_position, f32[8,192,128]{2,1,0:T(8,128)S(1)} %get-tuple-element.37.prod_ref, f32[192,128]{1,0:T(8,128)S(1)} %get-tuple-element.38.keep_ref, ...), custom_call_target="tpu_custom_call" | custom-call | flops 9437184 | bytes 8388608 | tf_op jit(solution)/shard_map/local_pass/pallas_call | solution.py:260
  25.6 0.0 collective-permute-done.other_ref.rest_0_
  25.6 0.0 copy-done
  25.6 0.7 join.1._
  26.3 2.1 %collective-permute-start.1 = (bf16[32,1024]{1,0:T(8,128)(2,1)S(1)}, bf16[32,1024]{1,0:T(8,128)(2,1)S(1)}, u32[]{:S(2)}, u32[]{:S(2)}) collective-permute-start(bf16[32,1024]{1,0:T(8,128)(2,1)S(1)} %join.1._), channel_id=1, source_target_pairs={{0,16},{8,24},{16,0},{24,8},{1,17},{9,25},{17,1},{25,9},{2,18},{10... | collective-permute-start | bytes 196616 | tf_op jit(solution)/shard_map/ppermute | solution.py:657
  28.4 2.2 %local_pass.3 = (f32[4,192,128]{2,1,0:T(8,128)S(1)}, f32[4,128,128]{2,1,0:T(8,128)S(1)}, f32[16,512]{1,0:T(8,128)S(1)}, bf16[1024,2048]{1,0:T(8,128)(2,1)S(1)}) custom-call(s32[1]{0:T(128)} %bitcast.lane_position, f32[8,192,128]{2,1,0:T(8,128)S(1)} %get-tuple-element.37.prod_ref, f32[192,128]{1,0:T(8,128)S(1)} %get-tuple-element.38.keep_ref, ...), custom_call_target="tpu_custom_call" | custom-call | flops 9437184 | bytes 8388608 | tf_op jit(solution)/shard_map/local_pass/pallas_call | solution.py:260
  30.6 0.0 collective-permute-done.1.rest_1_
  30.7 3.2 %gate.1 = (bf16[192,1024]{1,0:T(8,128)(2,1)S(1)}, bf16[192,1024]{1,0:T(8,128)(2,1)S(1)}, f32[192,1024]{1,0:T(8,128)S(1)}) custom-call(s32[1]{0:T(128)} %bitcast.1.position, s32[1]{0:T(128)} %bitcast.lane_position, s32[768]{0:T(1024)S(1)} %copy-done, f32[192,1024]{1,0:T(8,128)S(1)} %get-tuple-element.31.query_ref, ...), custom_call_target="tpu_custom_call" | custom-call | tf_op jit(solution)/shard_map/gate/pallas_call | solution.py:490
  33.9 0.1 collective-permute-start.6
  33.9 1.1 %shares.1 = (bf16[192,1024]{1,0:T(8,128)(2,1)S(1)}, f32[192,1024]{1,0:T(8,128)S(1)}) custom-call(s32[1]{0:T(128)} %bitcast.lane_position, bf16[192,1024]{1,0:T(8,128)(2,1)S(1)} %get-tuple-element.47.gated_ref, bf16[1024,2048]{1,0:T(8,128)(2,1)S(1)} %get-tuple-element.50.rest_0_), custom_call_target="tpu_custom_call" | custom-call | flops 805306368 | bytes 4194304 | tf_op jit(solution)/shard_map/shares/pallas_call | solution.py:450
  35.0 0.6 collective-permute-start.3
  35.6 4.5 %late_shares.1 = (bf16[192,1024]{1,0:T(8,128)(2,1)S(1)}, f32[192,1024]{1,0:T(8,128)S(1)}, bf16[192,1024]{1,0:T(8,128)(2,1)S(1)}, f32[192,1024]{1,0:T(8,128)S(1)}) custom-call(s32[1]{0:T(128)} %bitcast.lane_position, bf16[192,1024]{1,0:T(8,128)(2,1)S(1)} %get-tuple-element.47.gated_ref, bf16[1024,8192]{1,0:T(8,128)(2,1)} %out_ref.5), custom_call_target="tpu_custom_call" | custom-call | flops 1610612736 | bytes 8388608 | tf_op jit(solution)/shard_map/late_shares/pallas_call | solution.py:475
  40.1 0.1 collective-permute-start.8
  40.2 0.0 collective-permute-done.6.rest_1_
  40.2 0.1 merge.6
  40.3 2.1 %collective-permute-start.7 = (bf16[192,1024]{1,0:T(8,128)(2,1)S(1)}, bf16[192,1024]{1,0:T(8,128)(2,1)S(1)}, u32[]{:S(2)}, u32[]{:S(2)}) collective-permute-start(bf16[192,1024]{1,0:T(8,128)(2,1)S(1)} %merge.6), channel_id=1, source_target_pairs={{0,2},{1,3},{2,0},{3,1},{4,6},{5,7},{6,4},{7,5},{8,10},{9,11},{10,... | collective-permute-start | bytes 1179656 | tf_op jit(solution)/shard_map/ppermute | solution.py:547
  42.5 0.2 collective-permute-start.2
  42.7 0.0 collective-permute-done.3.rest_1_
  42.7 0.1 merge.5
  42.8 0.4 collective-permute-start.5
  43.2 0.7 collective-permute-start.4
  43.9 0.0 collective-permute-done.8.rest_1_
  43.9 0.1 merge.8.rest_0_
  44.0 8.5 %collective-permute-done.7.rest_4_.rest_1_ = bf16[192,1024]{1,0:T(8,128)(2,1)S(1)} collective-permute-done((bf16[192,1024]{1,0:T(8,128)(2,1)S(1)}, bf16[192,1024]{1,0:T(8,128)(2,1)S(1)}, u32[]{:S(2)}, u32[]{:S(2)}) %collective-permute-start.7) | collective-permute-done | bytes 393248 | tf_op jit(solution)/shard_map/ppermute | solution.py:547
  52.4 0.1 merge.9
  52.5 3.1 %collective-permute-start.9 = (bf16[192,1024]{1,0:T(8,128)(2,1)S(1)}, bf16[192,1024]{1,0:T(8,128)(2,1)S(1)}, u32[]{:S(2)}, u32[]{:S(2)}) collective-permute-start(bf16[192,1024]{1,0:T(8,128)(2,1)S(1)} %merge.9), channel_id=1, source_target_pairs={{0,4},{1,5},{2,6},{3,7},{4,0},{5,1},{6,2},{7,3},{8,12},{9,13},{10,... | collective-permute-start | bytes 1179656 | tf_op jit(solution)/shard_map/ppermute | solution.py:555
  55.6 0.0 collective-permute-done.2.rest_1_
  55.6 10.7 %collective-permute-done.5.rest_3_ = bf16[192,1024]{1,0:T(8,128)(2,1)S(1)} collective-permute-done((bf16[192,1024]{1,0:T(8,128)(2,1)S(1)}, bf16[192,1024]{1,0:T(8,128)(2,1)S(1)}, u32[]{:S(2)}, u32[]{:S(2)}) %collective-permute-start.5) | collective-permute-done | bytes 393248 | tf_op jit(solution)/shard_map/ppermute | solution.py:551
  66.3 0.0 collective-permute-done.4.rest_2_
  66.3 0.3 merge.7
  66.6 7.6 %collective-permute-done.9 = bf16[192,1024]{1,0:T(8,128)(2,1)S(1)} collective-permute-done((bf16[192,1024]{1,0:T(8,128)(2,1)S(1)}, bf16[192,1024]{1,0:T(8,128)(2,1)S(1)}, u32[]{:S(2)}, u32[]{:S(2)}) %collective-permute-start.9) | collective-permute-done | bytes 393248 | tf_op jit(solution)/shard_map/ppermute | solution.py:555
  74.1 0.8 %add_convert_fusion = bf16[192,1024]{1,0:T(8,128)(2,1)} fusion(f32[192,1024]{1,0:T(8,128)S(1)} %merge.7, bf16[192,1024]{1,0:T(8,128)(2,1)S(1)} %collective-permute-done.9), kind=kLoop, calls=%fused_computation | loop fusion | flops 589824 | bytes 1572864 | tf_op jit(solution)/shard_map/convert_element_type | solution.py:510
Async XLA Ops:
  20.3 5.3 %collective-permute-start = (bf16[32,1024]{1,0:T(8,128)(2,1)S(1)}, bf16[32,1024]{1,0:T(8,128)(2,1)S(1)}, u32[]{:S(2)}, u32[]{:S(2)}) collective-permute-start(bf16[32,1024]{1,0:T(8,128)(2,1)S(1)} %get-tuple-element.32._.mine_ref.block_ref), channel_id=1, source_target_pairs={{0,8},{8,0},{16,24},{24,16},{1,9},{9,1},{17,25},{25,17},{2,10},{10... | collective-permute-start | bytes 196616 | tf_op jit(solution)/shard_map/ppermute | solution.py:657
  23.4 2.2 %copy-start = (s32[768]{0:T(1024)S(1)}, s32[768]{0:T(1024)}, u32[]{:S(2)}) copy-start(s32[768]{0:T(1024)} %ids_ref.3) | copy-start | bytes 9220
  26.3 4.4 %collective-permute-start.1 = (bf16[32,1024]{1,0:T(8,128)(2,1)S(1)}, bf16[32,1024]{1,0:T(8,128)(2,1)S(1)}, u32[]{:S(2)}, u32[]{:S(2)}) collective-permute-start(bf16[32,1024]{1,0:T(8,128)(2,1)S(1)} %join.1._), channel_id=1, source_target_pairs={{0,16},{8,24},{16,0},{24,8},{1,17},{9,25},{17,1},{25,9},{2,18},{10... | collective-permute-start | bytes 196616 | tf_op jit(solution)/shard_map/ppermute | solution.py:657
  33.9 6.4 %collective-permute-start.6 = (bf16[192,1024]{1,0:T(8,128)(2,1)S(1)}, bf16[192,1024]{1,0:T(8,128)(2,1)S(1)}, u32[]{:S(2)}, u32[]{:S(2)}) collective-permute-start(bf16[192,1024]{1,0:T(8,128)(2,1)S(1)} %get-tuple-element.54), channel_id=1, source_target_pairs={{0,1},{1,0},{2,3},{3,2},{4,5},{5,4},{6,7},{7,6},{8,9},{9,8},{10,11... | collective-permute-start | bytes 1179656 | tf_op jit(solution)/shard_map/ppermute | solution.py:545
  35.0 7.7 %collective-permute-start.3 = (bf16[192,1024]{1,0:T(8,128)(2,1)S(1)}, bf16[192,1024]{1,0:T(8,128)(2,1)S(1)}, u32[]{:S(2)}, u32[]{:S(2)}) collective-permute-start(bf16[192,1024]{1,0:T(8,128)(2,1)S(1)} %get-tuple-element.52), channel_id=1, source_target_pairs={{0,1},{1,0},{2,3},{3,2},{4,5},{5,4},{6,7},{7,6},{8,9},{9,8},{10,11... | collective-permute-start | bytes 1179656 | tf_op jit(solution)/shard_map/ppermute | solution.py:549
  40.1 3.8 %collective-permute-start.8 = (bf16[192,1024]{1,0:T(8,128)(2,1)S(1)}, bf16[192,1024]{1,0:T(8,128)(2,1)S(1)}, u32[]{:S(2)}, u32[]{:S(2)}) collective-permute-start(bf16[192,1024]{1,0:T(8,128)(2,1)S(1)} %get-tuple-element.56), channel_id=1, source_target_pairs={{0,1},{1,0},{2,3},{3,2},{4,5},{5,4},{6,7},{7,6},{8,9},{9,8},{10,11... | collective-permute-start | bytes 1179656 | tf_op jit(solution)/shard_map/ppermute | solution.py:553
  40.3 12.1 %collective-permute-start.7 = (bf16[192,1024]{1,0:T(8,128)(2,1)S(1)}, bf16[192,1024]{1,0:T(8,128)(2,1)S(1)}, u32[]{:S(2)}, u32[]{:S(2)}) collective-permute-start(bf16[192,1024]{1,0:T(8,128)(2,1)S(1)} %merge.6), channel_id=1, source_target_pairs={{0,2},{1,3},{2,0},{3,1},{4,6},{5,7},{6,4},{7,5},{8,10},{9,11},{10,... | collective-permute-start | bytes 1179656 | tf_op jit(solution)/shard_map/ppermute | solution.py:547
  42.5 13.2 %collective-permute-start.2 = (bf16[192,1024]{1,0:T(8,128)(2,1)S(1)}, bf16[192,1024]{1,0:T(8,128)(2,1)S(1)}, u32[]{:S(2)}, u32[]{:S(2)}) collective-permute-start(bf16[192,1024]{1,0:T(8,128)(2,1)S(1)} %get-tuple-element.49), channel_id=1, source_target_pairs={{0,1},{1,0},{2,3},{3,2},{4,5},{5,4},{6,7},{7,6},{8,9},{9,8},{10,11... | collective-permute-start | bytes 1179656 | tf_op jit(solution)/shard_map/ppermute | solution.py:556
  42.8 23.5 %collective-permute-start.5 = (bf16[192,1024]{1,0:T(8,128)(2,1)S(1)}, bf16[192,1024]{1,0:T(8,128)(2,1)S(1)}, u32[]{:S(2)}, u32[]{:S(2)}) collective-permute-start(bf16[192,1024]{1,0:T(8,128)(2,1)S(1)} %merge.5), channel_id=1, source_target_pairs={{0,2},{1,3},{2,0},{3,1},{4,6},{5,7},{6,4},{7,5},{8,10},{9,11},{10,... | collective-permute-start | bytes 1179656 | tf_op jit(solution)/shard_map/ppermute | solution.py:551
  43.2 23.1 %collective-permute-start.4 = (bf16[192,1024]{1,0:T(8,128)(2,1)S(1)}, bf16[192,1024]{1,0:T(8,128)(2,1)S(1)}, u32[]{:S(2)}, u32[]{:S(2)}) collective-permute-start(bf16[192,1024]{1,0:T(8,128)(2,1)S(1)} %merge.5), channel_id=1, source_target_pairs={{2,4},{3,5},{4,2},{5,3},{10,12},{11,13},{12,10},{13,11},{18,20},{1... | collective-permute-start | bytes 1179656 | tf_op jit(solution)/shard_map/ppermute | solution.py:550
  52.5 21.6 %collective-permute-start.9 = (bf16[192,1024]{1,0:T(8,128)(2,1)S(1)}, bf16[192,1024]{1,0:T(8,128)(2,1)S(1)}, u32[]{:S(2)}, u32[]{:S(2)}) collective-permute-start(bf16[192,1024]{1,0:T(8,128)(2,1)S(1)} %merge.9), channel_id=1, source_target_pairs={{0,4},{1,5},{2,6},{3,7},{4,0},{5,1},{6,2},{7,3},{8,12},{9,13},{10,... | collective-permute-start | bytes 1179656 | tf_op jit(solution)/shard_map/ppermute | solution.py:555

commit v4 on v3

--- a/solution.py
+++ b/solution.py
@@ -334,13 +334,15 @@
 
 def gate_kernel(
     T, poles, spans, cuts, position, lane_position, ids_ref, query_ref, block_ref, visible_ref, taps_ref, rates_ref, skip_ref,
-    window_ref, *rest,
+    window_ref, out_ref, *rest,
 ):
     arrived, rest = rest[: len(spans)], rest[len(spans) :]
     parts, rest = [rest[3 * c : 3 * c + 3] for c in range(cuts)], rest[3 * cuts :]
-    gated_out, send_out, mine_out, carry, full = rest
+    gated_out, send_out, mine_out, third_out, carry, full, sem = rest
     run = T // PARTS
     tiles = query_ref.shape[1] // 128
+    copy = columns(lane_position[0], 2, out_ref, third_out, sem)
+    copy.start()
     me = position[0]
     base = me * T
     taps = [taps_ref[j] for j in range(3)]
@@ -406,6 +408,7 @@
         top = top + jnp.where(row == 0, fix0[:, lanes], 0.0) + jnp.where(row == 1, fix1[:, lanes], 0.0)
         gated_out[0:16, lanes] = (top_q * top).astype(bf16)
     share(lane_position[0], gated_out, window_ref, send_out, mine_out)
+    copy.wait()
 
 
 def target(index, slot):
@@ -459,33 +462,31 @@
     )(lane_position, gated, *windows)
 
 
-def late_share_kernel(slots, lane_position, gated_ref, out_ref, *rest):
-    outs, (windows, sem) = rest[:-2], rest[-2:]
-    copies = [columns(lane_position[0], slot, out_ref, windows.at[k], sem.at[k]) for k, slot in enumerate(slots)]
-    for copy in copies:
-        copy.start()
-    for k, copy in enumerate(copies):
-        copy.wait()
-        share(lane_position[0], gated_ref, windows.at[k], outs[2 * k], outs[2 * k + 1])
-
-
-def late_shares(slots, lane_position, gated, out_weight, width):
+def late_share_kernel(slot, lane_position, gated_ref, window_ref, out_ref, *rest):
+    outs, (window, sem) = rest[:-2], rest[-2:]
+    copy = columns(lane_position[0], slot, out_ref, window, sem)
+    copy.start()
+    share(lane_position[0], gated_ref, window_ref, outs[0], outs[1])
+    copy.wait()
+    share(lane_position[0], gated_ref, window, outs[2], outs[3])
+
+
+def late_shares(slot, lane_position, gated, window, out_weight, width):
     T, channels = gated.shape
-    count = len(slots)
     return pl.pallas_call(
-        functools.partial(late_share_kernel, slots),
-        out_shape=[jax.ShapeDtypeStruct((T, width), d) for _ in slots for d in (bf16, f32)],
-        in_specs=[smem(), vmem(), hbm()],
-        out_specs=[vmem()] * (2 * count),
-        scratch_shapes=[pltpu.VMEM((count, channels, 2 * width), bf16), pltpu.SemaphoreType.DMA((count,))],
-        compiler_params=pltpu.CompilerParams(vmem_limit_bytes=10 * MIB),
+        functools.partial(late_share_kernel, slot),
+        out_shape=[jax.ShapeDtypeStruct((T, width), d) for d in (bf16, f32, bf16, f32)],
+        in_specs=[smem(), vmem(), vmem(), hbm()],
+        out_specs=[vmem()] * 4,
+        scratch_shapes=[pltpu.VMEM((channels, 2 * width), bf16), pltpu.SemaphoreType.DMA],
+        compiler_params=pltpu.CompilerParams(vmem_limit_bytes=6 * MIB),
         cost_estimate=pl.CostEstimate(
-            flops=4 * T * channels * width * count, bytes_accessed=4 * channels * width * count, transcendentals=0),
+            flops=8 * T * channels * width, bytes_accessed=8 * channels * width, transcendentals=0),
         name="late_shares",
-    )(lane_position, gated, out_weight)
-
-
-def gate(T, spans, arrived, position, lane_position, ids, query, parts, block, visible, taps, rates, skip, window, width):
+    )(lane_position, gated, window, out_weight)
+
+
+def gate(T, spans, arrived, position, lane_position, ids, query, parts, block, visible, taps, rates, skip, window, out_weight, width):
     poles, channels = rates.shape
     return pl.pallas_call(
         functools.partial(gate_kernel, T, poles, tuple(spans), len(parts)),
@@ -493,16 +494,18 @@
             jax.ShapeDtypeStruct(query.shape, bf16),
             jax.ShapeDtypeStruct((T, width), bf16),
             jax.ShapeDtypeStruct((T, width), f32),
+            pltpu.VMEM(window.shape, bf16),
         ],
-        in_specs=[smem()] * 3 + [vmem()] * (7 + len(spans) + 3 * len(parts)),
-        out_specs=[vmem()] * 3,
+        in_specs=[smem()] * 3 + [vmem()] * 7 + [hbm()] + [vmem()] * (len(spans) + 3 * len(parts)),
+        out_specs=[vmem()] * 4,
         scratch_shapes=[
             pltpu.VMEM((channels // 128, PARTS * poles, 128), f32),
             pltpu.VMEM((channels // 128, T, 128), f32),
+            pltpu.SemaphoreType.DMA,
         ],
-        compiler_params=pltpu.CompilerParams(vmem_limit_bytes=6 * MIB),
+        compiler_params=pltpu.CompilerParams(vmem_limit_bytes=8 * MIB),
         name="gate",
-    )(position, lane_position, ids, query, block, visible, taps, rates, skip, window, *arrived,
+    )(position, lane_position, ids, query, block, visible, taps, rates, skip, window, out_weight, *arrived,
       *[a for part in parts for a in part])
 
 
@@ -535,7 +538,7 @@
     )(lane_position, *terms)
 
 
-def scatter_line(lane_position, gated, send, mine, window, out_weight, width):
+def scatter_line(lane_position, gated, send, mine, window, third, out_weight, width):
     pair = [(m, m ^ 1) for m in range(8)]
 
     def along(hops):
@@ -548,8 +551,8 @@
     send, mine = shares(lane_position, gated, [window], width)
     second = merge(lane_position, bf16, (mine, lax.ppermute(send, "mp", pair)))
     from_middle = lax.ppermute(second, "mp", along([(1, 2), (2, 1)]))
-    from_end = lax.ppermute(second, "mp", near)
-    send2, mine2, send3, mine3 = late_shares((2, 3), lane_position, gated, out_weight, width)
+    from_end = lax.ppermute(second, "mp", along([(0, 1), (3, 2)]))
+    send2, mine2, send3, mine3 = late_shares(3, lane_position, gated, third, out_weight, width)
     mine2 = merge(lane_position, f32, (mine2, lax.ppermute(send2, "mp", pair)))
     across = merge(lane_position, bf16, (mine2,), inner=from_near)
     from_across = lax.ppermute(across, "mp", along([(0, 2), (1, 3), (2, 0), (3, 1)]))
@@ -663,9 +666,9 @@
         windows.append(window)
         if k < cuts - 1:
             group = join(span, T, position, segment_ids, group, other, taps, rates, part[0])
-    gated, send, mine = gate(T, spans, arrived, position, lane_position, segment_ids, query, parts, block, visible, taps, rates,
-                             skip, windows[0], width)
-    return scatter_line(lane_position, gated, send, mine, windows[1], out_weight, width)
+    gated, send, mine, third = gate(T, spans, arrived, position, lane_position, segment_ids, query, parts, block, visible, taps, rates,
+                             skip, windows[0], out_weight, width)
+    return scatter_line(lane_position, gated, send, mine, windows[1], third, out_weight, width)
 
 
 def solution(mesh):

time: 75.1 us -> 75.6 us (level)
  starting transfers between devices: 12.4 us -> 14.5 us
  waiting for transfers between devices: 26.8 us -> 25.5 us
    ppermute x1, waiting for transfers between devices: 7.56 us -> 14.3 us  [scatter_line(): lax.ppermute(across, 'mp', along([(0, 2), (1, 3), (2, 0), (3, 1)]))]
    ppermute x1, waiting for transfers between devices: 10.7 us -> 4.76 us  [scatter_line(): from_end = lax.ppermute(second, 'mp', along([(0, 1), (3, 2)]))]
    ppermute x1, waiting for transfers between devices: 8.46 us -> 6.4 us  [scatter_line(): from_near = lax.ppermute(far, 'mp', near)]
    ppermute x1, starting transfers between devices: 0.42 us -> 2.29 us  [scatter_line(): from_end = lax.ppermute(second, 'mp', along([(0, 1), (3, 2)]))]
where the time goes in v4:
time: 75.6 us; the launch traced here: 75.4 us
  Pallas kernels  34.4 us (46%)
  waiting for transfers between devices  25.5 us (34%)
  starting transfers between devices  14.5 us (19%)
  other arithmetic  0.84 us (1%)
    pallas_call x1, Pallas kernels, front(): pl.pallas_call(functools.partial(front_kernel, geometry), out_shape=[jax....  20.3 us
    ppermute x1, waiting for transfers between devices, scatter_line(): lax.ppermute(across, 'mp', along([(0, 2), (1, 3), (2, 0), (3, 1)]))  14.3 us
    ppermute x1, waiting for transfers between devices, scatter_line(): from_near = lax.ppermute(far, 'mp', near)  6.4 us
    ppermute x2, starting transfers between devices, local(): other = lax.ppermute(group, 'ctx', [(a, a ^ span) for a in range(shards)])  5.14 us
    ppermute x1, waiting for transfers between devices, scatter_line(): from_end = lax.ppermute(second, 'mp', along([(0, 1), (3, 2)]))  4.76 us
    pallas_call x2, Pallas kernels, local_pass(): pl.pallas_call(functools.partial(local_kernel, poles, first, slot), out_s...  4.42 us
    pallas_call x1, Pallas kernels, late_shares(): pl.pallas_call(functools.partial(late_share_kernel, slot), out_shape=[jax...  4.11 us
    ppermute x1, starting transfers between devices, scatter_line(): lax.ppermute(across, 'mp', along([(0, 2), (1, 3), (2, 0), (3, 1)]))  3.32 us
  transfers between devices with their start and end apart: 10, of which 3 were waited for; matrix products, arithmetic and copies ran while one was open for 0% of the time, Pallas kernels for 14%

profile of v4, /device:TPU:0, one launch (start us, length us, event | category | flops | bytes accessed | tf_op | source)
XLA Modules:
  0.0 75.4 jit_solution(8785625000260209555)
XLA Ops:
  0.0 20.3 %front.1 = (f32[192,1024]{1,0:T(8,128)S(1)}, f32[8,192,128]{2,1,0:T(8,128)S(1)}, bf16[32,1024]{1,0:T(8,128)(2,1)S(1)}, f32[192,128]{1,0:T(8,128)S(1)}, f32[192,1...) custom-call(s32[1]{0:T(128)} %bitcast.1.position, ...), custom_call_target="tpu_custom_call" | custom-call | tf_op jit(solution)/shard_map/front/pallas_call | solution.py:177
  20.3 3.0 %collective-permute-start = (bf16[32,1024]{1,0:T(8,128)(2,1)S(1)}, bf16[32,1024]{1,0:T(8,128)(2,1)S(1)}, u32[]{:S(2)}, u32[]{:S(2)}) collective-permute-start(bf16[32,1024]{1,0:T(8,128)(2,1)S(1)} %get-tuple-element.33._.mine_ref.block_ref), channel_id=1, source_target_pairs={{0,8},{8,0},{16,24},{24,16},{1,9},{9,1},{17,25},{25,17},{2,10},{10... | collective-permute-start | bytes 196616 | tf_op jit(solution)/shard_map/ppermute | solution.py:660
  23.4 0.0 copy-start
  23.4 2.2 %local_pass.2 = (f32[4,192,128]{2,1,0:T(8,128)S(1)}, f32[4,128,128]{2,1,0:T(8,128)S(1)}, f32[16,512]{1,0:T(8,128)S(1)}, bf16[1024,2048]{1,0:T(8,128)(2,1)S(1)}) custom-call(s32[1]{0:T(128)} %bitcast.lane_position, f32[8,192,128]{2,1,0:T(8,128)S(1)} %get-tuple-element.38.prod_ref, f32[192,128]{1,0:T(8,128)S(1)} %get-tuple-element.39.keep_ref, ...), custom_call_target="tpu_custom_call" | custom-call | flops 9437184 | bytes 8388608 | tf_op jit(solution)/shard_map/local_pass/pallas_call | solution.py:260
  25.6 0.0 collective-permute-done.other_ref.rest_0_
  25.6 0.0 copy-done
  25.6 0.7 join.1._
  26.3 2.1 %collective-permute-start.1 = (bf16[32,1024]{1,0:T(8,128)(2,1)S(1)}, bf16[32,1024]{1,0:T(8,128)(2,1)S(1)}, u32[]{:S(2)}, u32[]{:S(2)}) collective-permute-start(bf16[32,1024]{1,0:T(8,128)(2,1)S(1)} %join.1._), channel_id=1, source_target_pairs={{0,16},{8,24},{16,0},{24,8},{1,17},{9,25},{17,1},{25,9},{2,18},{10... | collective-permute-start | bytes 196616 | tf_op jit(solution)/shard_map/ppermute | solution.py:660
  28.4 2.2 %local_pass.3 = (f32[4,192,128]{2,1,0:T(8,128)S(1)}, f32[4,128,128]{2,1,0:T(8,128)S(1)}, f32[16,512]{1,0:T(8,128)S(1)}, bf16[1024,2048]{1,0:T(8,128)(2,1)S(1)}) custom-call(s32[1]{0:T(128)} %bitcast.lane_position, f32[8,192,128]{2,1,0:T(8,128)S(1)} %get-tuple-element.38.prod_ref, f32[192,128]{1,0:T(8,128)S(1)} %get-tuple-element.39.keep_ref, ...), custom_call_target="tpu_custom_call" | custom-call | flops 9437184 | bytes 8388608 | tf_op jit(solution)/shard_map/local_pass/pallas_call | solution.py:260
  30.6 0.0 collective-permute-done.1.rest_1_
  30.7 3.2 %gate.1 = (bf16[192,1024]{1,0:T(8,128)(2,1)S(1)}, bf16[192,1024]{1,0:T(8,128)(2,1)S(1)}, f32[192,1024]{1,0:T(8,128)S(1)}, bf16[1024,2048]{1,0:T(8,128)(2,1)S(1)}) custom-call(s32[1]{0:T(128)} %bitcast.1.position, s32[1]{0:T(128)} %bitcast.lane_position, s32[768]{0:T(1024)S(1)} %copy-done, f32[192,1024]{1,0:T(8,128)S(1)} %get-tuple-element.32.query_ref, ...), custom_call_target="tpu_custom_call" | custom-call | tf_op jit(solution)/shard_map/gate/pallas_call | solution.py:491
  33.9 0.1 collective-permute-start.6
  34.0 1.1 %shares.1 = (bf16[192,1024]{1,0:T(8,128)(2,1)S(1)}, f32[192,1024]{1,0:T(8,128)S(1)}) custom-call(s32[1]{0:T(128)} %bitcast.lane_position, bf16[192,1024]{1,0:T(8,128)(2,1)S(1)} %get-tuple-element.48.gated_ref, bf16[1024,2048]{1,0:T(8,128)(2,1)S(1)} %get-tuple-element.52.rest_0_), custom_call_target="tpu_custom_call" | custom-call | flops 805306368 | bytes 4194304 | tf_op jit(solution)/shard_map/shares/pallas_call | solution.py:453
  35.0 0.6 collective-permute-start.3
  35.6 4.1 %late_shares.1 = (bf16[192,1024]{1,0:T(8,128)(2,1)S(1)}, f32[192,1024]{1,0:T(8,128)S(1)}, bf16[192,1024]{1,0:T(8,128)(2,1)S(1)}, f32[192,1024]{1,0:T(8,128)S(1)}) custom-call(s32[1]{0:T(128)} %bitcast.lane_position, bf16[192,1024]{1,0:T(8,128)(2,1)S(1)} %get-tuple-element.48.gated_ref, bf16[1024,2048]{1,0:T(8,128)(2,1)S(1)} %get-tuple-element.49.window_ref, ...), custom_call_target="tpu_custom_call" | custom-call | flops 1610612736 | bytes 8388608 | tf_op jit(solution)/shard_map/late_shares/pallas_call | solution.py:476
  39.7 0.1 collective-permute-start.8
  39.8 0.0 collective-permute-done.6.rest_1_
  39.8 0.1 merge.6
  39.9 2.1 %collective-permute-start.7 = (bf16[192,1024]{1,0:T(8,128)(2,1)S(1)}, bf16[192,1024]{1,0:T(8,128)(2,1)S(1)}, u32[]{:S(2)}, u32[]{:S(2)}) collective-permute-start(bf16[192,1024]{1,0:T(8,128)(2,1)S(1)} %merge.6), channel_id=1, source_target_pairs={{0,2},{1,3},{2,0},{3,1},{4,6},{5,7},{6,4},{7,5},{8,10},{9,11},{10,... | collective-permute-start | bytes 1179656 | tf_op jit(solution)/shard_map/ppermute | solution.py:550
  42.1 0.2 collective-permute-start.2
  42.2 0.0 collective-permute-done.3.rest_1_
  42.2 0.1 merge.5
  42.3 2.3 %collective-permute-start.5 = (bf16[192,1024]{1,0:T(8,128)(2,1)S(1)}, bf16[192,1024]{1,0:T(8,128)(2,1)S(1)}, u32[]{:S(2)}, u32[]{:S(2)}) collective-permute-start(bf16[192,1024]{1,0:T(8,128)(2,1)S(1)} %merge.5), channel_id=1, source_target_pairs={{0,2},{1,3},{6,4},{7,5},{8,10},{9,11},{14,12},{15,13},{16,18},{17,... | collective-permute-start | bytes 1179656 | tf_op jit(solution)/shard_map/ppermute | solution.py:554
  44.6 0.7 collective-permute-start.4
  45.3 0.0 collective-permute-done.8.rest_1_
  45.3 0.1 merge.8.rest_0_
  45.4 6.4 %collective-permute-done.7.rest_4_.rest_1_ = bf16[192,1024]{1,0:T(8,128)(2,1)S(1)} collective-permute-done((bf16[192,1024]{1,0:T(8,128)(2,1)S(1)}, bf16[192,1024]{1,0:T(8,128)(2,1)S(1)}, u32[]{:S(2)}, u32[]{:S(2)}) %collective-permute-start.7) | collective-permute-done | bytes 393248 | tf_op jit(solution)/shard_map/ppermute | solution.py:550
  51.8 0.1 merge.9
  51.9 3.3 %collective-permute-start.9 = (bf16[192,1024]{1,0:T(8,128)(2,1)S(1)}, bf16[192,1024]{1,0:T(8,128)(2,1)S(1)}, u32[]{:S(2)}, u32[]{:S(2)}) collective-permute-start(bf16[192,1024]{1,0:T(8,128)(2,1)S(1)} %merge.9), channel_id=1, source_target_pairs={{0,4},{1,5},{2,6},{3,7},{4,0},{5,1},{6,2},{7,3},{8,12},{9,13},{10,... | collective-permute-start | bytes 1179656 | tf_op jit(solution)/shard_map/ppermute | solution.py:558
  55.2 0.0 collective-permute-done.2.rest_1_
  55.2 4.8 %collective-permute-done.5.rest_3_ = bf16[192,1024]{1,0:T(8,128)(2,1)S(1)} collective-permute-done((bf16[192,1024]{1,0:T(8,128)(2,1)S(1)}, bf16[192,1024]{1,0:T(8,128)(2,1)S(1)}, u32[]{:S(2)}, u32[]{:S(2)}) %collective-permute-start.5) | collective-permute-done | bytes 393248 | tf_op jit(solution)/shard_map/ppermute | solution.py:554
  60.0 0.0 collective-permute-done.4.rest_2_
  60.0 0.3 merge.7
  60.3 14.3 %collective-permute-done.9 = bf16[192,1024]{1,0:T(8,128)(2,1)S(1)} collective-permute-done((bf16[192,1024]{1,0:T(8,128)(2,1)S(1)}, bf16[192,1024]{1,0:T(8,128)(2,1)S(1)}, u32[]{:S(2)}, u32[]{:S(2)}) %collective-permute-start.9) | collective-permute-done | bytes 393248 | tf_op jit(solution)/shard_map/ppermute | solution.py:558
  74.6 0.8 %add_convert_fusion = bf16[192,1024]{1,0:T(8,128)(2,1)} fusion(f32[192,1024]{1,0:T(8,128)S(1)} %merge.7, bf16[192,1024]{1,0:T(8,128)(2,1)S(1)} %collective-permute-done.9), kind=kLoop, calls=%fused_computation | loop fusion | flops 589824 | bytes 1572864 | tf_op jit(solution)/shard_map/convert_element_type | solution.py:513
Async XLA Ops:
  20.3 5.3 %collective-permute-start = (bf16[32,1024]{1,0:T(8,128)(2,1)S(1)}, bf16[32,1024]{1,0:T(8,128)(2,1)S(1)}, u32[]{:S(2)}, u32[]{:S(2)}) collective-permute-start(bf16[32,1024]{1,0:T(8,128)(2,1)S(1)} %get-tuple-element.33._.mine_ref.block_ref), channel_id=1, source_target_pairs={{0,8},{8,0},{16,24},{24,16},{1,9},{9,1},{17,25},{25,17},{2,10},{10... | collective-permute-start | bytes 196616 | tf_op jit(solution)/shard_map/ppermute | solution.py:660
  23.4 2.2 %copy-start = (s32[768]{0:T(1024)S(1)}, s32[768]{0:T(1024)}, u32[]{:S(2)}) copy-start(s32[768]{0:T(1024)} %ids_ref.3) | copy-start | bytes 9220
  26.3 4.4 %collective-permute-start.1 = (bf16[32,1024]{1,0:T(8,128)(2,1)S(1)}, bf16[32,1024]{1,0:T(8,128)(2,1)S(1)}, u32[]{:S(2)}, u32[]{:S(2)}) collective-permute-start(bf16[32,1024]{1,0:T(8,128)(2,1)S(1)} %join.1._), channel_id=1, source_target_pairs={{0,16},{8,24},{16,0},{24,8},{1,17},{9,25},{17,1},{25,9},{2,18},{10... | collective-permute-start | bytes 196616 | tf_op jit(solution)/shard_map/ppermute | solution.py:660
  33.9 5.9 %collective-permute-start.6 = (bf16[192,1024]{1,0:T(8,128)(2,1)S(1)}, bf16[192,1024]{1,0:T(8,128)(2,1)S(1)}, u32[]{:S(2)}, u32[]{:S(2)}) collective-permute-start(bf16[192,1024]{1,0:T(8,128)(2,1)S(1)} %get-tuple-element.56), channel_id=1, source_target_pairs={{0,1},{1,0},{2,3},{3,2},{4,5},{5,4},{6,7},{7,6},{8,9},{9,8},{10,11... | collective-permute-start | bytes 1179656 | tf_op jit(solution)/shard_map/ppermute | solution.py:548
  35.0 7.2 %collective-permute-start.3 = (bf16[192,1024]{1,0:T(8,128)(2,1)S(1)}, bf16[192,1024]{1,0:T(8,128)(2,1)S(1)}, u32[]{:S(2)}, u32[]{:S(2)}) collective-permute-start(bf16[192,1024]{1,0:T(8,128)(2,1)S(1)} %get-tuple-element.54), channel_id=1, source_target_pairs={{0,1},{1,0},{2,3},{3,2},{4,5},{5,4},{6,7},{7,6},{8,9},{9,8},{10,11... | collective-permute-start | bytes 1179656 | tf_op jit(solution)/shard_map/ppermute | solution.py:552
  39.7 5.6 %collective-permute-start.8 = (bf16[192,1024]{1,0:T(8,128)(2,1)S(1)}, bf16[192,1024]{1,0:T(8,128)(2,1)S(1)}, u32[]{:S(2)}, u32[]{:S(2)}) collective-permute-start(bf16[192,1024]{1,0:T(8,128)(2,1)S(1)} %get-tuple-element.58), channel_id=1, source_target_pairs={{0,1},{1,0},{2,3},{3,2},{4,5},{5,4},{6,7},{7,6},{8,9},{9,8},{10,11... | collective-permute-start | bytes 1179656 | tf_op jit(solution)/shard_map/ppermute | solution.py:556
  39.9 11.9 %collective-permute-start.7 = (bf16[192,1024]{1,0:T(8,128)(2,1)S(1)}, bf16[192,1024]{1,0:T(8,128)(2,1)S(1)}, u32[]{:S(2)}, u32[]{:S(2)}) collective-permute-start(bf16[192,1024]{1,0:T(8,128)(2,1)S(1)} %merge.6), channel_id=1, source_target_pairs={{0,2},{1,3},{2,0},{3,1},{4,6},{5,7},{6,4},{7,5},{8,10},{9,11},{10,... | collective-permute-start | bytes 1179656 | tf_op jit(solution)/shard_map/ppermute | solution.py:550
  42.1 13.2 %collective-permute-start.2 = (bf16[192,1024]{1,0:T(8,128)(2,1)S(1)}, bf16[192,1024]{1,0:T(8,128)(2,1)S(1)}, u32[]{:S(2)}, u32[]{:S(2)}) collective-permute-start(bf16[192,1024]{1,0:T(8,128)(2,1)S(1)} %get-tuple-element.51), channel_id=1, source_target_pairs={{0,1},{1,0},{2,3},{3,2},{4,5},{5,4},{6,7},{7,6},{8,9},{9,8},{10,11... | collective-permute-start | bytes 1179656 | tf_op jit(solution)/shard_map/ppermute | solution.py:559
  42.3 17.7 %collective-permute-start.5 = (bf16[192,1024]{1,0:T(8,128)(2,1)S(1)}, bf16[192,1024]{1,0:T(8,128)(2,1)S(1)}, u32[]{:S(2)}, u32[]{:S(2)}) collective-permute-start(bf16[192,1024]{1,0:T(8,128)(2,1)S(1)} %merge.5), channel_id=1, source_target_pairs={{0,2},{1,3},{6,4},{7,5},{8,10},{9,11},{14,12},{15,13},{16,18},{17,... | collective-permute-start | bytes 1179656 | tf_op jit(solution)/shard_map/ppermute | solution.py:554
  44.6 15.4 %collective-permute-start.4 = (bf16[192,1024]{1,0:T(8,128)(2,1)S(1)}, bf16[192,1024]{1,0:T(8,128)(2,1)S(1)}, u32[]{:S(2)}, u32[]{:S(2)}) collective-permute-start(bf16[192,1024]{1,0:T(8,128)(2,1)S(1)} %merge.5), channel_id=1, source_target_pairs={{2,4},{3,5},{4,2},{5,3},{10,12},{11,13},{12,10},{13,11},{18,20},{1... | collective-permute-start | bytes 1179656 | tf_op jit(solution)/shard_map/ppermute | solution.py:553
  51.9 22.7 %collective-permute-start.9 = (bf16[192,1024]{1,0:T(8,128)(2,1)S(1)}, bf16[192,1024]{1,0:T(8,128)(2,1)S(1)}, u32[]{:S(2)}, u32[]{:S(2)}) collective-permute-start(bf16[192,1024]{1,0:T(8,128)(2,1)S(1)} %merge.9), channel_id=1, source_target_pairs={{0,4},{1,5},{2,6},{3,7},{4,0},{5,1},{6,2},{7,3},{8,12},{9,13},{10,... | collective-permute-start | bytes 1179656 | tf_op jit(solution)/shard_map/ppermute | solution.py:558

commit v5 on v4

--- a/solution.py
+++ b/solution.py
@@ -267,7 +267,7 @@
         ),
         in_specs=[smem()] + [vmem()] * 5 + [hbm(), pl.BlockSpec(memory_space=pl.ANY)],
         out_specs=[vmem()] * 4,
-        scratch_shapes=[pltpu.SemaphoreType.DMA],
+        scratch_shapes=[pltpu.SemaphoreType.DMA((STREAMS,))],
         compiler_params=pltpu.CompilerParams(vmem_limit_bytes=8 * MIB),
         cost_estimate=pl.CostEstimate(flops=6 * T * poles * tiles * 128, bytes_accessed=8 * MIB, transcendentals=0),
         name="local_pass",
@@ -413,20 +413,40 @@
 
 def target(index, slot):
     chip = index // 2
-    odd = chip % 2
     if slot == 0:
-        return 3 - 3 * odd
+        return 3 - 3 * (chip % 2)
     if slot == 1:
-        return 1 + odd
+        return jnp.where(chip < 2, 2, 1)
     if slot == 2:
-        return (chip + 2) % 4
+        return jnp.where(chip < 2, 1 + 2 * chip, 2 * (chip - 2))
     return chip
 
 
+class Copies:
+    def __init__(self, copies):
+        self.copies = copies
+
+    def start(self):
+        for copy in self.copies:
+            copy.start()
+
+    def wait(self):
+        for copy in self.copies:
+            copy.wait()
+
+
+STREAMS = 4
+
+
 def columns(index, slot, out_ref, window, sem):
-    both = window.shape[1]
+    channels, both = window.shape
     start = pl.multiple_of(target(index, slot) * both, both)
-    return pltpu.make_async_copy(out_ref.at[:, pl.ds(start, both)], window, sem)
+    each = channels // STREAMS
+    return Copies([
+        pltpu.make_async_copy(
+            out_ref.at[pl.ds(k * each, each), pl.ds(start, both)], window.at[pl.ds(k * each, each)], sem.at[k])
+        for k in range(STREAMS)
+    ])
 
 
 def share(index, gated_ref, window, send_out, mine_out):
@@ -478,7 +498,7 @@
         out_shape=[jax.ShapeDtypeStruct((T, width), d) for d in (bf16, f32, bf16, f32)],
         in_specs=[smem(), vmem(), vmem(), hbm()],
         out_specs=[vmem()] * 4,
-        scratch_shapes=[pltpu.VMEM((channels, 2 * width), bf16), pltpu.SemaphoreType.DMA],
+        scratch_shapes=[pltpu.VMEM((channels, 2 * width), bf16), pltpu.SemaphoreType.DMA((STREAMS,))],
         compiler_params=pltpu.CompilerParams(vmem_limit_bytes=6 * MIB),
         cost_estimate=pl.CostEstimate(
             flops=8 * T * channels * width, bytes_accessed=8 * channels * width, transcendentals=0),
@@ -501,7 +521,7 @@
         scratch_shapes=[
             pltpu.VMEM((channels // 128, PARTS * poles, 128), f32),
             pltpu.VMEM((channels // 128, T, 128), f32),
-            pltpu.SemaphoreType.DMA,
+            pltpu.SemaphoreType.DMA((STREAMS,)),
         ],
         compiler_params=pltpu.CompilerParams(vmem_limit_bytes=8 * MIB),
         name="gate",
@@ -551,13 +571,13 @@
     send, mine = shares(lane_position, gated, [window], width)
     second = merge(lane_position, bf16, (mine, lax.ppermute(send, "mp", pair)))
     from_middle = lax.ppermute(second, "mp", along([(1, 2), (2, 1)]))
-    from_end = lax.ppermute(second, "mp", along([(0, 1), (3, 2)]))
+    from_end = lax.ppermute(second, "mp", along([(0, 2), (3, 1)]))
     send2, mine2, send3, mine3 = late_shares(3, lane_position, gated, third, out_weight, width)
     mine2 = merge(lane_position, f32, (mine2, lax.ppermute(send2, "mp", pair)))
-    across = merge(lane_position, bf16, (mine2,), inner=from_near)
-    from_across = lax.ppermute(across, "mp", along([(0, 2), (1, 3), (2, 0), (3, 1)]))
-    own = merge(lane_position, f32, (mine3, lax.ppermute(send3, "mp", pair), from_middle), inner=from_end, outer=from_near)
-    return total(own, from_across)
+    onward = merge(lane_position, bf16, (mine2,), inner=from_near)
+    from_round = lax.ppermute(onward, "mp", along([(0, 1), (1, 3), (3, 2), (2, 0)]))
+    own = merge(lane_position, f32, (mine3, lax.ppermute(send3, "mp", pair), from_middle, from_end), outer=from_near)
+    return total(own, from_round)
 
 
 def shifted(value, axis, steps):

time: 75.6 us -> 75.7 us (level)
  starting transfers between devices: 14.5 us -> 15.7 us
  waiting for transfers between devices: 25.5 us -> 24.3 us
    ppermute x1, waiting for transfers between devices: 6.4 us -> 4.16 us  [scatter_line(): from_near = lax.ppermute(far, 'mp', near)]
    ppermute x2, starting transfers between devices: 5.6 us -> 6.79 us  [the longest x1 4.52 us: scatter_line(): from_end = lax.ppermute(second, 'mp', along([(0, 2), (3, 1)]))]
    ppermute x2, waiting for transfers between devices: 19.1 us -> 20.1 us  [the longest x1 14.3 us: scatter_line(): lax.ppermute(onward, 'mp', along([(0, 1), (1, 3), (3, 2), (2, 0)]))]
where the time goes in v5:
time: 75.7 us; the launch traced here: 75.5 us
  Pallas kernels  34.6 us (46%)
  waiting for transfers between devices  24.3 us (32%)
  starting transfers between devices  15.7 us (21%)
  other arithmetic  0.84 us (1%)
    pallas_call x1, Pallas kernels, front(): pl.pallas_call(functools.partial(front_kernel, geometry), out_shape=[jax....  20.3 us
    ppermute x1, waiting for transfers between devices, scatter_line(): lax.ppermute(onward, 'mp', along([(0, 1), (1, 3), (3, 2), (2, 0)]))  14.3 us
    ppermute x1, waiting for transfers between devices, scatter_line(): from_end = lax.ppermute(second, 'mp', along([(0, 2), (3, 1)]))  5.83 us
    ppermute x2, starting transfers between devices, local(): other = lax.ppermute(group, 'ctx', [(a, a ^ span) for a in range(shards)])  5.13 us
    ppermute x1, starting transfers between devices, scatter_line(): from_end = lax.ppermute(second, 'mp', along([(0, 2), (3, 1)]))  4.52 us
    pallas_call x2, Pallas kernels, local_pass(): pl.pallas_call(functools.partial(local_kernel, poles, first, slot), out_s...  4.45 us
    ppermute x1, waiting for transfers between devices, scatter_line(): from_near = lax.ppermute(far, 'mp', near)  4.16 us
    pallas_call x1, Pallas kernels, late_shares(): pl.pallas_call(functools.partial(late_share_kernel, slot), out_shape=[jax...  4.12 us
  transfers between devices with their start and end apart: 10, of which 3 were waited for; matrix products, arithmetic and copies ran while one was open for 0% of the time, Pallas kernels for 14%

profile of v5, /device:TPU:0, one launch (start us, length us, event | category | flops | bytes accessed | tf_op | source)
XLA Modules:
  0.0 75.5 jit_solution(807145927889083990)
XLA Ops:
  0.0 20.3 %front.1 = (f32[192,1024]{1,0:T(8,128)S(1)}, f32[8,192,128]{2,1,0:T(8,128)S(1)}, bf16[32,1024]{1,0:T(8,128)(2,1)S(1)}, f32[192,128]{1,0:T(8,128)S(1)}, f32[192,1...) custom-call(s32[1]{0:T(128)} %bitcast.1.position, ...), custom_call_target="tpu_custom_call" | custom-call | tf_op jit(solution)/shard_map/front/pallas_call | solution.py:177
  20.3 3.0 %collective-permute-start = (bf16[32,1024]{1,0:T(8,128)(2,1)S(1)}, bf16[32,1024]{1,0:T(8,128)(2,1)S(1)}, u32[]{:S(2)}, u32[]{:S(2)}) collective-permute-start(bf16[32,1024]{1,0:T(8,128)(2,1)S(1)} %get-tuple-element.33._.mine_ref.block_ref), channel_id=1, source_target_pairs={{0,8},{8,0},{16,24},{24,16},{1,9},{9,1},{17,25},{25,17},{2,10},{10... | collective-permute-start | bytes 196616 | tf_op jit(solution)/shard_map/ppermute | solution.py:680
  23.4 0.0 copy-start
  23.4 2.2 %local_pass.2 = (f32[4,192,128]{2,1,0:T(8,128)S(1)}, f32[4,128,128]{2,1,0:T(8,128)S(1)}, f32[16,512]{1,0:T(8,128)S(1)}, bf16[1024,2048]{1,0:T(8,128)(2,1)S(1)}) custom-call(s32[1]{0:T(128)} %bitcast.lane_position, f32[8,192,128]{2,1,0:T(8,128)S(1)} %get-tuple-element.38.prod_ref, f32[192,128]{1,0:T(8,128)S(1)} %get-tuple-element.39.keep_ref, ...), custom_call_target="tpu_custom_call" | custom-call | flops 9437184 | bytes 8388608 | tf_op jit(solution)/shard_map/local_pass/pallas_call | solution.py:260
  25.6 0.0 collective-permute-done.other_ref.rest_0_
  25.6 0.0 copy-done
  25.6 0.7 join.1._
  26.3 2.1 %collective-permute-start.1 = (bf16[32,1024]{1,0:T(8,128)(2,1)S(1)}, bf16[32,1024]{1,0:T(8,128)(2,1)S(1)}, u32[]{:S(2)}, u32[]{:S(2)}) collective-permute-start(bf16[32,1024]{1,0:T(8,128)(2,1)S(1)} %join.1._), channel_id=1, source_target_pairs={{0,16},{8,24},{16,0},{24,8},{1,17},{9,25},{17,1},{25,9},{2,18},{10... | collective-permute-start | bytes 196616 | tf_op jit(solution)/shard_map/ppermute | solution.py:680
  28.4 2.2 %local_pass.3 = (f32[4,192,128]{2,1,0:T(8,128)S(1)}, f32[4,128,128]{2,1,0:T(8,128)S(1)}, f32[16,512]{1,0:T(8,128)S(1)}, bf16[1024,2048]{1,0:T(8,128)(2,1)S(1)}) custom-call(s32[1]{0:T(128)} %bitcast.lane_position, f32[8,192,128]{2,1,0:T(8,128)S(1)} %get-tuple-element.38.prod_ref, f32[192,128]{1,0:T(8,128)S(1)} %get-tuple-element.39.keep_ref, ...), custom_call_target="tpu_custom_call" | custom-call | flops 9437184 | bytes 8388608 | tf_op jit(solution)/shard_map/local_pass/pallas_call | solution.py:260
  30.6 0.0 collective-permute-done.1.rest_1_
  30.7 3.3 %gate.1 = (bf16[192,1024]{1,0:T(8,128)(2,1)S(1)}, bf16[192,1024]{1,0:T(8,128)(2,1)S(1)}, f32[192,1024]{1,0:T(8,128)S(1)}, bf16[1024,2048]{1,0:T(8,128)(2,1)S(1)}) custom-call(s32[1]{0:T(128)} %bitcast.1.position, s32[1]{0:T(128)} %bitcast.lane_position, s32[768]{0:T(1024)S(1)} %copy-done, f32[192,1024]{1,0:T(8,128)S(1)} %get-tuple-element.32.query_ref, ...), custom_call_target="tpu_custom_call" | custom-call | tf_op jit(solution)/shard_map/gate/pallas_call | solution.py:511
  34.0 0.1 collective-permute-start.6
  34.1 1.1 %shares.1 = (bf16[192,1024]{1,0:T(8,128)(2,1)S(1)}, f32[192,1024]{1,0:T(8,128)S(1)}) custom-call(s32[1]{0:T(128)} %bitcast.lane_position, bf16[192,1024]{1,0:T(8,128)(2,1)S(1)} %get-tuple-element.48.gated_ref, bf16[1024,2048]{1,0:T(8,128)(2,1)S(1)} %get-tuple-element.52.rest_0_), custom_call_target="tpu_custom_call" | custom-call | flops 805306368 | bytes 4194304 | tf_op jit(solution)/shard_map/shares/pallas_call | solution.py:473
  35.1 0.5 collective-permute-start.3
  35.7 4.1 %late_shares.1 = (bf16[192,1024]{1,0:T(8,128)(2,1)S(1)}, f32[192,1024]{1,0:T(8,128)S(1)}, bf16[192,1024]{1,0:T(8,128)(2,1)S(1)}, f32[192,1024]{1,0:T(8,128)S(1)}) custom-call(s32[1]{0:T(128)} %bitcast.lane_position, bf16[192,1024]{1,0:T(8,128)(2,1)S(1)} %get-tuple-element.48.gated_ref, bf16[1024,2048]{1,0:T(8,128)(2,1)S(1)} %get-tuple-element.49.window_ref, ...), custom_call_target="tpu_custom_call" | custom-call | flops 1610612736 | bytes 8388608 | tf_op jit(solution)/shard_map/late_shares/pallas_call | solution.py:496
  39.8 0.1 collective-permute-start.8
  39.9 0.0 collective-permute-done.6.rest_1_
  39.9 0.1 merge.6
  40.0 2.1 %collective-permute-start.7 = (bf16[192,1024]{1,0:T(8,128)(2,1)S(1)}, bf16[192,1024]{1,0:T(8,128)(2,1)S(1)}, u32[]{:S(2)}, u32[]{:S(2)}) collective-permute-start(bf16[192,1024]{1,0:T(8,128)(2,1)S(1)} %merge.6), channel_id=1, source_target_pairs={{0,2},{1,3},{2,0},{3,1},{4,6},{5,7},{6,4},{7,5},{8,10},{9,11},{10,... | collective-permute-start | bytes 1179656 | tf_op jit(solution)/shard_map/ppermute | solution.py:570
  42.2 0.2 collective-permute-start.2
  42.4 0.0 collective-permute-done.3.rest_1_
  42.4 0.1 merge.5
  42.5 4.5 %collective-permute-start.5 = (bf16[192,1024]{1,0:T(8,128)(2,1)S(1)}, bf16[192,1024]{1,0:T(8,128)(2,1)S(1)}, u32[]{:S(2)}, u32[]{:S(2)}) collective-permute-start(bf16[192,1024]{1,0:T(8,128)(2,1)S(1)} %merge.5), channel_id=1, source_target_pairs={{0,4},{1,5},{6,2},{7,3},{8,12},{9,13},{14,10},{15,11},{16,20},{17,... | collective-permute-start | bytes 1179656 | tf_op jit(solution)/shard_map/ppermute | solution.py:574
  47.0 0.7 collective-permute-start.4
  47.7 0.0 collective-permute-done.8.rest_1_
  47.7 0.1 merge.8.rest_0_
  47.8 4.2 %collective-permute-done.7.rest_4_.rest_1_ = bf16[192,1024]{1,0:T(8,128)(2,1)S(1)} collective-permute-done((bf16[192,1024]{1,0:T(8,128)(2,1)S(1)}, bf16[192,1024]{1,0:T(8,128)(2,1)S(1)}, u32[]{:S(2)}, u32[]{:S(2)}) %collective-permute-start.7) | collective-permute-done | bytes 393248 | tf_op jit(solution)/shard_map/ppermute | solution.py:570
  51.9 0.1 merge.9
  52.0 2.3 %collective-permute-start.9 = (bf16[192,1024]{1,0:T(8,128)(2,1)S(1)}, bf16[192,1024]{1,0:T(8,128)(2,1)S(1)}, u32[]{:S(2)}, u32[]{:S(2)}) collective-permute-start(bf16[192,1024]{1,0:T(8,128)(2,1)S(1)} %merge.9), channel_id=1, source_target_pairs={{0,2},{1,3},{2,6},{3,7},{6,4},{7,5},{4,0},{5,1},{8,10},{9,11},{10,... | collective-permute-start | bytes 1179656 | tf_op jit(solution)/shard_map/ppermute | solution.py:578
  54.3 0.0 collective-permute-done.2.rest_1_
  54.3 5.8 %collective-permute-done.5.rest_3_ = bf16[192,1024]{1,0:T(8,128)(2,1)S(1)} collective-permute-done((bf16[192,1024]{1,0:T(8,128)(2,1)S(1)}, bf16[192,1024]{1,0:T(8,128)(2,1)S(1)}, u32[]{:S(2)}, u32[]{:S(2)}) %collective-permute-start.5) | collective-permute-done | bytes 393248 | tf_op jit(solution)/shard_map/ppermute | solution.py:574
  60.1 0.0 collective-permute-done.4.rest_2_
  60.1 0.3 merge.7
  60.4 14.3 %collective-permute-done.9 = bf16[192,1024]{1,0:T(8,128)(2,1)S(1)} collective-permute-done((bf16[192,1024]{1,0:T(8,128)(2,1)S(1)}, bf16[192,1024]{1,0:T(8,128)(2,1)S(1)}, u32[]{:S(2)}, u32[]{:S(2)}) %collective-permute-start.9) | collective-permute-done | bytes 393248 | tf_op jit(solution)/shard_map/ppermute | solution.py:578
  74.7 0.8 %add_convert_fusion = bf16[192,1024]{1,0:T(8,128)(2,1)} fusion(f32[192,1024]{1,0:T(8,128)S(1)} %merge.7, bf16[192,1024]{1,0:T(8,128)(2,1)S(1)} %collective-permute-done.9), kind=kLoop, calls=%fused_computation | loop fusion | flops 589824 | bytes 1572864 | tf_op jit(solution)/shard_map/convert_element_type | solution.py:533
Async XLA Ops:
  20.3 5.3 %collective-permute-start = (bf16[32,1024]{1,0:T(8,128)(2,1)S(1)}, bf16[32,1024]{1,0:T(8,128)(2,1)S(1)}, u32[]{:S(2)}, u32[]{:S(2)}) collective-permute-start(bf16[32,1024]{1,0:T(8,128)(2,1)S(1)} %get-tuple-element.33._.mine_ref.block_ref), channel_id=1, source_target_pairs={{0,8},{8,0},{16,24},{24,16},{1,9},{9,1},{17,25},{25,17},{2,10},{10... | collective-permute-start | bytes 196616 | tf_op jit(solution)/shard_map/ppermute | solution.py:680
  23.4 2.2 %copy-start = (s32[768]{0:T(1024)S(1)}, s32[768]{0:T(1024)}, u32[]{:S(2)}) copy-start(s32[768]{0:T(1024)} %ids_ref.3) | copy-start | bytes 9220
  26.3 4.4 %collective-permute-start.1 = (bf16[32,1024]{1,0:T(8,128)(2,1)S(1)}, bf16[32,1024]{1,0:T(8,128)(2,1)S(1)}, u32[]{:S(2)}, u32[]{:S(2)}) collective-permute-start(bf16[32,1024]{1,0:T(8,128)(2,1)S(1)} %join.1._), channel_id=1, source_target_pairs={{0,16},{8,24},{16,0},{24,8},{1,17},{9,25},{17,1},{25,9},{2,18},{10... | collective-permute-start | bytes 196616 | tf_op jit(solution)/shard_map/ppermute | solution.py:680
  34.0 5.9 %collective-permute-start.6 = (bf16[192,1024]{1,0:T(8,128)(2,1)S(1)}, bf16[192,1024]{1,0:T(8,128)(2,1)S(1)}, u32[]{:S(2)}, u32[]{:S(2)}) collective-permute-start(bf16[192,1024]{1,0:T(8,128)(2,1)S(1)} %get-tuple-element.56), channel_id=1, source_target_pairs={{0,1},{1,0},{2,3},{3,2},{4,5},{5,4},{6,7},{7,6},{8,9},{9,8},{10,11... | collective-permute-start | bytes 1179656 | tf_op jit(solution)/shard_map/ppermute | solution.py:568
  35.1 7.2 %collective-permute-start.3 = (bf16[192,1024]{1,0:T(8,128)(2,1)S(1)}, bf16[192,1024]{1,0:T(8,128)(2,1)S(1)}, u32[]{:S(2)}, u32[]{:S(2)}) collective-permute-start(bf16[192,1024]{1,0:T(8,128)(2,1)S(1)} %get-tuple-element.54), channel_id=1, source_target_pairs={{0,1},{1,0},{2,3},{3,2},{4,5},{5,4},{6,7},{7,6},{8,9},{9,8},{10,11... | collective-permute-start | bytes 1179656 | tf_op jit(solution)/shard_map/ppermute | solution.py:572
  39.8 7.9 %collective-permute-start.8 = (bf16[192,1024]{1,0:T(8,128)(2,1)S(1)}, bf16[192,1024]{1,0:T(8,128)(2,1)S(1)}, u32[]{:S(2)}, u32[]{:S(2)}) collective-permute-start(bf16[192,1024]{1,0:T(8,128)(2,1)S(1)} %get-tuple-element.58), channel_id=1, source_target_pairs={{0,1},{1,0},{2,3},{3,2},{4,5},{5,4},{6,7},{7,6},{8,9},{9,8},{10,11... | collective-permute-start | bytes 1179656 | tf_op jit(solution)/shard_map/ppermute | solution.py:576
  40.0 11.9 %collective-permute-start.7 = (bf16[192,1024]{1,0:T(8,128)(2,1)S(1)}, bf16[192,1024]{1,0:T(8,128)(2,1)S(1)}, u32[]{:S(2)}, u32[]{:S(2)}) collective-permute-start(bf16[192,1024]{1,0:T(8,128)(2,1)S(1)} %merge.6), channel_id=1, source_target_pairs={{0,2},{1,3},{2,0},{3,1},{4,6},{5,7},{6,4},{7,5},{8,10},{9,11},{10,... | collective-permute-start | bytes 1179656 | tf_op jit(solution)/shard_map/ppermute | solution.py:570
  42.2 12.1 %collective-permute-start.2 = (bf16[192,1024]{1,0:T(8,128)(2,1)S(1)}, bf16[192,1024]{1,0:T(8,128)(2,1)S(1)}, u32[]{:S(2)}, u32[]{:S(2)}) collective-permute-start(bf16[192,1024]{1,0:T(8,128)(2,1)S(1)} %get-tuple-element.51), channel_id=1, source_target_pairs={{0,1},{1,0},{2,3},{3,2},{4,5},{5,4},{6,7},{7,6},{8,9},{9,8},{10,11... | collective-permute-start | bytes 1179656 | tf_op jit(solution)/shard_map/ppermute | solution.py:579
  42.5 17.7 %collective-permute-start.5 = (bf16[192,1024]{1,0:T(8,128)(2,1)S(1)}, bf16[192,1024]{1,0:T(8,128)(2,1)S(1)}, u32[]{:S(2)}, u32[]{:S(2)}) collective-permute-start(bf16[192,1024]{1,0:T(8,128)(2,1)S(1)} %merge.5), channel_id=1, source_target_pairs={{0,4},{1,5},{6,2},{7,3},{8,12},{9,13},{14,10},{15,11},{16,20},{17,... | collective-permute-start | bytes 1179656 | tf_op jit(solution)/shard_map/ppermute | solution.py:574
  47.0 13.2 %collective-permute-start.4 = (bf16[192,1024]{1,0:T(8,128)(2,1)S(1)}, bf16[192,1024]{1,0:T(8,128)(2,1)S(1)}, u32[]{:S(2)}, u32[]{:S(2)}) collective-permute-start(bf16[192,1024]{1,0:T(8,128)(2,1)S(1)} %merge.5), channel_id=1, source_target_pairs={{2,4},{3,5},{4,2},{5,3},{10,12},{11,13},{12,10},{13,11},{18,20},{1... | collective-permute-start | bytes 1179656 | tf_op jit(solution)/shard_map/ppermute | solution.py:573
  52.0 22.7 %collective-permute-start.9 = (bf16[192,1024]{1,0:T(8,128)(2,1)S(1)}, bf16[192,1024]{1,0:T(8,128)(2,1)S(1)}, u32[]{:S(2)}, u32[]{:S(2)}) collective-permute-start(bf16[192,1024]{1,0:T(8,128)(2,1)S(1)} %merge.9), channel_id=1, source_target_pairs={{0,2},{1,3},{2,6},{3,7},{6,4},{7,5},{4,0},{5,1},{8,10},{9,11},{10,... | collective-permute-start | bytes 1179656 | tf_op jit(solution)/shard_map/ppermute | solution.py:578

commit v6 on v5

--- a/solution.py
+++ b/solution.py
@@ -482,28 +482,26 @@
     )(lane_position, gated, *windows)
 
 
-def late_share_kernel(slot, lane_position, gated_ref, window_ref, out_ref, *rest):
-    outs, (window, sem) = rest[:-2], rest[-2:]
+def late_share_kernel(slot, lane_position, gated_ref, out_ref, send_out, mine_out, window, sem):
     copy = columns(lane_position[0], slot, out_ref, window, sem)
     copy.start()
-    share(lane_position[0], gated_ref, window_ref, outs[0], outs[1])
     copy.wait()
-    share(lane_position[0], gated_ref, window, outs[2], outs[3])
-
-
-def late_shares(slot, lane_position, gated, window, out_weight, width):
+    share(lane_position[0], gated_ref, window, send_out, mine_out)
+
+
+def late_share(slot, lane_position, gated, out_weight, width):
     T, channels = gated.shape
     return pl.pallas_call(
         functools.partial(late_share_kernel, slot),
-        out_shape=[jax.ShapeDtypeStruct((T, width), d) for d in (bf16, f32, bf16, f32)],
-        in_specs=[smem(), vmem(), vmem(), hbm()],
-        out_specs=[vmem()] * 4,
+        out_shape=[jax.ShapeDtypeStruct((T, width), d) for d in (bf16, f32)],
+        in_specs=[smem(), vmem(), hbm()],
+        out_specs=[vmem()] * 2,
         scratch_shapes=[pltpu.VMEM((channels, 2 * width), bf16), pltpu.SemaphoreType.DMA((STREAMS,))],
         compiler_params=pltpu.CompilerParams(vmem_limit_bytes=6 * MIB),
         cost_estimate=pl.CostEstimate(
-            flops=8 * T * channels * width, bytes_accessed=8 * channels * width, transcendentals=0),
-        name="late_shares",
-    )(lane_position, gated, window, out_weight)
+            flops=4 * T * channels * width, bytes_accessed=4 * channels * width, transcendentals=0),
+        name="late_share",
+    )(lane_position, gated, out_weight)
 
 
 def gate(T, spans, arrived, position, lane_position, ids, query, parts, block, visible, taps, rates, skip, window, out_weight, width):
@@ -572,10 +570,11 @@
     second = merge(lane_position, bf16, (mine, lax.ppermute(send, "mp", pair)))
     from_middle = lax.ppermute(second, "mp", along([(1, 2), (2, 1)]))
     from_end = lax.ppermute(second, "mp", along([(0, 2), (3, 1)]))
-    send2, mine2, send3, mine3 = late_shares(3, lane_position, gated, third, out_weight, width)
+    send2, mine2 = shares(lane_position, gated, [third], width)
     mine2 = merge(lane_position, f32, (mine2, lax.ppermute(send2, "mp", pair)))
     onward = merge(lane_position, bf16, (mine2,), inner=from_near)
     from_round = lax.ppermute(onward, "mp", along([(0, 1), (1, 3), (3, 2), (2, 0)]))
+    send3, mine3 = late_share(3, lane_position, gated, out_weight, width)
     own = merge(lane_position, f32, (mine3, lax.ppermute(send3, "mp", pair), from_middle, from_end), outer=from_near)
     return total(own, from_round)
 

time: 75.7 us -> 75.9 us (level)
    ppermute x1, waiting for transfers between devices: 14.3 us -> 17.6 us  [scatter_line(): lax.ppermute(onward, 'mp', along([(0, 1), (1, 3), (3, 2), (2, 0)]))]
    ppermute x1, waiting for transfers between devices: 4.16 us -> 0.85 us  [scatter_line(): from_near = lax.ppermute(far, 'mp', near)]
    pallas_call x1 -> x2, Pallas kernels: 1.07 us -> 2.12 us  [shares(): pl.pallas_call(functools.partial(share_kernel, count), out_shape=[jax.Sha...]
    pallas_call x1, Pallas kernels: 4.12 us -> 3.25 us  [late_share(): pl.pallas_call(functools.partial(late_share_kernel, slot), out_shape=[jax...]
where the time goes in v6:
time: 75.9 us; the launch traced here: 75.8 us
  Pallas kernels  34.7 us (46%)
  waiting for transfers between devices  24.3 us (32%)
  starting transfers between devices  15.7 us (21%)
  other arithmetic  0.84 us (1%)
    pallas_call x1, Pallas kernels, front(): pl.pallas_call(functools.partial(front_kernel, geometry), out_shape=[jax....  20.3 us
    ppermute x1, waiting for transfers between devices, scatter_line(): lax.ppermute(onward, 'mp', along([(0, 1), (1, 3), (3, 2), (2, 0)]))  17.6 us
    ppermute x1, waiting for transfers between devices, scatter_line(): from_end = lax.ppermute(second, 'mp', along([(0, 2), (3, 1)]))  5.84 us
    ppermute x2, starting transfers between devices, local(): other = lax.ppermute(group, 'ctx', [(a, a ^ span) for a in range(shards)])  5.13 us
    ppermute x1, starting transfers between devices, scatter_line(): from_end = lax.ppermute(second, 'mp', along([(0, 2), (3, 1)]))  4.52 us
    pallas_call x2, Pallas kernels, local_pass(): pl.pallas_call(functools.partial(local_kernel, poles, first, slot), out_s...  4.45 us
    pallas_call x1, Pallas kernels, gate(): pl.pallas_call(functools.partial(gate_kernel, T, poles, tuple(spans), len...  3.3 us
    pallas_call x1, Pallas kernels, late_share(): pl.pallas_call(functools.partial(late_share_kernel, slot), out_shape=[jax...  3.25 us
  transfers between devices with their start and end apart: 10, of which 3 were waited for; matrix products, arithmetic and copies ran while one was open for 0% of the time, Pallas kernels for 14%

profile of v6, /device:TPU:0, one launch (start us, length us, event | category | flops | bytes accessed | tf_op | source)
XLA Modules:
  0.0 75.8 jit_solution(5885588900272528342)
XLA Ops:
  0.0 20.3 %front.1 = (f32[192,1024]{1,0:T(8,128)S(1)}, f32[8,192,128]{2,1,0:T(8,128)S(1)}, bf16[32,1024]{1,0:T(8,128)(2,1)S(1)}, f32[192,128]{1,0:T(8,128)S(1)}, f32[192,1...) custom-call(s32[1]{0:T(128)} %bitcast.1.position, ...), custom_call_target="tpu_custom_call" | custom-call | tf_op jit(solution)/shard_map/front/pallas_call | solution.py:177
  20.3 3.0 %collective-permute-start = (bf16[32,1024]{1,0:T(8,128)(2,1)S(1)}, bf16[32,1024]{1,0:T(8,128)(2,1)S(1)}, u32[]{:S(2)}, u32[]{:S(2)}) collective-permute-start(bf16[32,1024]{1,0:T(8,128)(2,1)S(1)} %get-tuple-element.33._.mine_ref.block_ref), channel_id=1, source_target_pairs={{0,8},{8,0},{16,24},{24,16},{1,9},{9,1},{17,25},{25,17},{2,10},{10... | collective-permute-start | bytes 196616 | tf_op jit(solution)/shard_map/ppermute | solution.py:679
  23.4 0.0 copy-start
  23.4 2.2 %local_pass.2 = (f32[4,192,128]{2,1,0:T(8,128)S(1)}, f32[4,128,128]{2,1,0:T(8,128)S(1)}, f32[16,512]{1,0:T(8,128)S(1)}, bf16[1024,2048]{1,0:T(8,128)(2,1)S(1)}) custom-call(s32[1]{0:T(128)} %bitcast.lane_position, f32[8,192,128]{2,1,0:T(8,128)S(1)} %get-tuple-element.38.prod_ref, f32[192,128]{1,0:T(8,128)S(1)} %get-tuple-element.39.keep_ref, ...), custom_call_target="tpu_custom_call" | custom-call | flops 9437184 | bytes 8388608 | tf_op jit(solution)/shard_map/local_pass/pallas_call | solution.py:260
  25.6 0.0 collective-permute-done.other_ref.rest_0_
  25.6 0.0 copy-done
  25.6 0.7 join.1._
  26.3 2.1 %collective-permute-start.1 = (bf16[32,1024]{1,0:T(8,128)(2,1)S(1)}, bf16[32,1024]{1,0:T(8,128)(2,1)S(1)}, u32[]{:S(2)}, u32[]{:S(2)}) collective-permute-start(bf16[32,1024]{1,0:T(8,128)(2,1)S(1)} %join.1._), channel_id=1, source_target_pairs={{0,16},{8,24},{16,0},{24,8},{1,17},{9,25},{17,1},{25,9},{2,18},{10... | collective-permute-start | bytes 196616 | tf_op jit(solution)/shard_map/ppermute | solution.py:679
  28.4 2.2 %local_pass.3 = (f32[4,192,128]{2,1,0:T(8,128)S(1)}, f32[4,128,128]{2,1,0:T(8,128)S(1)}, f32[16,512]{1,0:T(8,128)S(1)}, bf16[1024,2048]{1,0:T(8,128)(2,1)S(1)}) custom-call(s32[1]{0:T(128)} %bitcast.lane_position, f32[8,192,128]{2,1,0:T(8,128)S(1)} %get-tuple-element.38.prod_ref, f32[192,128]{1,0:T(8,128)S(1)} %get-tuple-element.39.keep_ref, ...), custom_call_target="tpu_custom_call" | custom-call | flops 9437184 | bytes 8388608 | tf_op jit(solution)/shard_map/local_pass/pallas_call | solution.py:260
  30.6 0.0 collective-permute-done.1.rest_1_
  30.7 3.3 %gate.1 = (bf16[192,1024]{1,0:T(8,128)(2,1)S(1)}, bf16[192,1024]{1,0:T(8,128)(2,1)S(1)}, f32[192,1024]{1,0:T(8,128)S(1)}, bf16[1024,2048]{1,0:T(8,128)(2,1)S(1)}) custom-call(s32[1]{0:T(128)} %bitcast.1.position, s32[1]{0:T(128)} %bitcast.lane_position, s32[768]{0:T(1024)S(1)} %copy-done, f32[192,1024]{1,0:T(8,128)S(1)} %get-tuple-element.32.query_ref, ...), custom_call_target="tpu_custom_call" | custom-call | tf_op jit(solution)/shard_map/gate/pallas_call | solution.py:509
  34.0 0.1 collective-permute-start.6
  34.1 1.1 %shares.2 = (bf16[192,1024]{1,0:T(8,128)(2,1)S(1)}, f32[192,1024]{1,0:T(8,128)S(1)}) custom-call(s32[1]{0:T(128)} %bitcast.lane_position, bf16[192,1024]{1,0:T(8,128)(2,1)S(1)} %get-tuple-element.48.gated_ref, bf16[1024,2048]{1,0:T(8,128)(2,1)S(1)} %get-tuple-element.51.rest_0_), custom_call_target="tpu_custom_call" | custom-call | flops 805306368 | bytes 4194304 | tf_op jit(solution)/shard_map/shares/pallas_call | solution.py:473
  35.1 0.5 collective-permute-start.3
  35.7 1.1 %shares.3 = (bf16[192,1024]{1,0:T(8,128)(2,1)S(1)}, f32[192,1024]{1,0:T(8,128)S(1)}) custom-call(s32[1]{0:T(128)} %bitcast.lane_position, bf16[192,1024]{1,0:T(8,128)(2,1)S(1)} %get-tuple-element.48.gated_ref, bf16[1024,2048]{1,0:T(8,128)(2,1)S(1)} %get-tuple-element.56.rest_0_), custom_call_target="tpu_custom_call" | custom-call | flops 805306368 | bytes 4194304 | tf_op jit(solution)/shard_map/shares/pallas_call | solution.py:473
  36.7 0.1 collective-permute-start.8
  36.8 0.0 collective-permute-done.6.rest_1_
  36.8 0.1 merge.6
  36.9 2.1 %collective-permute-start.7 = (bf16[192,1024]{1,0:T(8,128)(2,1)S(1)}, bf16[192,1024]{1,0:T(8,128)(2,1)S(1)}, u32[]{:S(2)}, u32[]{:S(2)}) collective-permute-start(bf16[192,1024]{1,0:T(8,128)(2,1)S(1)} %merge.6), channel_id=1, source_target_pairs={{0,2},{1,3},{2,0},{3,1},{4,6},{5,7},{6,4},{7,5},{8,10},{9,11},{10,... | collective-permute-start | bytes 1179656 | tf_op jit(solution)/shard_map/ppermute | solution.py:568
  39.1 3.3 %late_share.1 = (bf16[192,1024]{1,0:T(8,128)(2,1)S(1)}, f32[192,1024]{1,0:T(8,128)S(1)}) custom-call(s32[1]{0:T(128)} %bitcast.lane_position, bf16[192,1024]{1,0:T(8,128)(2,1)S(1)} %get-tuple-element.48.gated_ref, bf16[1024,8192]{1,0:T(8,128)(2,1)} %out_ref.7), custom_call_target="tpu_custom_call" | custom-call | flops 805306368 | bytes 4194304 | tf_op jit(solution)/shard_map/late_share/pallas_call | solution.py:494
  42.3 0.3 collective-permute-start.2
  42.6 0.0 collective-permute-done.3.rest_1_
  42.6 0.1 merge.5
  42.7 4.5 %collective-permute-start.5 = (bf16[192,1024]{1,0:T(8,128)(2,1)S(1)}, bf16[192,1024]{1,0:T(8,128)(2,1)S(1)}, u32[]{:S(2)}, u32[]{:S(2)}) collective-permute-start(bf16[192,1024]{1,0:T(8,128)(2,1)S(1)} %merge.5), channel_id=1, source_target_pairs={{0,4},{1,5},{6,2},{7,3},{8,12},{9,13},{14,10},{15,11},{16,20},{17,... | collective-permute-start | bytes 1179656 | tf_op jit(solution)/shard_map/ppermute | solution.py:572
  47.2 0.7 collective-permute-start.4
  47.9 0.0 collective-permute-done.8.rest_1_
  47.9 0.1 merge.8.rest_0_
  48.0 0.8 %collective-permute-done.7.rest_4_.rest_1_ = bf16[192,1024]{1,0:T(8,128)(2,1)S(1)} collective-permute-done((bf16[192,1024]{1,0:T(8,128)(2,1)S(1)}, bf16[192,1024]{1,0:T(8,128)(2,1)S(1)}, u32[]{:S(2)}, u32[]{:S(2)}) %collective-permute-start.7) | collective-permute-done | bytes 393248 | tf_op jit(solution)/shard_map/ppermute | solution.py:568
  48.9 0.1 merge.9
  49.0 2.3 %collective-permute-start.9 = (bf16[192,1024]{1,0:T(8,128)(2,1)S(1)}, bf16[192,1024]{1,0:T(8,128)(2,1)S(1)}, u32[]{:S(2)}, u32[]{:S(2)}) collective-permute-start(bf16[192,1024]{1,0:T(8,128)(2,1)S(1)} %merge.9), channel_id=1, source_target_pairs={{0,2},{1,3},{2,6},{3,7},{6,4},{7,5},{4,0},{5,1},{8,10},{9,11},{10,... | collective-permute-start | bytes 1179656 | tf_op jit(solution)/shard_map/ppermute | solution.py:576
  51.2 0.0 collective-permute-done.2.rest_1_
  51.2 5.8 %collective-permute-done.5.rest_3_ = bf16[192,1024]{1,0:T(8,128)(2,1)S(1)} collective-permute-done((bf16[192,1024]{1,0:T(8,128)(2,1)S(1)}, bf16[192,1024]{1,0:T(8,128)(2,1)S(1)}, u32[]{:S(2)}, u32[]{:S(2)}) %collective-permute-start.5) | collective-permute-done | bytes 393248 | tf_op jit(solution)/shard_map/ppermute | solution.py:572
  57.1 0.0 collective-permute-done.4.rest_2_
  57.1 0.2 merge.7
  57.3 17.6 %collective-permute-done.9 = bf16[192,1024]{1,0:T(8,128)(2,1)S(1)} collective-permute-done((bf16[192,1024]{1,0:T(8,128)(2,1)S(1)}, bf16[192,1024]{1,0:T(8,128)(2,1)S(1)}, u32[]{:S(2)}, u32[]{:S(2)}) %collective-permute-start.9) | collective-permute-done | bytes 393248 | tf_op jit(solution)/shard_map/ppermute | solution.py:576
  74.9 0.8 %add_convert_fusion = bf16[192,1024]{1,0:T(8,128)(2,1)} fusion(f32[192,1024]{1,0:T(8,128)S(1)} %merge.7, bf16[192,1024]{1,0:T(8,128)(2,1)S(1)} %collective-permute-done.9), kind=kLoop, calls=%fused_computation | loop fusion | flops 589824 | bytes 1572864 | tf_op jit(solution)/shard_map/convert_element_type | solution.py:531
Async XLA Ops:
  20.3 5.3 %collective-permute-start = (bf16[32,1024]{1,0:T(8,128)(2,1)S(1)}, bf16[32,1024]{1,0:T(8,128)(2,1)S(1)}, u32[]{:S(2)}, u32[]{:S(2)}) collective-permute-start(bf16[32,1024]{1,0:T(8,128)(2,1)S(1)} %get-tuple-element.33._.mine_ref.block_ref), channel_id=1, source_target_pairs={{0,8},{8,0},{16,24},{24,16},{1,9},{9,1},{17,25},{25,17},{2,10},{10... | collective-permute-start | bytes 196616 | tf_op jit(solution)/shard_map/ppermute | solution.py:679
  23.4 2.2 %copy-start = (s32[768]{0:T(1024)S(1)}, s32[768]{0:T(1024)}, u32[]{:S(2)}) copy-start(s32[768]{0:T(1024)} %ids_ref.3) | copy-start | bytes 9220
  26.3 4.4 %collective-permute-start.1 = (bf16[32,1024]{1,0:T(8,128)(2,1)S(1)}, bf16[32,1024]{1,0:T(8,128)(2,1)S(1)}, u32[]{:S(2)}, u32[]{:S(2)}) collective-permute-start(bf16[32,1024]{1,0:T(8,128)(2,1)S(1)} %join.1._), channel_id=1, source_target_pairs={{0,16},{8,24},{16,0},{24,8},{1,17},{9,25},{17,1},{25,9},{2,18},{10... | collective-permute-start | bytes 196616 | tf_op jit(solution)/shard_map/ppermute | solution.py:679
  34.0 2.9 %collective-permute-start.6 = (bf16[192,1024]{1,0:T(8,128)(2,1)S(1)}, bf16[192,1024]{1,0:T(8,128)(2,1)S(1)}, u32[]{:S(2)}, u32[]{:S(2)}) collective-permute-start(bf16[192,1024]{1,0:T(8,128)(2,1)S(1)} %get-tuple-element.55), channel_id=1, source_target_pairs={{0,1},{1,0},{2,3},{3,2},{4,5},{5,4},{6,7},{7,6},{8,9},{9,8},{10,11... | collective-permute-start | bytes 1179656 | tf_op jit(solution)/shard_map/ppermute | solution.py:566
  35.1 7.5 %collective-permute-start.3 = (bf16[192,1024]{1,0:T(8,128)(2,1)S(1)}, bf16[192,1024]{1,0:T(8,128)(2,1)S(1)}, u32[]{:S(2)}, u32[]{:S(2)}) collective-permute-start(bf16[192,1024]{1,0:T(8,128)(2,1)S(1)} %get-tuple-element.53), channel_id=1, source_target_pairs={{0,1},{1,0},{2,3},{3,2},{4,5},{5,4},{6,7},{7,6},{8,9},{9,8},{10,11... | collective-permute-start | bytes 1179656 | tf_op jit(solution)/shard_map/ppermute | solution.py:570
  36.7 11.2 %collective-permute-start.8 = (bf16[192,1024]{1,0:T(8,128)(2,1)S(1)}, bf16[192,1024]{1,0:T(8,128)(2,1)S(1)}, u32[]{:S(2)}, u32[]{:S(2)}) collective-permute-start(bf16[192,1024]{1,0:T(8,128)(2,1)S(1)} %get-tuple-element.58), channel_id=1, source_target_pairs={{0,1},{1,0},{2,3},{3,2},{4,5},{5,4},{6,7},{7,6},{8,9},{9,8},{10,11... | collective-permute-start | bytes 1179656 | tf_op jit(solution)/shard_map/ppermute | solution.py:574
  36.9 11.9 %collective-permute-start.7 = (bf16[192,1024]{1,0:T(8,128)(2,1)S(1)}, bf16[192,1024]{1,0:T(8,128)(2,1)S(1)}, u32[]{:S(2)}, u32[]{:S(2)}) collective-permute-start(bf16[192,1024]{1,0:T(8,128)(2,1)S(1)} %merge.6), channel_id=1, source_target_pairs={{0,2},{1,3},{2,0},{3,1},{4,6},{5,7},{6,4},{7,5},{8,10},{9,11},{10,... | collective-permute-start | bytes 1179656 | tf_op jit(solution)/shard_map/ppermute | solution.py:568
  42.3 8.9 %collective-permute-start.2 = (bf16[192,1024]{1,0:T(8,128)(2,1)S(1)}, bf16[192,1024]{1,0:T(8,128)(2,1)S(1)}, u32[]{:S(2)}, u32[]{:S(2)}) collective-permute-start(bf16[192,1024]{1,0:T(8,128)(2,1)S(1)} %get-tuple-element.50), channel_id=1, source_target_pairs={{0,1},{1,0},{2,3},{3,2},{4,5},{5,4},{6,7},{7,6},{8,9},{9,8},{10,11... | collective-permute-start | bytes 1179656 | tf_op jit(solution)/shard_map/ppermute | solution.py:578
  42.7 14.4 %collective-permute-start.5 = (bf16[192,1024]{1,0:T(8,128)(2,1)S(1)}, bf16[192,1024]{1,0:T(8,128)(2,1)S(1)}, u32[]{:S(2)}, u32[]{:S(2)}) collective-permute-start(bf16[192,1024]{1,0:T(8,128)(2,1)S(1)} %merge.5), channel_id=1, source_target_pairs={{0,4},{1,5},{6,2},{7,3},{8,12},{9,13},{14,10},{15,11},{16,20},{17,... | collective-permute-start | bytes 1179656 | tf_op jit(solution)/shard_map/ppermute | solution.py:572
  47.2 9.8 %collective-permute-start.4 = (bf16[192,1024]{1,0:T(8,128)(2,1)S(1)}, bf16[192,1024]{1,0:T(8,128)(2,1)S(1)}, u32[]{:S(2)}, u32[]{:S(2)}) collective-permute-start(bf16[192,1024]{1,0:T(8,128)(2,1)S(1)} %merge.5), channel_id=1, source_target_pairs={{2,4},{3,5},{4,2},{5,3},{10,12},{11,13},{12,10},{13,11},{18,20},{1... | collective-permute-start | bytes 1179656 | tf_op jit(solution)/shard_map/ppermute | solution.py:571
  49.0 26.0 %collective-permute-start.9 = (bf16[192,1024]{1,0:T(8,128)(2,1)S(1)}, bf16[192,1024]{1,0:T(8,128)(2,1)S(1)}, u32[]{:S(2)}, u32[]{:S(2)}) collective-permute-start(bf16[192,1024]{1,0:T(8,128)(2,1)S(1)} %merge.9), channel_id=1, source_target_pairs={{0,2},{1,3},{2,6},{3,7},{6,4},{7,5},{4,0},{5,1},{8,10},{9,11},{10,... | collective-permute-start | bytes 1179656 | tf_op jit(solution)/shard_map/ppermute | solution.py:576

commit v7 on v6

--- a/solution.py
+++ b/solution.py
@@ -36,8 +36,8 @@
 
 def front_kernel(
     geometry, position, ids_ref, tokens_ref, gain_ref, weight_ref, taps_ref, rates_ref, residues_ref, skip_ref,
-    query_out, prod_out, block_out, keep_out, visible_out, taps, rates, residues, skip,
-    ids, gain, tok, normed, ring, total, proj, head, idcol, near, twice, ending, sem, tok_sem, ring_sem,
+    raw_out, prod_out, block_out, keep_out, twice, visible_out, taps, rates, residues, skip,
+    ids, gain, tok, normed, ring, total, proj, head, idcol, near, ending, sem, tok_sem, ring_sem,
 ):
     T, depth, channels, cb_size, kc_size, slots, poles = geometry
     run = T // PARTS
@@ -85,8 +85,9 @@
     before = near[pl.ds(7, PARTS, stride=run), :]
     for i in range(run):
         visible_out[i * 8 : (i + 1) * 8, :] = (near[pl.ds(8 + i, PARTS, stride=run), :] == before).astype(f32)
-    for i in range(3):
+    for i in range(2):
         proj[i, 0:8, :] = jnp.zeros((8, cb_size), f32)
+    raw_out[0:8, :] = jnp.zeros((8, channels), f32)
     head[...] = jnp.zeros(head.shape, f32)
     small[1].wait()
 
@@ -108,19 +109,19 @@
         feats = []
         m1 = jnp.concatenate([keep_out[...]] * (cb_size // 128), axis=1)
         m2 = jnp.concatenate([twice[...]] * (cb_size // 128), axis=1)
-        for i in range(3):
-            p = total[i].astype(bf16).astype(f32)
+        query = total[0].astype(bf16).astype(f32)
+        raw_out[8 : 8 + T, cols] = query
+        head[4:6, :] = query[T - 2 : T]
+        for i in range(2):
+            p = total[i + 1].astype(bf16).astype(f32)
             proj[i, 8 : 8 + T, :] = p
-            tap = [taps[j, i : i + 1, cols] for j in range(3)]
+            tap = [taps[j, i + 1 : i + 2, cols] for j in range(3)]
             feats.append(
                 tap[0] * p + m1 * (tap[1] * proj[i, 7 : 7 + T, :]) + m2 * (tap[2] * proj[i, 6 : 6 + T, :]))
-        query_out[:, cols] = feats[0]
-        for i in range(1, 3):
-            head[2 * (i - 1) : 2 * i, :] = proj[i, 8:10, :]
-        for i in range(3):
-            head[4 + 2 * i : 6 + 2 * i, :] = proj[i, 6 + T : 8 + T, :]
+            head[2 * i : 2 * i + 2, :] = proj[i, 8:10, :]
+            head[6 + 2 * i : 8 + 2 * i, :] = proj[i, 6 + T : 8 + T, :]
         block_out[poles : poles + HEAD, cols] = head[...].astype(bf16)
-        product = feats[1] * feats[2]
+        product = feats[0] * feats[1]
         back = 7.0 - lax.broadcasted_iota(jnp.int32, (8, 128), 0).astype(f32)
         for lane in range(cb_size // 128):
             tile = cb * (cb_size // 128) + lane
@@ -177,14 +178,15 @@
     return pl.pallas_call(
         functools.partial(front_kernel, geometry),
         out_shape=[
-            jax.ShapeDtypeStruct((T, channels), f32),
+            jax.ShapeDtypeStruct((T + 8, channels), f32),
             jax.ShapeDtypeStruct((channels // 128, T, 128), f32),
             jax.ShapeDtypeStruct((poles + HEAD, channels), bf16),
             jax.ShapeDtypeStruct((T, 128), f32),
             jax.ShapeDtypeStruct((T, 128), f32),
+            jax.ShapeDtypeStruct((T, 128), f32),
         ] + kept,
         in_specs=[smem()] + [hbm()] * 8,
-        out_specs=[vmem()] * 9,
+        out_specs=[vmem()] * 10,
         scratch_shapes=[
             pltpu.VMEM(ids2.shape, ids2.dtype),
             pltpu.VMEM(gain.shape, f32),
@@ -192,11 +194,10 @@
             pltpu.VMEM((T, depth), bf16),
             pltpu.VMEM((slots, 3, kc_size, cb_size), bf16),
             pltpu.VMEM((3, T, cb_size), f32),
-            pltpu.VMEM((3, T + 8, cb_size), f32),
+            pltpu.VMEM((2, T + 8, cb_size), f32),
             pltpu.VMEM((HEAD, cb_size), f32),
             pltpu.VMEM((ids2.shape[0] * 128 + 8, 128), f32),
             pltpu.VMEM((T + 8, 128), f32),
-            pltpu.VMEM((T, 128), f32),
             pltpu.VMEM((T, 128), f32),
             pltpu.SemaphoreType.DMA((6,)),
             pltpu.SemaphoreType.DMA((4,)),
@@ -215,8 +216,8 @@
 
 
 def local_kernel(
-    poles, first, slot, lane_position, prod_ref, keep_ref, rates_ref, residues_ref, skip_ref, out_ref, _,
-    local_out, state_out, pole_out, window_out, sem,
+    poles, first, slot, lane_position, prod_ref, keep_ref, twice_ref, raw_ref, taps_ref, rates_ref, residues_ref, skip_ref,
+    out_ref, _, local_out, state_out, pole_out, query_out, window_out, sem,
 ):
     copy = columns(lane_position[0], slot, out_ref, window_out, sem)
     copy.start()
@@ -243,6 +244,11 @@
         states = lax.fori_loop(0, run, token, tuple(jnp.zeros((8, 128), f32) for _ in range(poles)), unroll=2)
         for n in range(poles):
             state_out[tile, pl.ds(n, PARTS, stride=poles), :] = states[n]
+        tap = [taps_ref[j, 0:1, lanes] for j in range(3)]
+        query_out[tile] = (
+            tap[0] * raw_ref[8 : 8 + T, lanes]
+            + keep_ref[...] * (tap[1] * raw_ref[7 : 7 + T, lanes])
+            + twice_ref[...] * (tap[2] * raw_ref[6 : 6 + T, lanes]))
         return 0
 
     lax.fori_loop(0, tiles, tile_body, 0)
@@ -255,7 +261,9 @@
     return terms[0]
 
 
-def local_pass(first, tiles, slot, lane_position, product, keep, rates, residues, skip, out_weight, width, after):
+def local_pass(
+    first, tiles, slot, lane_position, product, keep, twice, raw, taps, rates, residues, skip, out_weight, width, after,
+):
     T, poles = product.shape[1], rates.shape[0]
     return pl.pallas_call(
         functools.partial(local_kernel, poles, first, slot),
@@ -263,15 +271,16 @@
             jax.ShapeDtypeStruct((tiles, T, 128), f32),
             jax.ShapeDtypeStruct((tiles, PARTS * poles, 128), f32),
             jax.ShapeDtypeStruct((poles, tiles * 128), f32),
+            jax.ShapeDtypeStruct((tiles, T, 128), f32),
             jax.ShapeDtypeStruct((out_weight.shape[0], 2 * width), bf16),
         ),
-        in_specs=[smem()] + [vmem()] * 5 + [hbm(), pl.BlockSpec(memory_space=pl.ANY)],
-        out_specs=[vmem()] * 4,
+        in_specs=[smem()] + [vmem()] * 8 + [hbm(), pl.BlockSpec(memory_space=pl.ANY)],
+        out_specs=[vmem()] * 5,
         scratch_shapes=[pltpu.SemaphoreType.DMA((STREAMS,))],
         compiler_params=pltpu.CompilerParams(vmem_limit_bytes=8 * MIB),
         cost_estimate=pl.CostEstimate(flops=6 * T * poles * tiles * 128, bytes_accessed=8 * MIB, transcendentals=0),
         name="local_pass",
-    )(lane_position, product, keep, rates, residues, skip, out_weight, after)
+    )(lane_position, product, keep, twice, raw, taps, rates, residues, skip, out_weight, after)
 
 
 def first_products(first, last, taps, ids_ref, base):
@@ -333,21 +342,21 @@
 
 
 def gate_kernel(
-    T, poles, spans, cuts, position, lane_position, ids_ref, query_ref, block_ref, visible_ref, taps_ref, rates_ref, skip_ref,
+    T, poles, spans, cuts, position, lane_position, ids_ref, block_ref, visible_ref, taps_ref, rates_ref, skip_ref,
     window_ref, out_ref, *rest,
 ):
     arrived, rest = rest[: len(spans)], rest[len(spans) :]
-    parts, rest = [rest[3 * c : 3 * c + 3] for c in range(cuts)], rest[3 * cuts :]
+    parts, rest = [rest[4 * c : 4 * c + 4] for c in range(cuts)], rest[4 * cuts :]
     gated_out, send_out, mine_out, third_out, carry, full, sem = rest
     run = T // PARTS
-    tiles = query_ref.shape[1] // 128
+    tiles = block_ref.shape[1] // 128
     copy = columns(lane_position[0], 2, out_ref, third_out, sem)
     copy.start()
     me = position[0]
     base = me * T
     taps = [taps_ref[j] for j in range(3)]
     rates, skip = rates_ref[...], skip_ref[...]
-    weight = jnp.concatenate([pole_ref[...] for _, _, pole_ref in parts], axis=1)
+    weight = jnp.concatenate([pole_ref[...] for _, _, pole_ref, _ in parts], axis=1)
     each = tiles // cuts
     prior = jnp.zeros(block_ref.shape, f32)
     prior_state, prior_first, prior_last = unpack(prior, poles)
@@ -402,8 +411,9 @@
     row = lax.broadcasted_iota(jnp.int32, (16, 128), 0)
     for tile in range(tiles):
         lanes = slice(tile * 128, tile * 128 + 128)
-        gated_out[:, lanes] = (query_ref[:, lanes] * full[tile]).astype(bf16)
-        top_q, top = query_ref[0:16, lanes], full[tile, 0:16, :]
+        query_ref = parts[tile // each][3].at[tile % each]
+        gated_out[:, lanes] = (query_ref[...] * full[tile]).astype(bf16)
+        top_q, top = query_ref[0:16, :], full[tile, 0:16, :]
         top_q = top_q + jnp.where(row == 0, q_shift[0][:, lanes], 0.0) + jnp.where(row == 1, q_shift[1][:, lanes], 0.0)
         top = top + jnp.where(row == 0, fix0[:, lanes], 0.0) + jnp.where(row == 1, fix1[:, lanes], 0.0)
         gated_out[0:16, lanes] = (top_q * top).astype(bf16)
@@ -504,17 +514,17 @@
     )(lane_position, gated, out_weight)
 
 
-def gate(T, spans, arrived, position, lane_position, ids, query, parts, block, visible, taps, rates, skip, window, out_weight, width):
+def gate(T, spans, arrived, position, lane_position, ids, parts, block, visible, taps, rates, skip, window, out_weight, width):
     poles, channels = rates.shape
     return pl.pallas_call(
         functools.partial(gate_kernel, T, poles, tuple(spans), len(parts)),
         out_shape=[
-            jax.ShapeDtypeStruct(query.shape, bf16),
+            jax.ShapeDtypeStruct((T, channels), bf16),
             jax.ShapeDtypeStruct((T, width), bf16),
             jax.ShapeDtypeStruct((T, width), f32),
             pltpu.VMEM(window.shape, bf16),
         ],
-        in_specs=[smem()] * 3 + [vmem()] * 7 + [hbm()] + [vmem()] * (len(spans) + 3 * len(parts)),
+        in_specs=[smem()] * 3 + [vmem()] * 6 + [hbm()] + [vmem()] * (len(spans) + 4 * len(parts)),
         out_specs=[vmem()] * 4,
         scratch_shapes=[
             pltpu.VMEM((channels // 128, PARTS * poles, 128), f32),
@@ -523,7 +533,7 @@
         ],
         compiler_params=pltpu.CompilerParams(vmem_limit_bytes=8 * MIB),
         name="gate",
-    )(position, lane_position, ids, query, block, visible, taps, rates, skip, window, out_weight, *arrived,
+    )(position, lane_position, ids, block, visible, taps, rates, skip, window, out_weight, *arrived,
       *[a for part in parts for a in part])
 
 
@@ -669,7 +679,7 @@
     width = out_weight.shape[1] // lax.axis_size("mp")
     weight3 = jnp.transpose(in_weight, (1, 0, 2))
     out_weight = pltpu.with_memory_space_constraint(out_weight, pltpu.HBM)
-    query, product, block, keep, visible, taps, rates, residues, skip = front(
+    raw, product, block, keep, twice, visible, taps, rates, residues, skip = front(
         position, segment_ids.reshape(-1, 128), tokens, norm_gain[None], weight3, short_filter, rates, residues, skip[None])
     cuts = shards.bit_length() - 1
     each = product.shape[0] // cuts
@@ -680,12 +690,13 @@
         spans.append(span)
         arrived.append(other)
         *part, window = local_pass(
-            k * each, each, min(k, 1), lane_position, product, keep, rates, residues, skip, out_weight, width, group)
+            k * each, each, min(k, 1), lane_position, product, keep, twice, raw, taps, rates, residues, skip,
+            out_weight, width, group)
         parts.append(part)
         windows.append(window)
         if k < cuts - 1:
             group = join(span, T, position, segment_ids, group, other, taps, rates, part[0])
-    gated, send, mine, third = gate(T, spans, arrived, position, lane_position, segment_ids, query, parts, block, visible, taps, rates,
+    gated, send, mine, third = gate(T, spans, arrived, position, lane_position, segment_ids, parts, block, visible, taps, rates,
                              skip, windows[0], out_weight, width)
     return scatter_line(lane_position, gated, send, mine, windows[1], third, out_weight, width)
 

time: 75.9 us -> 75.4 us (level)
  no operation moved by 1% of the time
where the time goes in v7:
time: 75.4 us; the launch traced here: 75.2 us
  Pallas kernels  34.2 us (45%)
  waiting for transfers between devices  24.4 us (32%)
  starting transfers between devices  15.7 us (21%)
  other arithmetic  0.84 us (1%)
    pallas_call x1, Pallas kernels, front(): pl.pallas_call(functools.partial(front_kernel, geometry), out_shape=[jax....  19.8 us
    ppermute x1, waiting for transfers between devices, scatter_line(): lax.ppermute(onward, 'mp', along([(0, 1), (1, 3), (3, 2), (2, 0)]))  17.7 us
    ppermute x1, waiting for transfers between devices, scatter_line(): from_end = lax.ppermute(second, 'mp', along([(0, 2), (3, 1)]))  5.83 us
    ppermute x2, starting transfers between devices, local(): other = lax.ppermute(group, 'ctx', [(a, a ^ span) for a in range(shards)])  5.13 us
    ppermute x1, starting transfers between devices, scatter_line(): from_end = lax.ppermute(second, 'mp', along([(0, 2), (3, 1)]))  4.52 us
    pallas_call x2, Pallas kernels, local_pass(): pl.pallas_call(functools.partial(local_kernel, poles, first, slot), out_s...  4.45 us
    pallas_call x1, Pallas kernels, gate(): pl.pallas_call(functools.partial(gate_kernel, T, poles, tuple(spans), len...  3.28 us
    pallas_call x1, Pallas kernels, late_share(): pl.pallas_call(functools.partial(late_share_kernel, slot), out_shape=[jax...  3.26 us
  transfers between devices with their start and end apart: 10, of which 3 were waited for; matrix products, arithmetic and copies ran while one was open for 0% of the time, Pallas kernels for 14%

profile of v7, /device:TPU:0, one launch (start us, length us, event | category | flops | bytes accessed | tf_op | source)
XLA Modules:
  0.0 75.2 jit_solution(3202485835464362664)
XLA Ops:
  0.0 19.8 %front.1 = (f32[200,1024]{1,0:T(8,128)S(1)}, f32[8,192,128]{2,1,0:T(8,128)S(1)}, bf16[32,1024]{1,0:T(8,128)(2,1)S(1)}, f32[192,128]{1,0:T(8,128)S(1)}, f32[192,1...) custom-call(s32[1]{0:T(128)} %bitcast.1.position, ...), custom_call_target="tpu_custom_call" | custom-call | tf_op jit(solution)/shard_map/front/pallas_call | solution.py:178
  19.8 3.0 %collective-permute-start = (bf16[32,1024]{1,0:T(8,128)(2,1)S(1)}, bf16[32,1024]{1,0:T(8,128)(2,1)S(1)}, u32[]{:S(2)}, u32[]{:S(2)}) collective-permute-start(bf16[32,1024]{1,0:T(8,128)(2,1)S(1)} %get-tuple-element.35._.mine_ref.block_ref), channel_id=1, source_target_pairs={{0,8},{8,0},{16,24},{24,16},{1,9},{9,1},{17,25},{25,17},{2,10},{10... | collective-permute-start | bytes 196616 | tf_op jit(solution)/shard_map/ppermute | solution.py:689
  22.8 0.0 copy-start
  22.8 2.2 %local_pass.2 = (f32[4,192,128]{2,1,0:T(8,128)S(1)}, f32[4,128,128]{2,1,0:T(8,128)S(1)}, f32[16,512]{1,0:T(8,128)S(1)}, f32[4,192,128]{2,1,0:T(8,128)S(1)}, bf16[1024,2048]{1,0:T(8,128)(2,1)S(1)}) custom-call(s32[1]{0:T(128)} %bitcast.lane_position, f32[8,192,128]{2,1,0:T(8,128)S(1)} %get-tuple-element.40.prod_ref, ...), custom_call_target="tpu_custom_call" | custom-call | flops 9437184 | bytes 8388608 | tf_op jit(solution)/shard_map/local_pass/pallas_call | solution.py:268
  25.1 0.0 collective-permute-done.other_ref.rest_0_
  25.1 0.0 copy-done
  25.1 0.7 join.1._
  25.8 2.1 %collective-permute-start.1 = (bf16[32,1024]{1,0:T(8,128)(2,1)S(1)}, bf16[32,1024]{1,0:T(8,128)(2,1)S(1)}, u32[]{:S(2)}, u32[]{:S(2)}) collective-permute-start(bf16[32,1024]{1,0:T(8,128)(2,1)S(1)} %join.1._), channel_id=1, source_target_pairs={{0,16},{8,24},{16,0},{24,8},{1,17},{9,25},{17,1},{25,9},{2,18},{10... | collective-permute-start | bytes 196616 | tf_op jit(solution)/shard_map/ppermute | solution.py:689
  27.9 2.2 %local_pass.3 = (f32[4,192,128]{2,1,0:T(8,128)S(1)}, f32[4,128,128]{2,1,0:T(8,128)S(1)}, f32[16,512]{1,0:T(8,128)S(1)}, f32[4,192,128]{2,1,0:T(8,128)S(1)}, bf16[1024,2048]{1,0:T(8,128)(2,1)S(1)}) custom-call(s32[1]{0:T(128)} %bitcast.lane_position, f32[8,192,128]{2,1,0:T(8,128)S(1)} %get-tuple-element.40.prod_ref, ...), custom_call_target="tpu_custom_call" | custom-call | flops 9437184 | bytes 8388608 | tf_op jit(solution)/shard_map/local_pass/pallas_call | solution.py:268
  30.1 0.0 collective-permute-done.1.rest_1_
  30.1 3.3 %gate.1 = (bf16[192,1024]{1,0:T(8,128)(2,1)S(1)}, bf16[192,1024]{1,0:T(8,128)(2,1)S(1)}, f32[192,1024]{1,0:T(8,128)S(1)}, bf16[1024,2048]{1,0:T(8,128)(2,1)S(1)}) custom-call(s32[1]{0:T(128)} %bitcast.1.position, s32[1]{0:T(128)} %bitcast.lane_position, s32[768]{0:T(1024)S(1)} %copy-done, bf16[32,1024]{1,0:T(8,128)(2,1)S(1)} %get-tuple-element.35._.mine_ref.block_ref, ...), custom_call_target="tpu_custom_call" | custom-call | tf_op jit(solution)/shard_map/gate/pallas_call | solution.py:519
  33.4 0.1 collective-permute-start.6
  33.5 1.1 %shares.2 = (bf16[192,1024]{1,0:T(8,128)(2,1)S(1)}, f32[192,1024]{1,0:T(8,128)S(1)}) custom-call(s32[1]{0:T(128)} %bitcast.lane_position, bf16[192,1024]{1,0:T(8,128)(2,1)S(1)} %get-tuple-element.54.gated_ref, bf16[1024,2048]{1,0:T(8,128)(2,1)S(1)} %get-tuple-element.57.rest_0_), custom_call_target="tpu_custom_call" | custom-call | flops 805306368 | bytes 4194304 | tf_op jit(solution)/shard_map/shares/pallas_call | solution.py:483
  34.5 0.6 collective-permute-start.3
  35.1 1.0 %shares.3 = (bf16[192,1024]{1,0:T(8,128)(2,1)S(1)}, f32[192,1024]{1,0:T(8,128)S(1)}) custom-call(s32[1]{0:T(128)} %bitcast.lane_position, bf16[192,1024]{1,0:T(8,128)(2,1)S(1)} %get-tuple-element.54.gated_ref, bf16[1024,2048]{1,0:T(8,128)(2,1)S(1)} %get-tuple-element.62.rest_0_), custom_call_target="tpu_custom_call" | custom-call | flops 805306368 | bytes 4194304 | tf_op jit(solution)/shard_map/shares/pallas_call | solution.py:483
  36.2 0.1 collective-permute-start.8
  36.3 0.0 collective-permute-done.6.rest_1_
  36.3 0.1 merge.6
  36.3 2.1 %collective-permute-start.7 = (bf16[192,1024]{1,0:T(8,128)(2,1)S(1)}, bf16[192,1024]{1,0:T(8,128)(2,1)S(1)}, u32[]{:S(2)}, u32[]{:S(2)}) collective-permute-start(bf16[192,1024]{1,0:T(8,128)(2,1)S(1)} %merge.6), channel_id=1, source_target_pairs={{0,2},{1,3},{2,0},{3,1},{4,6},{5,7},{6,4},{7,5},{8,10},{9,11},{10,... | collective-permute-start | bytes 1179656 | tf_op jit(solution)/shard_map/ppermute | solution.py:578
  38.5 3.3 %late_share.1 = (bf16[192,1024]{1,0:T(8,128)(2,1)S(1)}, f32[192,1024]{1,0:T(8,128)S(1)}) custom-call(s32[1]{0:T(128)} %bitcast.lane_position, bf16[192,1024]{1,0:T(8,128)(2,1)S(1)} %get-tuple-element.54.gated_ref, bf16[1024,8192]{1,0:T(8,128)(2,1)} %out_ref.7), custom_call_target="tpu_custom_call" | custom-call | flops 805306368 | bytes 4194304 | tf_op jit(solution)/shard_map/late_share/pallas_call | solution.py:504
  41.7 0.3 collective-permute-start.2
  42.0 0.0 collective-permute-done.3.rest_1_
  42.0 0.1 merge.5
  42.1 4.5 %collective-permute-start.5 = (bf16[192,1024]{1,0:T(8,128)(2,1)S(1)}, bf16[192,1024]{1,0:T(8,128)(2,1)S(1)}, u32[]{:S(2)}, u32[]{:S(2)}) collective-permute-start(bf16[192,1024]{1,0:T(8,128)(2,1)S(1)} %merge.5), channel_id=1, source_target_pairs={{0,4},{1,5},{6,2},{7,3},{8,12},{9,13},{14,10},{15,11},{16,20},{17,... | collective-permute-start | bytes 1179656 | tf_op jit(solution)/shard_map/ppermute | solution.py:582
  46.6 0.7 collective-permute-start.4
  47.3 0.0 collective-permute-done.8.rest_1_
  47.3 0.1 merge.8.rest_0_
  47.4 0.8 %collective-permute-done.7.rest_4_.rest_1_ = bf16[192,1024]{1,0:T(8,128)(2,1)S(1)} collective-permute-done((bf16[192,1024]{1,0:T(8,128)(2,1)S(1)}, bf16[192,1024]{1,0:T(8,128)(2,1)S(1)}, u32[]{:S(2)}, u32[]{:S(2)}) %collective-permute-start.7) | collective-permute-done | bytes 393248 | tf_op jit(solution)/shard_map/ppermute | solution.py:578
  48.2 0.1 merge.9
  48.3 2.2 %collective-permute-start.9 = (bf16[192,1024]{1,0:T(8,128)(2,1)S(1)}, bf16[192,1024]{1,0:T(8,128)(2,1)S(1)}, u32[]{:S(2)}, u32[]{:S(2)}) collective-permute-start(bf16[192,1024]{1,0:T(8,128)(2,1)S(1)} %merge.9), channel_id=1, source_target_pairs={{0,2},{1,3},{2,6},{3,7},{6,4},{7,5},{4,0},{5,1},{8,10},{9,11},{10,... | collective-permute-start | bytes 1179656 | tf_op jit(solution)/shard_map/ppermute | solution.py:586
  50.6 0.0 collective-permute-done.2.rest_1_
  50.6 5.8 %collective-permute-done.5.rest_3_ = bf16[192,1024]{1,0:T(8,128)(2,1)S(1)} collective-permute-done((bf16[192,1024]{1,0:T(8,128)(2,1)S(1)}, bf16[192,1024]{1,0:T(8,128)(2,1)S(1)}, u32[]{:S(2)}, u32[]{:S(2)}) %collective-permute-start.5) | collective-permute-done | bytes 393248 | tf_op jit(solution)/shard_map/ppermute | solution.py:582
  56.4 0.0 collective-permute-done.4.rest_2_
  56.4 0.2 merge.7
  56.7 17.7 %collective-permute-done.9 = bf16[192,1024]{1,0:T(8,128)(2,1)S(1)} collective-permute-done((bf16[192,1024]{1,0:T(8,128)(2,1)S(1)}, bf16[192,1024]{1,0:T(8,128)(2,1)S(1)}, u32[]{:S(2)}, u32[]{:S(2)}) %collective-permute-start.9) | collective-permute-done | bytes 393248 | tf_op jit(solution)/shard_map/ppermute | solution.py:586
  74.3 0.8 %add_convert_fusion = bf16[192,1024]{1,0:T(8,128)(2,1)} fusion(f32[192,1024]{1,0:T(8,128)S(1)} %merge.7, bf16[192,1024]{1,0:T(8,128)(2,1)S(1)} %collective-permute-done.9), kind=kLoop, calls=%fused_computation | loop fusion | flops 589824 | bytes 1572864 | tf_op jit(solution)/shard_map/convert_element_type | solution.py:541
Async XLA Ops:
  19.8 5.3 %collective-permute-start = (bf16[32,1024]{1,0:T(8,128)(2,1)S(1)}, bf16[32,1024]{1,0:T(8,128)(2,1)S(1)}, u32[]{:S(2)}, u32[]{:S(2)}) collective-permute-start(bf16[32,1024]{1,0:T(8,128)(2,1)S(1)} %get-tuple-element.35._.mine_ref.block_ref), channel_id=1, source_target_pairs={{0,8},{8,0},{16,24},{24,16},{1,9},{9,1},{17,25},{25,17},{2,10},{10... | collective-permute-start | bytes 196616 | tf_op jit(solution)/shard_map/ppermute | solution.py:689
  22.8 2.2 %copy-start = (s32[768]{0:T(1024)S(1)}, s32[768]{0:T(1024)}, u32[]{:S(2)}) copy-start(s32[768]{0:T(1024)} %ids_ref.3) | copy-start | bytes 9220
  25.8 4.4 %collective-permute-start.1 = (bf16[32,1024]{1,0:T(8,128)(2,1)S(1)}, bf16[32,1024]{1,0:T(8,128)(2,1)S(1)}, u32[]{:S(2)}, u32[]{:S(2)}) collective-permute-start(bf16[32,1024]{1,0:T(8,128)(2,1)S(1)} %join.1._), channel_id=1, source_target_pairs={{0,16},{8,24},{16,0},{24,8},{1,17},{9,25},{17,1},{25,9},{2,18},{10... | collective-permute-start | bytes 196616 | tf_op jit(solution)/shard_map/ppermute | solution.py:689
  33.4 2.9 %collective-permute-start.6 = (bf16[192,1024]{1,0:T(8,128)(2,1)S(1)}, bf16[192,1024]{1,0:T(8,128)(2,1)S(1)}, u32[]{:S(2)}, u32[]{:S(2)}) collective-permute-start(bf16[192,1024]{1,0:T(8,128)(2,1)S(1)} %get-tuple-element.61), channel_id=1, source_target_pairs={{0,1},{1,0},{2,3},{3,2},{4,5},{5,4},{6,7},{7,6},{8,9},{9,8},{10,11... | collective-permute-start | bytes 1179656 | tf_op jit(solution)/shard_map/ppermute | solution.py:576
  34.5 7.5 %collective-permute-start.3 = (bf16[192,1024]{1,0:T(8,128)(2,1)S(1)}, bf16[192,1024]{1,0:T(8,128)(2,1)S(1)}, u32[]{:S(2)}, u32[]{:S(2)}) collective-permute-start(bf16[192,1024]{1,0:T(8,128)(2,1)S(1)} %get-tuple-element.59), channel_id=1, source_target_pairs={{0,1},{1,0},{2,3},{3,2},{4,5},{5,4},{6,7},{7,6},{8,9},{9,8},{10,11... | collective-permute-start | bytes 1179656 | tf_op jit(solution)/shard_map/ppermute | solution.py:580
  36.2 11.2 %collective-permute-start.8 = (bf16[192,1024]{1,0:T(8,128)(2,1)S(1)}, bf16[192,1024]{1,0:T(8,128)(2,1)S(1)}, u32[]{:S(2)}, u32[]{:S(2)}) collective-permute-start(bf16[192,1024]{1,0:T(8,128)(2,1)S(1)} %get-tuple-element.64), channel_id=1, source_target_pairs={{0,1},{1,0},{2,3},{3,2},{4,5},{5,4},{6,7},{7,6},{8,9},{9,8},{10,11... | collective-permute-start | bytes 1179656 | tf_op jit(solution)/shard_map/ppermute | solution.py:584
  36.3 11.9 %collective-permute-start.7 = (bf16[192,1024]{1,0:T(8,128)(2,1)S(1)}, bf16[192,1024]{1,0:T(8,128)(2,1)S(1)}, u32[]{:S(2)}, u32[]{:S(2)}) collective-permute-start(bf16[192,1024]{1,0:T(8,128)(2,1)S(1)} %merge.6), channel_id=1, source_target_pairs={{0,2},{1,3},{2,0},{3,1},{4,6},{5,7},{6,4},{7,5},{8,10},{9,11},{10,... | collective-permute-start | bytes 1179656 | tf_op jit(solution)/shard_map/ppermute | solution.py:578
  41.7 8.8 %collective-permute-start.2 = (bf16[192,1024]{1,0:T(8,128)(2,1)S(1)}, bf16[192,1024]{1,0:T(8,128)(2,1)S(1)}, u32[]{:S(2)}, u32[]{:S(2)}) collective-permute-start(bf16[192,1024]{1,0:T(8,128)(2,1)S(1)} %get-tuple-element.56), channel_id=1, source_target_pairs={{0,1},{1,0},{2,3},{3,2},{4,5},{5,4},{6,7},{7,6},{8,9},{9,8},{10,11... | collective-permute-start | bytes 1179656 | tf_op jit(solution)/shard_map/ppermute | solution.py:588
  42.1 14.3 %collective-permute-start.5 = (bf16[192,1024]{1,0:T(8,128)(2,1)S(1)}, bf16[192,1024]{1,0:T(8,128)(2,1)S(1)}, u32[]{:S(2)}, u32[]{:S(2)}) collective-permute-start(bf16[192,1024]{1,0:T(8,128)(2,1)S(1)} %merge.5), channel_id=1, source_target_pairs={{0,4},{1,5},{6,2},{7,3},{8,12},{9,13},{14,10},{15,11},{16,20},{17,... | collective-permute-start | bytes 1179656 | tf_op jit(solution)/shard_map/ppermute | solution.py:582
  46.6 9.8 %collective-permute-start.4 = (bf16[192,1024]{1,0:T(8,128)(2,1)S(1)}, bf16[192,1024]{1,0:T(8,128)(2,1)S(1)}, u32[]{:S(2)}, u32[]{:S(2)}) collective-permute-start(bf16[192,1024]{1,0:T(8,128)(2,1)S(1)} %merge.5), channel_id=1, source_target_pairs={{2,4},{3,5},{4,2},{5,3},{10,12},{11,13},{12,10},{13,11},{18,20},{1... | collective-permute-start | bytes 1179656 | tf_op jit(solution)/shard_map/ppermute | solution.py:581
  48.3 26.0 %collective-permute-start.9 = (bf16[192,1024]{1,0:T(8,128)(2,1)S(1)}, bf16[192,1024]{1,0:T(8,128)(2,1)S(1)}, u32[]{:S(2)}, u32[]{:S(2)}) collective-permute-start(bf16[192,1024]{1,0:T(8,128)(2,1)S(1)} %merge.9), channel_id=1, source_target_pairs={{0,2},{1,3},{2,6},{3,7},{6,4},{7,5},{4,0},{5,1},{8,10},{9,11},{10,... | collective-permute-start | bytes 1179656 | tf_op jit(solution)/shard_map/ppermute | solution.py:586

commit v8 on v7

--- a/solution.py
+++ b/solution.py
@@ -566,6 +566,46 @@
     )(lane_position, *terms)
 
 
+def halves_kernel(_, mine_ref, other_ref, top_out, bottom_out):
+    rows = top_out.shape[0]
+    value = (mine_ref[...] + other_ref[...].astype(f32)).astype(bf16)
+    top_out[...] = value[:rows]
+    bottom_out[...] = value[rows:]
+
+
+def halves(lane_position, mine, other):
+    terms = [pltpu.with_memory_space_constraint(a, pltpu.VMEM) for a in (mine, other)]
+    return pl.pallas_call(
+        halves_kernel,
+        out_shape=(jax.ShapeDtypeStruct((mine.shape[0] // 2, mine.shape[1]), bf16),) * 2,
+        in_specs=[smem()] + [vmem()] * 2,
+        out_specs=[vmem()] * 2,
+        compiler_params=pltpu.CompilerParams(vmem_limit_bytes=3 * MIB),
+        name="halves",
+    )(lane_position, *terms)
+
+
+def own_kernel(lane_position, mine_ref, other_ref, near_ref, middle_ref, end_ref, again_ref, out):
+    rows = middle_ref.shape[0]
+    chip = lane_position[0] // 2
+    outer = (chip == 0) | (chip == 3)
+    value = mine_ref[...] + other_ref[...].astype(f32) + jnp.where(outer, near_ref[...].astype(f32), 0.0)
+    out[0:rows, :] = value[:rows] + (middle_ref[...].astype(f32) + end_ref[...].astype(f32))
+    out[rows:, :] = value[rows:] + again_ref[...].astype(f32)
+
+
+def gather_own(lane_position, mine, *others):
+    terms = [pltpu.with_memory_space_constraint(a, pltpu.VMEM) for a in (mine, *others)]
+    return pl.pallas_call(
+        own_kernel,
+        out_shape=jax.ShapeDtypeStruct(mine.shape, f32),
+        in_specs=[smem()] + [vmem()] * len(terms),
+        out_specs=vmem(),
+        compiler_params=pltpu.CompilerParams(vmem_limit_bytes=3 * MIB),
+        name="gather_own",
+    )(lane_position, *terms)
+
+
 def scatter_line(lane_position, gated, send, mine, window, third, out_weight, width):
     pair = [(m, m ^ 1) for m in range(8)]
 
@@ -577,15 +617,18 @@
     far = merge(lane_position, bf16, (mine, traded))
     from_near = lax.ppermute(far, "mp", near)
     send, mine = shares(lane_position, gated, [window], width)
-    second = merge(lane_position, bf16, (mine, lax.ppermute(send, "mp", pair)))
-    from_middle = lax.ppermute(second, "mp", along([(1, 2), (2, 1)]))
-    from_end = lax.ppermute(second, "mp", along([(0, 2), (3, 1)]))
+    top, bottom = halves(lane_position, mine, lax.ppermute(send, "mp", pair))
+    beside = lax.ppermute(bottom, "mp", near)
+    from_middle = lax.ppermute(top, "mp", along([(1, 2), (2, 1)]))
+    from_end = lax.ppermute(top, "mp", along([(0, 2), (3, 1)]))
     send2, mine2 = shares(lane_position, gated, [third], width)
     mine2 = merge(lane_position, f32, (mine2, lax.ppermute(send2, "mp", pair)))
     onward = merge(lane_position, bf16, (mine2,), inner=from_near)
     from_round = lax.ppermute(onward, "mp", along([(0, 1), (1, 3), (3, 2), (2, 0)]))
     send3, mine3 = late_share(3, lane_position, gated, out_weight, width)
-    own = merge(lane_position, f32, (mine3, lax.ppermute(send3, "mp", pair), from_middle, from_end), outer=from_near)
+    both = merge(lane_position, bf16, (bottom, beside))
+    again = lax.ppermute(both, "mp", along([(1, 2), (2, 1)]))
+    own = gather_own(lane_position, mine3, lax.ppermute(send3, "mp", pair), from_near, from_middle, from_end, again)
     return total(own, from_round)
 
 

time: 75.4 us -> 72.7 us (0.964)
  the two profiles are of different devices: /device:TPU:0 before, /device:TPU:16 now
where the time goes in v8:
time: 72.7 us; the launch traced here: 72.5 us
  Pallas kernels  34.1 us (47%)
  waiting for transfers between devices  22.8 us (31%)
  starting transfers between devices  14.5 us (20%)
  other arithmetic  0.84 us (1%)
    pallas_call x1, Pallas kernels, front(): pl.pallas_call(functools.partial(front_kernel, geometry), out_shape=[jax....  19.8 us
    ppermute x1, waiting for transfers between devices, scatter_line(): from_near = lax.ppermute(far, 'mp', near)  6.15 us
    ppermute x1, waiting for transfers between devices, scatter_line(): from_middle = lax.ppermute(top, 'mp', along([(1, 2), (2, 1)]))  5.24 us
    ppermute x1, starting transfers between devices, scatter_line(): from_middle = lax.ppermute(top, 'mp', along([(1, 2), (2, 1)]))  4.92 us
    pallas_call x2, Pallas kernels, local_pass(): pl.pallas_call(functools.partial(local_kernel, poles, first, slot), out_s...  4.45 us
    ppermute x1, waiting for transfers between devices, scatter_line(): from_end = lax.ppermute(top, 'mp', along([(0, 2), (3, 1)]))  4.16 us
    ppermute x1, waiting for transfers between devices, scatter_line(): beside = lax.ppermute(bottom, 'mp', near)  3.79 us
    pallas_call x1, Pallas kernels, gate(): pl.pallas_call(functools.partial(gate_kernel, T, poles, tuple(spans), len...  3.27 us
  transfers between devices with their start and end apart: 12, of which 7 were waited for; matrix products, arithmetic and copies ran while one was open for 0% of the time, Pallas kernels for 14%

profile of v8, /device:TPU:16, one launch (start us, length us, event | category | flops | bytes accessed | tf_op | source)
XLA Modules:
  0.0 72.5 jit_solution(17547087540647112149)
XLA Ops:
  0.0 19.8 %front.1 = (f32[200,1024]{1,0:T(8,128)S(1)}, f32[8,192,128]{2,1,0:T(8,128)S(1)}, bf16[32,1024]{1,0:T(8,128)(2,1)S(1)}, f32[192,128]{1,0:T(8,128)S(1)}, f32[192,1...) custom-call(s32[1]{0:T(128)} %bitcast.1.position, ...), custom_call_target="tpu_custom_call" | custom-call | tf_op jit(solution)/shard_map/front/pallas_call | solution.py:178
  19.8 1.6 %collective-permute-start = (bf16[32,1024]{1,0:T(8,128)(2,1)S(1)}, bf16[32,1024]{1,0:T(8,128)(2,1)S(1)}, u32[]{:S(2)}, u32[]{:S(2)}) collective-permute-start(bf16[32,1024]{1,0:T(8,128)(2,1)S(1)} %get-tuple-element.37._.mine_ref.block_ref), channel_id=1, source_target_pairs={{0,8},{8,0},{16,24},{24,16},{1,9},{9,1},{17,25},{25,17},{2,10},{10... | collective-permute-start | bytes 196616 | tf_op jit(solution)/shard_map/ppermute | solution.py:732
  21.3 0.0 copy-start
  21.3 2.2 %local_pass.2 = (f32[4,192,128]{2,1,0:T(8,128)S(1)}, f32[4,128,128]{2,1,0:T(8,128)S(1)}, f32[16,512]{1,0:T(8,128)S(1)}, f32[4,192,128]{2,1,0:T(8,128)S(1)}, bf16[1024,2048]{1,0:T(8,128)(2,1)S(1)}) custom-call(s32[1]{0:T(128)} %bitcast.lane_position._, f32[8,192,128]{2,1,0:T(8,128)S(1)} %get-tuple-element.42.prod_ref, ...), custom_call_target="tpu_custom_call" | custom-call | flops 9437184 | bytes 8388608 | tf_op jit(solution)/shard_map/local_pass/pallas_call | solution.py:268
  23.6 0.5 collective-permute-done.other_ref.rest_0_
  24.1 0.0 copy-done
  24.1 0.7 join.1._
  24.8 1.6 %collective-permute-start.1 = (bf16[32,1024]{1,0:T(8,128)(2,1)S(1)}, bf16[32,1024]{1,0:T(8,128)(2,1)S(1)}, u32[]{:S(2)}, u32[]{:S(2)}) collective-permute-start(bf16[32,1024]{1,0:T(8,128)(2,1)S(1)} %join.1._), channel_id=1, source_target_pairs={{0,16},{8,24},{16,0},{24,8},{1,17},{9,25},{17,1},{25,9},{2,18},{10... | collective-permute-start | bytes 196616 | tf_op jit(solution)/shard_map/ppermute | solution.py:732
  26.4 2.2 %local_pass.3 = (f32[4,192,128]{2,1,0:T(8,128)S(1)}, f32[4,128,128]{2,1,0:T(8,128)S(1)}, f32[16,512]{1,0:T(8,128)S(1)}, f32[4,192,128]{2,1,0:T(8,128)S(1)}, bf16[1024,2048]{1,0:T(8,128)(2,1)S(1)}) custom-call(s32[1]{0:T(128)} %bitcast.lane_position._, f32[8,192,128]{2,1,0:T(8,128)S(1)} %get-tuple-element.42.prod_ref, ...), custom_call_target="tpu_custom_call" | custom-call | flops 9437184 | bytes 8388608 | tf_op jit(solution)/shard_map/local_pass/pallas_call | solution.py:268
  28.6 0.5 collective-permute-done.1.rest_1_
  29.1 3.3 %gate.1 = (bf16[192,1024]{1,0:T(8,128)(2,1)S(1)}, bf16[192,1024]{1,0:T(8,128)(2,1)S(1)}, f32[192,1024]{1,0:T(8,128)S(1)}, bf16[1024,2048]{1,0:T(8,128)(2,1)S(1)}) custom-call(s32[1]{0:T(128)} %bitcast.1.position, s32[1]{0:T(128)} %bitcast.lane_position._, s32[768]{0:T(1024)S(1)} %copy-done, bf16[32,1024]{1,0:T(8,128)(2,1)S(1)} %get-tuple-element.37._.mine_ref.block_ref, ...), custom_call_target="tpu_custom_call" | custom-call | tf_op jit(solution)/shard_map/gate/pallas_call | solution.py:519
  32.4 0.1 collective-permute-start.3
  32.5 1.1 %shares.2 = (bf16[192,1024]{1,0:T(8,128)(2,1)S(1)}, f32[192,1024]{1,0:T(8,128)S(1)}) custom-call(s32[1]{0:T(128)} %bitcast.lane_position._, bf16[192,1024]{1,0:T(8,128)(2,1)S(1)} %get-tuple-element.56.gated_ref, bf16[1024,2048]{1,0:T(8,128)(2,1)S(1)} %get-tuple-element.61.rest_0_), custom_call_target="tpu_custom_call" | custom-call | flops 805306368 | bytes 4194304 | tf_op jit(solution)/shard_map/shares/pallas_call | solution.py:483
  33.6 0.6 collective-permute-start.5
  34.1 1.0 %shares.3 = (bf16[192,1024]{1,0:T(8,128)(2,1)S(1)}, f32[192,1024]{1,0:T(8,128)S(1)}) custom-call(s32[1]{0:T(128)} %bitcast.lane_position._, bf16[192,1024]{1,0:T(8,128)(2,1)S(1)} %get-tuple-element.56.gated_ref, bf16[1024,2048]{1,0:T(8,128)(2,1)S(1)} %get-tuple-element.66.rest_0_), custom_call_target="tpu_custom_call" | custom-call | flops 805306368 | bytes 4194304 | tf_op jit(solution)/shard_map/shares/pallas_call | solution.py:483
  35.2 0.1 collective-permute-start.10
  35.3 0.0 collective-permute-done.3.rest_1_
  35.3 0.1 merge.4
  35.4 1.6 %collective-permute-start.4 = (bf16[192,1024]{1,0:T(8,128)(2,1)S(1)}, bf16[192,1024]{1,0:T(8,128)(2,1)S(1)}, u32[]{:S(2)}, u32[]{:S(2)}) collective-permute-start(bf16[192,1024]{1,0:T(8,128)(2,1)S(1)} %merge.4), channel_id=1, source_target_pairs={{0,2},{1,3},{2,0},{3,1},{4,6},{5,7},{6,4},{7,5},{8,10},{9,11},{10,... | collective-permute-start | bytes 1179656 | tf_op jit(solution)/shard_map/ppermute | solution.py:618
  37.0 3.3 %late_share.1 = (bf16[192,1024]{1,0:T(8,128)(2,1)S(1)}, f32[192,1024]{1,0:T(8,128)S(1)}) custom-call(s32[1]{0:T(128)} %bitcast.lane_position._, bf16[192,1024]{1,0:T(8,128)(2,1)S(1)} %get-tuple-element.56.gated_ref, bf16[1024,8192]{1,0:T(8,128)(2,1)} %out_ref.7), custom_call_target="tpu_custom_call" | custom-call | flops 805306368 | bytes 4194304 | tf_op jit(solution)/shard_map/late_share/pallas_call | solution.py:504
  40.3 0.3 collective-permute-start.2
  40.5 0.0 collective-permute-done.5.other_ref
  40.5 0.1 halves.1
  40.6 0.5 collective-permute-start.8
  41.2 0.0 collective-permute-done.10.rest_1_
  41.2 0.1 merge.6.rest_0_
  41.3 6.2 %collective-permute-done.4.near_ref.rest_1_ = bf16[192,1024]{1,0:T(8,128)(2,1)S(1)} collective-permute-done((bf16[192,1024]{1,0:T(8,128)(2,1)S(1)}, bf16[192,1024]{1,0:T(8,128)(2,1)S(1)}, u32[]{:S(2)}, u32[]{:S(2)}) %collective-permute-start.4) | collective-permute-done | bytes 393248 | tf_op jit(solution)/shard_map/ppermute | solution.py:618
  47.4 0.1 merge.7
  47.5 0.1 collective-permute-start.11
  47.6 1.3 %collective-permute-start.7 = (bf16[96,1024]{1,0:T(8,128)(2,1)S(1)}, bf16[96,1024]{1,0:T(8,128)(2,1)S(1)}, u32[]{:S(2)}, u32[]{:S(2)}) collective-permute-start(bf16[96,1024]{1,0:T(8,128)(2,1)S(1)} %get-tuple-element.64), channel_id=1, source_target_pairs={{0,4},{1,5},{6,2},{7,3},{8,12},{9,13},{14,10},{15,11},{16,20},{17,... | collective-permute-start | bytes 589832 | tf_op jit(solution)/shard_map/ppermute | solution.py:623
  48.9 4.9 %collective-permute-start.6 = (bf16[96,1024]{1,0:T(8,128)(2,1)S(1)}, bf16[96,1024]{1,0:T(8,128)(2,1)S(1)}, u32[]{:S(2)}, u32[]{:S(2)}) collective-permute-start(bf16[96,1024]{1,0:T(8,128)(2,1)S(1)} %get-tuple-element.64), channel_id=1, source_target_pairs={{2,4},{3,5},{4,2},{5,3},{10,12},{11,13},{12,10},{13,11},{18,20},{1... | collective-permute-start | bytes 589832 | tf_op jit(solution)/shard_map/ppermute | solution.py:622
  53.8 3.8 %collective-permute-done.8.rest_1_ = bf16[96,1024]{1,0:T(8,128)(2,1)S(1)} collective-permute-done((bf16[96,1024]{1,0:T(8,128)(2,1)S(1)}, bf16[96,1024]{1,0:T(8,128)(2,1)S(1)}, u32[]{:S(2)}, u32[]{:S(2)}) %collective-permute-start.8) | collective-permute-done | bytes 196640 | tf_op jit(solution)/shard_map/ppermute | solution.py:621
  57.6 1.9 %collective-permute-start.9 = (bf16[96,1024]{1,0:T(8,128)(2,1)S(1)}, bf16[96,1024]{1,0:T(8,128)(2,1)S(1)}, u32[]{:S(2)}, u32[]{:S(2)}) collective-permute-start(bf16[96,1024]{1,0:T(8,128)(2,1)S(1)} %merge.5), channel_id=1, source_target_pairs={{2,4},{3,5},{4,2},{5,3},{10,12},{11,13},{12,10},{13,11},{18,20},{1... | collective-permute-start | bytes 589832 | tf_op jit(solution)/shard_map/ppermute | solution.py:630
  59.6 0.0 collective-permute-done.2.other_ref
  59.6 4.2 %collective-permute-done.7.end_ref = bf16[96,1024]{1,0:T(8,128)(2,1)S(1)} collective-permute-done((bf16[96,1024]{1,0:T(8,128)(2,1)S(1)}, bf16[96,1024]{1,0:T(8,128)(2,1)S(1)}, u32[]{:S(2)}, u32[]{:S(2)}) %collective-permute-start.7) | collective-permute-done | bytes 196640 | tf_op jit(solution)/shard_map/ppermute | solution.py:623
  63.7 5.2 %collective-permute-done.6.middle_ref = bf16[96,1024]{1,0:T(8,128)(2,1)S(1)} collective-permute-done((bf16[96,1024]{1,0:T(8,128)(2,1)S(1)}, bf16[96,1024]{1,0:T(8,128)(2,1)S(1)}, u32[]{:S(2)}, u32[]{:S(2)}) %collective-permute-start.6) | collective-permute-done | bytes 196640 | tf_op jit(solution)/shard_map/ppermute | solution.py:622
  69.0 2.4 %collective-permute-done.9.again_ref = bf16[96,1024]{1,0:T(8,128)(2,1)S(1)} collective-permute-done((bf16[96,1024]{1,0:T(8,128)(2,1)S(1)}, bf16[96,1024]{1,0:T(8,128)(2,1)S(1)}, u32[]{:S(2)}, u32[]{:S(2)}) %collective-permute-start.9) | collective-permute-done | bytes 196640 | tf_op jit(solution)/shard_map/ppermute | solution.py:630
  71.4 0.2 gather_own.1
  71.6 0.0 collective-permute-done.11
  71.6 0.8 %add_convert_fusion = bf16[192,1024]{1,0:T(8,128)(2,1)} fusion(f32[192,1024]{1,0:T(8,128)S(1)} %gather_own.1, bf16[192,1024]{1,0:T(8,128)(2,1)S(1)} %collective-permute-done.11), kind=kLoop, calls=%fused_computation | loop fusion | flops 589824 | bytes 1572864 | tf_op jit(solution)/shard_map/convert_element_type | solution.py:541
  (1 shorter events, 0.0 us)
Async XLA Ops:
  19.8 4.3 %collective-permute-start = (bf16[32,1024]{1,0:T(8,128)(2,1)S(1)}, bf16[32,1024]{1,0:T(8,128)(2,1)S(1)}, u32[]{:S(2)}, u32[]{:S(2)}) collective-permute-start(bf16[32,1024]{1,0:T(8,128)(2,1)S(1)} %get-tuple-element.37._.mine_ref.block_ref), channel_id=1, source_target_pairs={{0,8},{8,0},{16,24},{24,16},{1,9},{9,1},{17,25},{25,17},{2,10},{10... | collective-permute-start | bytes 196616 | tf_op jit(solution)/shard_map/ppermute | solution.py:732
  21.3 2.8 %copy-start = (s32[768]{0:T(1024)S(1)}, s32[768]{0:T(1024)}, u32[]{:S(2)}) copy-start(s32[768]{0:T(1024)} %ids_ref.3) | copy-start | bytes 9220
  24.8 4.3 %collective-permute-start.1 = (bf16[32,1024]{1,0:T(8,128)(2,1)S(1)}, bf16[32,1024]{1,0:T(8,128)(2,1)S(1)}, u32[]{:S(2)}, u32[]{:S(2)}) collective-permute-start(bf16[32,1024]{1,0:T(8,128)(2,1)S(1)} %join.1._), channel_id=1, source_target_pairs={{0,16},{8,24},{16,0},{24,8},{1,17},{9,25},{17,1},{25,9},{2,18},{10... | collective-permute-start | bytes 196616 | tf_op jit(solution)/shard_map/ppermute | solution.py:732
  32.4 2.9 %collective-permute-start.3 = (bf16[192,1024]{1,0:T(8,128)(2,1)S(1)}, bf16[192,1024]{1,0:T(8,128)(2,1)S(1)}, u32[]{:S(2)}, u32[]{:S(2)}) collective-permute-start(bf16[192,1024]{1,0:T(8,128)(2,1)S(1)} %get-tuple-element.60), channel_id=1, source_target_pairs={{0,1},{1,0},{2,3},{3,2},{4,5},{5,4},{6,7},{7,6},{8,9},{9,8},{10,11... | collective-permute-start | bytes 1179656 | tf_op jit(solution)/shard_map/ppermute | solution.py:616
  33.6 7.0 %collective-permute-start.5 = (bf16[192,1024]{1,0:T(8,128)(2,1)S(1)}, bf16[192,1024]{1,0:T(8,128)(2,1)S(1)}, u32[]{:S(2)}, u32[]{:S(2)}) collective-permute-start(bf16[192,1024]{1,0:T(8,128)(2,1)S(1)} %get-tuple-element.63), channel_id=1, source_target_pairs={{0,1},{1,0},{2,3},{3,2},{4,5},{5,4},{6,7},{7,6},{8,9},{9,8},{10,11... | collective-permute-start | bytes 1179656 | tf_op jit(solution)/shard_map/ppermute | solution.py:620
  35.2 6.0 %collective-permute-start.10 = (bf16[192,1024]{1,0:T(8,128)(2,1)S(1)}, bf16[192,1024]{1,0:T(8,128)(2,1)S(1)}, u32[]{:S(2)}, u32[]{:S(2)}) collective-permute-start(bf16[192,1024]{1,0:T(8,128)(2,1)S(1)} %get-tuple-element.68), channel_id=1, source_target_pairs={{0,1},{1,0},{2,3},{3,2},{4,5},{5,4},{6,7},{7,6},{8,9},{9,8},{10,11... | collective-permute-start | bytes 1179656 | tf_op jit(solution)/shard_map/ppermute | solution.py:625
  35.4 12.1 %collective-permute-start.4 = (bf16[192,1024]{1,0:T(8,128)(2,1)S(1)}, bf16[192,1024]{1,0:T(8,128)(2,1)S(1)}, u32[]{:S(2)}, u32[]{:S(2)}) collective-permute-start(bf16[192,1024]{1,0:T(8,128)(2,1)S(1)} %merge.4), channel_id=1, source_target_pairs={{0,2},{1,3},{2,0},{3,1},{4,6},{5,7},{6,4},{7,5},{8,10},{9,11},{10,... | collective-permute-start | bytes 1179656 | tf_op jit(solution)/shard_map/ppermute | solution.py:618
  40.3 19.3 %collective-permute-start.2 = (bf16[192,1024]{1,0:T(8,128)(2,1)S(1)}, bf16[192,1024]{1,0:T(8,128)(2,1)S(1)}, u32[]{:S(2)}, u32[]{:S(2)}) collective-permute-start(bf16[192,1024]{1,0:T(8,128)(2,1)S(1)} %get-tuple-element.58), channel_id=1, source_target_pairs={{0,1},{1,0},{2,3},{3,2},{4,5},{5,4},{6,7},{7,6},{8,9},{9,8},{10,11... | collective-permute-start | bytes 1179656 | tf_op jit(solution)/shard_map/ppermute | solution.py:631
  40.6 17.0 %collective-permute-start.8 = (bf16[96,1024]{1,0:T(8,128)(2,1)S(1)}, bf16[96,1024]{1,0:T(8,128)(2,1)S(1)}, u32[]{:S(2)}, u32[]{:S(2)}) collective-permute-start(bf16[96,1024]{1,0:T(8,128)(2,1)S(1)} %get-tuple-element.65.rest_0_), channel_id=1, source_target_pairs={{0,2},{1,3},{2,0},{3,1},{4,6},{5,7},{6,4},{7,5},{8,10},{9,11},{10,... | collective-permute-start | bytes 589832 | tf_op jit(solution)/shard_map/ppermute | solution.py:621
  47.5 24.1 %collective-permute-start.11 = (bf16[192,1024]{1,0:T(8,128)(2,1)S(1)}, bf16[192,1024]{1,0:T(8,128)(2,1)S(1)}, u32[]{:S(2)}, u32[]{:S(2)}) collective-permute-start(bf16[192,1024]{1,0:T(8,128)(2,1)S(1)} %merge.7), channel_id=1, source_target_pairs={{0,2},{1,3},{2,6},{3,7},{6,4},{7,5},{4,0},{5,1},{8,10},{9,11},{10,... | collective-permute-start | bytes 1179656 | tf_op jit(solution)/shard_map/ppermute | solution.py:627
  47.6 16.2 %collective-permute-start.7 = (bf16[96,1024]{1,0:T(8,128)(2,1)S(1)}, bf16[96,1024]{1,0:T(8,128)(2,1)S(1)}, u32[]{:S(2)}, u32[]{:S(2)}) collective-permute-start(bf16[96,1024]{1,0:T(8,128)(2,1)S(1)} %get-tuple-element.64), channel_id=1, source_target_pairs={{0,4},{1,5},{6,2},{7,3},{8,12},{9,13},{14,10},{15,11},{16,20},{17,... | collective-permute-start | bytes 589832 | tf_op jit(solution)/shard_map/ppermute | solution.py:623
  48.9 20.1 %collective-permute-start.6 = (bf16[96,1024]{1,0:T(8,128)(2,1)S(1)}, bf16[96,1024]{1,0:T(8,128)(2,1)S(1)}, u32[]{:S(2)}, u32[]{:S(2)}) collective-permute-start(bf16[96,1024]{1,0:T(8,128)(2,1)S(1)} %get-tuple-element.64), channel_id=1, source_target_pairs={{2,4},{3,5},{4,2},{5,3},{10,12},{11,13},{12,10},{13,11},{18,20},{1... | collective-permute-start | bytes 589832 | tf_op jit(solution)/shard_map/ppermute | solution.py:622
  57.6 13.7 %collective-permute-start.9 = (bf16[96,1024]{1,0:T(8,128)(2,1)S(1)}, bf16[96,1024]{1,0:T(8,128)(2,1)S(1)}, u32[]{:S(2)}, u32[]{:S(2)}) collective-permute-start(bf16[96,1024]{1,0:T(8,128)(2,1)S(1)} %merge.5), channel_id=1, source_target_pairs={{2,4},{3,5},{4,2},{5,3},{10,12},{11,13},{12,10},{13,11},{18,20},{1... | collective-permute-start | bytes 589832 | tf_op jit(solution)/shard_map/ppermute | solution.py:630

commit v9 on v8

--- a/solution.py
+++ b/solution.py
@@ -347,7 +347,7 @@
 ):
     arrived, rest = rest[: len(spans)], rest[len(spans) :]
     parts, rest = [rest[4 * c : 4 * c + 4] for c in range(cuts)], rest[4 * cuts :]
-    gated_out, send_out, mine_out, third_out, carry, full, sem = rest
+    gated_out, send_out, third_out, carry, full, sem = rest
     run = T // PARTS
     tiles = block_ref.shape[1] // 128
     copy = columns(lane_position[0], 2, out_ref, third_out, sem)
@@ -417,7 +417,7 @@
         top_q = top_q + jnp.where(row == 0, q_shift[0][:, lanes], 0.0) + jnp.where(row == 1, q_shift[1][:, lanes], 0.0)
         top = top + jnp.where(row == 0, fix0[:, lanes], 0.0) + jnp.where(row == 1, fix1[:, lanes], 0.0)
         gated_out[0:16, lanes] = (top_q * top).astype(bf16)
-    share(lane_position[0], gated_out, window_ref, send_out, mine_out)
+    share(lane_position[0], gated_out, window_ref, send_out, None)
     copy.wait()
 
 
@@ -460,13 +460,13 @@
 
 
 def share(index, gated_ref, window, send_out, mine_out):
-    width = send_out.shape[1]
+    width = window.shape[1] // 2
     tile = 256
     core = index % 2
 
-    for j in range(width // tile):
-        at = slice(j * tile, j * tile + tile)
-        for out, half in ((send_out, 1 - core), (mine_out, core)):
+    for out, half in ((send_out, 1 - core), (mine_out, core)):
+        for j in range(width // tile if out is not None else 0):
+            at = slice(j * tile, j * tile + tile)
             cols = pl.ds(pl.multiple_of(half * width + j * tile, tile), tile)
             out[:, at] = jnp.dot(gated_ref[...], window[:, cols], preferred_element_type=f32).astype(out.dtype)
 
@@ -490,6 +490,25 @@
             flops=4 * T * channels * width * count, bytes_accessed=4 * channels * width * count, transcendentals=0),
         name="shares",
     )(lane_position, gated, *windows)
+
+
+def second_kernel(lane_position, gated_ref, first_ref, second_ref, first_mine, send_out, mine_out):
+    share(lane_position[0], gated_ref, second_ref, send_out, mine_out)
+    share(lane_position[0], gated_ref, first_ref, None, first_mine)
+
+
+def second_shares(lane_position, gated, first, second, width):
+    T, channels = gated.shape
+    return pl.pallas_call(
+        second_kernel,
+        out_shape=[jax.ShapeDtypeStruct((T, width), d) for d in (f32, bf16, f32)],
+        in_specs=[smem()] + [vmem()] * 3,
+        out_specs=[vmem()] * 3,
+        compiler_params=pltpu.CompilerParams(vmem_limit_bytes=4 * MIB),
+        cost_estimate=pl.CostEstimate(
+            flops=6 * T * channels * width, bytes_accessed=6 * channels * width, transcendentals=0),
+        name="second_shares",
+    )(lane_position, gated, first, second)
 
 
 def late_share_kernel(slot, lane_position, gated_ref, out_ref, send_out, mine_out, window, sem):
@@ -521,11 +540,10 @@
         out_shape=[
             jax.ShapeDtypeStruct((T, channels), bf16),
             jax.ShapeDtypeStruct((T, width), bf16),
-            jax.ShapeDtypeStruct((T, width), f32),
             pltpu.VMEM(window.shape, bf16),
         ],
         in_specs=[smem()] * 3 + [vmem()] * 6 + [hbm()] + [vmem()] * (len(spans) + 4 * len(parts)),
-        out_specs=[vmem()] * 4,
+        out_specs=[vmem()] * 3,
         scratch_shapes=[
             pltpu.VMEM((channels // 128, PARTS * poles, 128), f32),
             pltpu.VMEM((channels // 128, T, 128), f32),
@@ -606,7 +624,7 @@
     )(lane_position, *terms)
 
 
-def scatter_line(lane_position, gated, send, mine, window, third, out_weight, width):
+def scatter_line(lane_position, gated, send, windows, third, out_weight, width):
     pair = [(m, m ^ 1) for m in range(8)]
 
     def along(hops):
@@ -614,9 +632,9 @@
 
     near = along([(0, 1), (1, 0), (2, 3), (3, 2)])
     traded = lax.ppermute(send, "mp", pair)
-    far = merge(lane_position, bf16, (mine, traded))
+    first_mine, send, mine = second_shares(lane_position, gated, *windows, width)
+    far = merge(lane_position, bf16, (first_mine, traded))
     from_near = lax.ppermute(far, "mp", near)
-    send, mine = shares(lane_position, gated, [window], width)
     top, bottom = halves(lane_position, mine, lax.ppermute(send, "mp", pair))
     beside = lax.ppermute(bottom, "mp", near)
     from_middle = lax.ppermute(top, "mp", along([(1, 2), (2, 1)]))
@@ -739,9 +757,9 @@
         windows.append(window)
         if k < cuts - 1:
             group = join(span, T, position, segment_ids, group, other, taps, rates, part[0])
-    gated, send, mine, third = gate(T, spans, arrived, position, lane_position, segment_ids, parts, block, visible, taps, rates,
+    gated, send, third = gate(T, spans, arrived, position, lane_position, segment_ids, parts, block, visible, taps, rates,
                              skip, windows[0], out_weight, width)
-    return scatter_line(lane_position, gated, send, mine, windows[1], third, out_weight, width)
+    return scatter_line(lane_position, gated, send, windows[:2], third, out_weight, width)
 
 
 def solution(mesh):

time: 72.7 us -> 72.6 us (level)
    pallas_call x0 -> x1, Pallas kernels: none -> 1.46 us  [second_shares(): pl.pallas_call(second_kernel, out_shape=[jax.ShapeDtypeStruct((T, width),...]
    pallas_call x2 -> x1, Pallas kernels: 2.11 us -> 1.03 us  [shares(): pl.pallas_call(functools.partial(share_kernel, count), out_shape=[jax.Sha...]
  transfers between devices with their start and end apart: 12 -> 12, of which waited for: 7 -> 7; matrix products, arithmetic and copies ran while one was open for 0% -> 0% of each run, Pallas kernels for 14% -> 15%
where the time goes in v9:
time: 72.6 us; the launch traced here: 72.4 us
  Pallas kernels  34 us (47%)
  waiting for transfers between devices  22.9 us (32%)
  starting transfers between devices  14.5 us (20%)
  other arithmetic  0.84 us (1%)
    pallas_call x1, Pallas kernels, front(): pl.pallas_call(functools.partial(front_kernel, geometry), out_shape=[jax....  19.8 us
    ppermute x1, waiting for transfers between devices, scatter_line(): from_near = lax.ppermute(far, 'mp', near)  6.21 us
    ppermute x1, waiting for transfers between devices, scatter_line(): from_middle = lax.ppermute(top, 'mp', along([(1, 2), (2, 1)]))  5.22 us
    ppermute x1, starting transfers between devices, scatter_line(): from_middle = lax.ppermute(top, 'mp', along([(1, 2), (2, 1)]))  4.92 us
    pallas_call x2, Pallas kernels, local_pass(): pl.pallas_call(functools.partial(local_kernel, poles, first, slot), out_s...  4.45 us
    ppermute x1, waiting for transfers between devices, scatter_line(): from_end = lax.ppermute(top, 'mp', along([(0, 2), (3, 1)]))  4.15 us
    ppermute x1, waiting for transfers between devices, scatter_line(): beside = lax.ppermute(bottom, 'mp', near)  3.83 us
    pallas_call x1, Pallas kernels, late_share(): pl.pallas_call(functools.partial(late_share_kernel, slot), out_shape=[jax...  3.25 us
  transfers between devices with their start and end apart: 12, of which 7 were waited for; matrix products, arithmetic and copies ran while one was open for 0% of the time, Pallas kernels for 15%

profile of v9, /device:TPU:16, one launch (start us, length us, event | category | flops | bytes accessed | tf_op | source)
XLA Modules:
  0.0 72.4 jit_solution(4240032512844205926)
XLA Ops:
  0.0 19.8 %front.1 = (f32[200,1024]{1,0:T(8,128)S(1)}, f32[8,192,128]{2,1,0:T(8,128)S(1)}, bf16[32,1024]{1,0:T(8,128)(2,1)S(1)}, f32[192,128]{1,0:T(8,128)S(1)}, f32[192,1...) custom-call(s32[1]{0:T(128)} %bitcast.1.position, ...), custom_call_target="tpu_custom_call" | custom-call | tf_op jit(solution)/shard_map/front/pallas_call | solution.py:178
  19.8 1.6 %collective-permute-start = (bf16[32,1024]{1,0:T(8,128)(2,1)S(1)}, bf16[32,1024]{1,0:T(8,128)(2,1)S(1)}, u32[]{:S(2)}, u32[]{:S(2)}) collective-permute-start(bf16[32,1024]{1,0:T(8,128)(2,1)S(1)} %get-tuple-element.37._.mine_ref.block_ref), channel_id=1, source_target_pairs={{0,8},{8,0},{16,24},{24,16},{1,9},{9,1},{17,25},{25,17},{2,10},{10... | collective-permute-start | bytes 196616 | tf_op jit(solution)/shard_map/ppermute | solution.py:750
  21.3 0.0 copy-start
  21.3 2.2 %local_pass.2 = (f32[4,192,128]{2,1,0:T(8,128)S(1)}, f32[4,128,128]{2,1,0:T(8,128)S(1)}, f32[16,512]{1,0:T(8,128)S(1)}, f32[4,192,128]{2,1,0:T(8,128)S(1)}, bf16[1024,2048]{1,0:T(8,128)(2,1)S(1)}) custom-call(s32[1]{0:T(128)} %bitcast.lane_position._, f32[8,192,128]{2,1,0:T(8,128)S(1)} %get-tuple-element.42.prod_ref, ...), custom_call_target="tpu_custom_call" | custom-call | flops 9437184 | bytes 8388608 | tf_op jit(solution)/shard_map/local_pass/pallas_call | solution.py:268
  23.6 0.5 collective-permute-done.other_ref.rest_0_
  24.1 0.0 copy-done
  24.1 0.7 join.1._
  24.8 1.6 %collective-permute-start.1 = (bf16[32,1024]{1,0:T(8,128)(2,1)S(1)}, bf16[32,1024]{1,0:T(8,128)(2,1)S(1)}, u32[]{:S(2)}, u32[]{:S(2)}) collective-permute-start(bf16[32,1024]{1,0:T(8,128)(2,1)S(1)} %join.1._), channel_id=1, source_target_pairs={{0,16},{8,24},{16,0},{24,8},{1,17},{9,25},{17,1},{25,9},{2,18},{10... | collective-permute-start | bytes 196616 | tf_op jit(solution)/shard_map/ppermute | solution.py:750
  26.4 2.2 %local_pass.3 = (f32[4,192,128]{2,1,0:T(8,128)S(1)}, f32[4,128,128]{2,1,0:T(8,128)S(1)}, f32[16,512]{1,0:T(8,128)S(1)}, f32[4,192,128]{2,1,0:T(8,128)S(1)}, bf16[1024,2048]{1,0:T(8,128)(2,1)S(1)}) custom-call(s32[1]{0:T(128)} %bitcast.lane_position._, f32[8,192,128]{2,1,0:T(8,128)S(1)} %get-tuple-element.42.prod_ref, ...), custom_call_target="tpu_custom_call" | custom-call | flops 9437184 | bytes 8388608 | tf_op jit(solution)/shard_map/local_pass/pallas_call | solution.py:268
  28.6 0.5 collective-permute-done.1.rest_1_
  29.1 2.9 %gate.1 = (bf16[192,1024]{1,0:T(8,128)(2,1)S(1)}, bf16[192,1024]{1,0:T(8,128)(2,1)S(1)}, bf16[1024,2048]{1,0:T(8,128)(2,1)S(1)}) custom-call(s32[1]{0:T(128)} %bitcast.1.position, s32[1]{0:T(128)} %bitcast.lane_position._, s32[768]{0:T(1024)S(1)} %copy-done, bf16[32,1024]{1,0:T(8,128)(2,1)S(1)} %get-tuple-element.37._.mine_ref.block_ref, ...), custom_call_target="tpu_custom_call" | custom-call | tf_op jit(solution)/shard_map/gate/pallas_call | solution.py:538
  32.0 0.1 collective-permute-start.3
  32.1 1.5 %second_shares.1 = (f32[192,1024]{1,0:T(8,128)S(1)}, bf16[192,1024]{1,0:T(8,128)(2,1)S(1)}, f32[192,1024]{1,0:T(8,128)S(1)}) custom-call(s32[1]{0:T(128)} %bitcast.lane_position._, bf16[192,1024]{1,0:T(8,128)(2,1)S(1)} %get-tuple-element.56.gated_ref, bf16[1024,2048]{1,0:T(8,128)(2,1)S(1)} %get-tuple-element.47.window_ref.first_ref, ...), custom_call_target="tpu_custom_call" | custom-call | flops 1207959552 | bytes 6291456 | tf_op jit(solution)/shard_map/second_shares/pallas_call | solution.py:502
  33.5 0.5 collective-permute-start.5
  34.1 1.0 %shares.1 = (bf16[192,1024]{1,0:T(8,128)(2,1)S(1)}, f32[192,1024]{1,0:T(8,128)S(1)}) custom-call(s32[1]{0:T(128)} %bitcast.lane_position._, bf16[192,1024]{1,0:T(8,128)(2,1)S(1)} %get-tuple-element.56.gated_ref, bf16[1024,2048]{1,0:T(8,128)(2,1)S(1)} %get-tuple-element.66.rest_0_), custom_call_target="tpu_custom_call" | custom-call | flops 805306368 | bytes 4194304 | tf_op jit(solution)/shard_map/shares/pallas_call | solution.py:483
  35.1 0.1 collective-permute-start.10
  35.2 0.0 collective-permute-done.3.rest_1_
  35.2 0.1 merge.4
  35.3 1.6 %collective-permute-start.4 = (bf16[192,1024]{1,0:T(8,128)(2,1)S(1)}, bf16[192,1024]{1,0:T(8,128)(2,1)S(1)}, u32[]{:S(2)}, u32[]{:S(2)}) collective-permute-start(bf16[192,1024]{1,0:T(8,128)(2,1)S(1)} %merge.4), channel_id=1, source_target_pairs={{0,2},{1,3},{2,0},{3,1},{4,6},{5,7},{6,4},{7,5},{8,10},{9,11},{10,... | collective-permute-start | bytes 1179656 | tf_op jit(solution)/shard_map/ppermute | solution.py:637
  36.9 3.2 %late_share.1 = (bf16[192,1024]{1,0:T(8,128)(2,1)S(1)}, f32[192,1024]{1,0:T(8,128)S(1)}) custom-call(s32[1]{0:T(128)} %bitcast.lane_position._, bf16[192,1024]{1,0:T(8,128)(2,1)S(1)} %get-tuple-element.56.gated_ref, bf16[1024,8192]{1,0:T(8,128)(2,1)} %out_ref.7), custom_call_target="tpu_custom_call" | custom-call | flops 805306368 | bytes 4194304 | tf_op jit(solution)/shard_map/late_share/pallas_call | solution.py:523
  40.2 0.3 collective-permute-start.2
  40.5 0.0 collective-permute-done.5.other_ref
  40.5 0.1 halves.1
  40.5 0.5 collective-permute-start.8
  41.1 0.0 collective-permute-done.10.rest_1_
  41.1 0.1 merge.6.rest_0_
  41.1 6.2 %collective-permute-done.4.near_ref.rest_1_ = bf16[192,1024]{1,0:T(8,128)(2,1)S(1)} collective-permute-done((bf16[192,1024]{1,0:T(8,128)(2,1)S(1)}, bf16[192,1024]{1,0:T(8,128)(2,1)S(1)}, u32[]{:S(2)}, u32[]{:S(2)}) %collective-permute-start.4) | collective-permute-done | bytes 393248 | tf_op jit(solution)/shard_map/ppermute | solution.py:637
  47.3 0.1 merge.7
  47.4 0.1 collective-permute-start.11
  47.5 1.3 %collective-permute-start.7 = (bf16[96,1024]{1,0:T(8,128)(2,1)S(1)}, bf16[96,1024]{1,0:T(8,128)(2,1)S(1)}, u32[]{:S(2)}, u32[]{:S(2)}) collective-permute-start(bf16[96,1024]{1,0:T(8,128)(2,1)S(1)} %get-tuple-element.64), channel_id=1, source_target_pairs={{0,4},{1,5},{6,2},{7,3},{8,12},{9,13},{14,10},{15,11},{16,20},{17,... | collective-permute-start | bytes 589832 | tf_op jit(solution)/shard_map/ppermute | solution.py:641
  48.8 4.9 %collective-permute-start.6 = (bf16[96,1024]{1,0:T(8,128)(2,1)S(1)}, bf16[96,1024]{1,0:T(8,128)(2,1)S(1)}, u32[]{:S(2)}, u32[]{:S(2)}) collective-permute-start(bf16[96,1024]{1,0:T(8,128)(2,1)S(1)} %get-tuple-element.64), channel_id=1, source_target_pairs={{2,4},{3,5},{4,2},{5,3},{10,12},{11,13},{12,10},{13,11},{18,20},{1... | collective-permute-start | bytes 589832 | tf_op jit(solution)/shard_map/ppermute | solution.py:640
  53.7 3.8 %collective-permute-done.8.rest_1_ = bf16[96,1024]{1,0:T(8,128)(2,1)S(1)} collective-permute-done((bf16[96,1024]{1,0:T(8,128)(2,1)S(1)}, bf16[96,1024]{1,0:T(8,128)(2,1)S(1)}, u32[]{:S(2)}, u32[]{:S(2)}) %collective-permute-start.8) | collective-permute-done | bytes 196640 | tf_op jit(solution)/shard_map/ppermute | solution.py:639
  57.6 1.9 %collective-permute-start.9 = (bf16[96,1024]{1,0:T(8,128)(2,1)S(1)}, bf16[96,1024]{1,0:T(8,128)(2,1)S(1)}, u32[]{:S(2)}, u32[]{:S(2)}) collective-permute-start(bf16[96,1024]{1,0:T(8,128)(2,1)S(1)} %merge.5), channel_id=1, source_target_pairs={{2,4},{3,5},{4,2},{5,3},{10,12},{11,13},{12,10},{13,11},{18,20},{1... | collective-permute-start | bytes 589832 | tf_op jit(solution)/shard_map/ppermute | solution.py:648
  59.5 0.0 collective-permute-done.2.other_ref
  59.6 4.1 %collective-permute-done.7.end_ref = bf16[96,1024]{1,0:T(8,128)(2,1)S(1)} collective-permute-done((bf16[96,1024]{1,0:T(8,128)(2,1)S(1)}, bf16[96,1024]{1,0:T(8,128)(2,1)S(1)}, u32[]{:S(2)}, u32[]{:S(2)}) %collective-permute-start.7) | collective-permute-done | bytes 196640 | tf_op jit(solution)/shard_map/ppermute | solution.py:641
  63.7 5.2 %collective-permute-done.6.middle_ref = bf16[96,1024]{1,0:T(8,128)(2,1)S(1)} collective-permute-done((bf16[96,1024]{1,0:T(8,128)(2,1)S(1)}, bf16[96,1024]{1,0:T(8,128)(2,1)S(1)}, u32[]{:S(2)}, u32[]{:S(2)}) %collective-permute-start.6) | collective-permute-done | bytes 196640 | tf_op jit(solution)/shard_map/ppermute | solution.py:640
  68.9 2.4 %collective-permute-done.9.again_ref = bf16[96,1024]{1,0:T(8,128)(2,1)S(1)} collective-permute-done((bf16[96,1024]{1,0:T(8,128)(2,1)S(1)}, bf16[96,1024]{1,0:T(8,128)(2,1)S(1)}, u32[]{:S(2)}, u32[]{:S(2)}) %collective-permute-start.9) | collective-permute-done | bytes 196640 | tf_op jit(solution)/shard_map/ppermute | solution.py:648
  71.4 0.2 gather_own.1
  71.6 0.0 collective-permute-done.11
  71.6 0.8 %add_convert_fusion = bf16[192,1024]{1,0:T(8,128)(2,1)} fusion(f32[192,1024]{1,0:T(8,128)S(1)} %gather_own.1, bf16[192,1024]{1,0:T(8,128)(2,1)S(1)} %collective-permute-done.11), kind=kLoop, calls=%fused_computation | loop fusion | flops 589824 | bytes 1572864 | tf_op jit(solution)/shard_map/convert_element_type | solution.py:559
  (1 shorter events, 0.0 us)
Async XLA Ops:
  19.8 4.3 %collective-permute-start = (bf16[32,1024]{1,0:T(8,128)(2,1)S(1)}, bf16[32,1024]{1,0:T(8,128)(2,1)S(1)}, u32[]{:S(2)}, u32[]{:S(2)}) collective-permute-start(bf16[32,1024]{1,0:T(8,128)(2,1)S(1)} %get-tuple-element.37._.mine_ref.block_ref), channel_id=1, source_target_pairs={{0,8},{8,0},{16,24},{24,16},{1,9},{9,1},{17,25},{25,17},{2,10},{10... | collective-permute-start | bytes 196616 | tf_op jit(solution)/shard_map/ppermute | solution.py:750
  21.3 2.8 %copy-start = (s32[768]{0:T(1024)S(1)}, s32[768]{0:T(1024)}, u32[]{:S(2)}) copy-start(s32[768]{0:T(1024)} %ids_ref.3) | copy-start | bytes 9220
  24.8 4.3 %collective-permute-start.1 = (bf16[32,1024]{1,0:T(8,128)(2,1)S(1)}, bf16[32,1024]{1,0:T(8,128)(2,1)S(1)}, u32[]{:S(2)}, u32[]{:S(2)}) collective-permute-start(bf16[32,1024]{1,0:T(8,128)(2,1)S(1)} %join.1._), channel_id=1, source_target_pairs={{0,16},{8,24},{16,0},{24,8},{1,17},{9,25},{17,1},{25,9},{2,18},{10... | collective-permute-start | bytes 196616 | tf_op jit(solution)/shard_map/ppermute | solution.py:750
  32.0 3.2 %collective-permute-start.3 = (bf16[192,1024]{1,0:T(8,128)(2,1)S(1)}, bf16[192,1024]{1,0:T(8,128)(2,1)S(1)}, u32[]{:S(2)}, u32[]{:S(2)}) collective-permute-start(bf16[192,1024]{1,0:T(8,128)(2,1)S(1)} %get-tuple-element.61), channel_id=1, source_target_pairs={{0,1},{1,0},{2,3},{3,2},{4,5},{5,4},{6,7},{7,6},{8,9},{9,8},{10,11... | collective-permute-start | bytes 1179656 | tf_op jit(solution)/shard_map/ppermute | solution.py:634
  33.5 6.9 %collective-permute-start.5 = (bf16[192,1024]{1,0:T(8,128)(2,1)S(1)}, bf16[192,1024]{1,0:T(8,128)(2,1)S(1)}, u32[]{:S(2)}, u32[]{:S(2)}) collective-permute-start(bf16[192,1024]{1,0:T(8,128)(2,1)S(1)} %get-tuple-element.63), channel_id=1, source_target_pairs={{0,1},{1,0},{2,3},{3,2},{4,5},{5,4},{6,7},{7,6},{8,9},{9,8},{10,11... | collective-permute-start | bytes 1179656 | tf_op jit(solution)/shard_map/ppermute | solution.py:638
  35.1 5.9 %collective-permute-start.10 = (bf16[192,1024]{1,0:T(8,128)(2,1)S(1)}, bf16[192,1024]{1,0:T(8,128)(2,1)S(1)}, u32[]{:S(2)}, u32[]{:S(2)}) collective-permute-start(bf16[192,1024]{1,0:T(8,128)(2,1)S(1)} %get-tuple-element.68), channel_id=1, source_target_pairs={{0,1},{1,0},{2,3},{3,2},{4,5},{5,4},{6,7},{7,6},{8,9},{9,8},{10,11... | collective-permute-start | bytes 1179656 | tf_op jit(solution)/shard_map/ppermute | solution.py:643
  35.3 12.1 %collective-permute-start.4 = (bf16[192,1024]{1,0:T(8,128)(2,1)S(1)}, bf16[192,1024]{1,0:T(8,128)(2,1)S(1)}, u32[]{:S(2)}, u32[]{:S(2)}) collective-permute-start(bf16[192,1024]{1,0:T(8,128)(2,1)S(1)} %merge.4), channel_id=1, source_target_pairs={{0,2},{1,3},{2,0},{3,1},{4,6},{5,7},{6,4},{7,5},{8,10},{9,11},{10,... | collective-permute-start | bytes 1179656 | tf_op jit(solution)/shard_map/ppermute | solution.py:637
  40.2 19.4 %collective-permute-start.2 = (bf16[192,1024]{1,0:T(8,128)(2,1)S(1)}, bf16[192,1024]{1,0:T(8,128)(2,1)S(1)}, u32[]{:S(2)}, u32[]{:S(2)}) collective-permute-start(bf16[192,1024]{1,0:T(8,128)(2,1)S(1)} %get-tuple-element.58), channel_id=1, source_target_pairs={{0,1},{1,0},{2,3},{3,2},{4,5},{5,4},{6,7},{7,6},{8,9},{9,8},{10,11... | collective-permute-start | bytes 1179656 | tf_op jit(solution)/shard_map/ppermute | solution.py:649
  40.5 17.0 %collective-permute-start.8 = (bf16[96,1024]{1,0:T(8,128)(2,1)S(1)}, bf16[96,1024]{1,0:T(8,128)(2,1)S(1)}, u32[]{:S(2)}, u32[]{:S(2)}) collective-permute-start(bf16[96,1024]{1,0:T(8,128)(2,1)S(1)} %get-tuple-element.65.rest_0_), channel_id=1, source_target_pairs={{0,2},{1,3},{2,0},{3,1},{4,6},{5,7},{6,4},{7,5},{8,10},{9,11},{10,... | collective-permute-start | bytes 589832 | tf_op jit(solution)/shard_map/ppermute | solution.py:639
  47.4 24.1 %collective-permute-start.11 = (bf16[192,1024]{1,0:T(8,128)(2,1)S(1)}, bf16[192,1024]{1,0:T(8,128)(2,1)S(1)}, u32[]{:S(2)}, u32[]{:S(2)}) collective-permute-start(bf16[192,1024]{1,0:T(8,128)(2,1)S(1)} %merge.7), channel_id=1, source_target_pairs={{0,2},{1,3},{2,6},{3,7},{6,4},{7,5},{4,0},{5,1},{8,10},{9,11},{10,... | collective-permute-start | bytes 1179656 | tf_op jit(solution)/shard_map/ppermute | solution.py:645
  47.5 16.2 %collective-permute-start.7 = (bf16[96,1024]{1,0:T(8,128)(2,1)S(1)}, bf16[96,1024]{1,0:T(8,128)(2,1)S(1)}, u32[]{:S(2)}, u32[]{:S(2)}) collective-permute-start(bf16[96,1024]{1,0:T(8,128)(2,1)S(1)} %get-tuple-element.64), channel_id=1, source_target_pairs={{0,4},{1,5},{6,2},{7,3},{8,12},{9,13},{14,10},{15,11},{16,20},{17,... | collective-permute-start | bytes 589832 | tf_op jit(solution)/shard_map/ppermute | solution.py:641
  48.8 20.1 %collective-permute-start.6 = (bf16[96,1024]{1,0:T(8,128)(2,1)S(1)}, bf16[96,1024]{1,0:T(8,128)(2,1)S(1)}, u32[]{:S(2)}, u32[]{:S(2)}) collective-permute-start(bf16[96,1024]{1,0:T(8,128)(2,1)S(1)} %get-tuple-element.64), channel_id=1, source_target_pairs={{2,4},{3,5},{4,2},{5,3},{10,12},{11,13},{12,10},{13,11},{18,20},{1... | collective-permute-start | bytes 589832 | tf_op jit(solution)/shard_map/ppermute | solution.py:640
  57.6 13.7 %collective-permute-start.9 = (bf16[96,1024]{1,0:T(8,128)(2,1)S(1)}, bf16[96,1024]{1,0:T(8,128)(2,1)S(1)}, u32[]{:S(2)}, u32[]{:S(2)}) collective-permute-start(bf16[96,1024]{1,0:T(8,128)(2,1)S(1)} %merge.5), channel_id=1, source_target_pairs={{2,4},{3,5},{4,2},{5,3},{10,12},{11,13},{12,10},{13,11},{18,20},{1... | collective-permute-start | bytes 589832 | tf_op jit(solution)/shard_map/ppermute | solution.py:648

commit v10 on v9

--- a/solution.py
+++ b/solution.py
@@ -137,7 +137,7 @@
                 return tuple(sums[n] * leap[n] + p for n in range(poles))
 
             sums = lax.fori_loop(
-                0, T // 8, eight, tuple(jnp.zeros((8, 128), f32) for _ in range(poles)), unroll=4)
+                0, T // 8, eight, tuple(jnp.zeros((8, 128), f32) for _ in range(poles)), unroll=T // 8)
             ends = [
                 jnp.sum(sums[n] * jnp.exp(-back * r16[n : n + 1]), axis=0, keepdims=True) for n in range(poles)
             ]
@@ -635,7 +635,8 @@
     first_mine, send, mine = second_shares(lane_position, gated, *windows, width)
     far = merge(lane_position, bf16, (first_mine, traded))
     from_near = lax.ppermute(far, "mp", near)
-    top, bottom = halves(lane_position, mine, lax.ppermute(send, "mp", pair))
+    traded = lax.ppermute(send, "mp", pair)
+    top, bottom = halves(lane_position, mine, traded)
     beside = lax.ppermute(bottom, "mp", near)
     from_middle = lax.ppermute(top, "mp", along([(1, 2), (2, 1)]))
     from_end = lax.ppermute(top, "mp", along([(0, 2), (3, 1)]))

time: 72.6 us -> 72.2 us (level)
  no operation moved by 1% of the time
where the time goes in v10:
time: 72.2 us; the launch traced here: 72 us
  Pallas kernels  33.6 us (47%)
  waiting for transfers between devices  22.9 us (32%)
  starting transfers between devices  14.5 us (20%)
  other arithmetic  0.84 us (1%)
    pallas_call x1, Pallas kernels, front(): pl.pallas_call(functools.partial(front_kernel, geometry), out_shape=[jax....  19.4 us
    ppermute x1, waiting for transfers between devices, scatter_line(): from_near = lax.ppermute(far, 'mp', near)  6.21 us
    ppermute x1, waiting for transfers between devices, scatter_line(): from_middle = lax.ppermute(top, 'mp', along([(1, 2), (2, 1)]))  5.22 us
    ppermute x1, starting transfers between devices, scatter_line(): from_middle = lax.ppermute(top, 'mp', along([(1, 2), (2, 1)]))  4.92 us
    pallas_call x2, Pallas kernels, local_pass(): pl.pallas_call(functools.partial(local_kernel, poles, first, slot), out_s...  4.45 us
    ppermute x1, waiting for transfers between devices, scatter_line(): from_end = lax.ppermute(top, 'mp', along([(0, 2), (3, 1)]))  4.15 us
    ppermute x1, waiting for transfers between devices, scatter_line(): beside = lax.ppermute(bottom, 'mp', near)  3.83 us
    pallas_call x1, Pallas kernels, late_share(): pl.pallas_call(functools.partial(late_share_kernel, slot), out_shape=[jax...  3.25 us
  transfers between devices with their start and end apart: 12, of which 7 were waited for; matrix products, arithmetic and copies ran while one was open for 0% of the time, Pallas kernels for 15%

profile of v10, /device:TPU:16, one launch (start us, length us, event | category | flops | bytes accessed | tf_op | source)
XLA Modules:
  0.0 72.0 jit_solution(8282269513958021242)
XLA Ops:
  0.0 19.4 %front.1 = (f32[200,1024]{1,0:T(8,128)S(1)}, f32[8,192,128]{2,1,0:T(8,128)S(1)}, bf16[32,1024]{1,0:T(8,128)(2,1)S(1)}, f32[192,128]{1,0:T(8,128)S(1)}, f32[192,1...) custom-call(s32[1]{0:T(128)} %bitcast.1.position, ...), custom_call_target="tpu_custom_call" | custom-call | tf_op jit(solution)/shard_map/front/pallas_call | solution.py:178
  19.4 1.6 %collective-permute-start = (bf16[32,1024]{1,0:T(8,128)(2,1)S(1)}, bf16[32,1024]{1,0:T(8,128)(2,1)S(1)}, u32[]{:S(2)}, u32[]{:S(2)}) collective-permute-start(bf16[32,1024]{1,0:T(8,128)(2,1)S(1)} %get-tuple-element.37._.mine_ref.block_ref), channel_id=1, source_target_pairs={{0,8},{8,0},{16,24},{24,16},{1,9},{9,1},{17,25},{25,17},{2,10},{10... | collective-permute-start | bytes 196616 | tf_op jit(solution)/shard_map/ppermute | solution.py:751
  20.9 0.0 copy-start
  20.9 2.2 %local_pass.2 = (f32[4,192,128]{2,1,0:T(8,128)S(1)}, f32[4,128,128]{2,1,0:T(8,128)S(1)}, f32[16,512]{1,0:T(8,128)S(1)}, f32[4,192,128]{2,1,0:T(8,128)S(1)}, bf16[1024,2048]{1,0:T(8,128)(2,1)S(1)}) custom-call(s32[1]{0:T(128)} %bitcast.lane_position._, f32[8,192,128]{2,1,0:T(8,128)S(1)} %get-tuple-element.42.prod_ref, ...), custom_call_target="tpu_custom_call" | custom-call | flops 9437184 | bytes 8388608 | tf_op jit(solution)/shard_map/local_pass/pallas_call | solution.py:268
  23.2 0.5 collective-permute-done.other_ref.rest_0_
  23.7 0.0 copy-done
  23.7 0.7 join.1._
  24.4 1.6 %collective-permute-start.1 = (bf16[32,1024]{1,0:T(8,128)(2,1)S(1)}, bf16[32,1024]{1,0:T(8,128)(2,1)S(1)}, u32[]{:S(2)}, u32[]{:S(2)}) collective-permute-start(bf16[32,1024]{1,0:T(8,128)(2,1)S(1)} %join.1._), channel_id=1, source_target_pairs={{0,16},{8,24},{16,0},{24,8},{1,17},{9,25},{17,1},{25,9},{2,18},{10... | collective-permute-start | bytes 196616 | tf_op jit(solution)/shard_map/ppermute | solution.py:751
  26.0 2.2 %local_pass.3 = (f32[4,192,128]{2,1,0:T(8,128)S(1)}, f32[4,128,128]{2,1,0:T(8,128)S(1)}, f32[16,512]{1,0:T(8,128)S(1)}, f32[4,192,128]{2,1,0:T(8,128)S(1)}, bf16[1024,2048]{1,0:T(8,128)(2,1)S(1)}) custom-call(s32[1]{0:T(128)} %bitcast.lane_position._, f32[8,192,128]{2,1,0:T(8,128)S(1)} %get-tuple-element.42.prod_ref, ...), custom_call_target="tpu_custom_call" | custom-call | flops 9437184 | bytes 8388608 | tf_op jit(solution)/shard_map/local_pass/pallas_call | solution.py:268
  28.2 0.5 collective-permute-done.1.rest_1_
  28.7 2.8 %gate.1 = (bf16[192,1024]{1,0:T(8,128)(2,1)S(1)}, bf16[192,1024]{1,0:T(8,128)(2,1)S(1)}, bf16[1024,2048]{1,0:T(8,128)(2,1)S(1)}) custom-call(s32[1]{0:T(128)} %bitcast.1.position, s32[1]{0:T(128)} %bitcast.lane_position._, s32[768]{0:T(1024)S(1)} %copy-done, bf16[32,1024]{1,0:T(8,128)(2,1)S(1)} %get-tuple-element.37._.mine_ref.block_ref, ...), custom_call_target="tpu_custom_call" | custom-call | tf_op jit(solution)/shard_map/gate/pallas_call | solution.py:538
  31.6 0.1 collective-permute-start.3
  31.7 1.5 %second_shares.1 = (f32[192,1024]{1,0:T(8,128)S(1)}, bf16[192,1024]{1,0:T(8,128)(2,1)S(1)}, f32[192,1024]{1,0:T(8,128)S(1)}) custom-call(s32[1]{0:T(128)} %bitcast.lane_position._, bf16[192,1024]{1,0:T(8,128)(2,1)S(1)} %get-tuple-element.56.gated_ref, bf16[1024,2048]{1,0:T(8,128)(2,1)S(1)} %get-tuple-element.47.window_ref.first_ref, ...), custom_call_target="tpu_custom_call" | custom-call | flops 1207959552 | bytes 6291456 | tf_op jit(solution)/shard_map/second_shares/pallas_call | solution.py:502
  33.1 0.5 collective-permute-start.5
  33.7 1.0 %shares.1 = (bf16[192,1024]{1,0:T(8,128)(2,1)S(1)}, f32[192,1024]{1,0:T(8,128)S(1)}) custom-call(s32[1]{0:T(128)} %bitcast.lane_position._, bf16[192,1024]{1,0:T(8,128)(2,1)S(1)} %get-tuple-element.56.gated_ref, bf16[1024,2048]{1,0:T(8,128)(2,1)S(1)} %get-tuple-element.66.rest_0_), custom_call_target="tpu_custom_call" | custom-call | flops 805306368 | bytes 4194304 | tf_op jit(solution)/shard_map/shares/pallas_call | solution.py:483
  34.7 0.1 collective-permute-start.10
  34.8 0.0 collective-permute-done.3.rest_1_
  34.8 0.1 merge.4
  34.9 1.6 %collective-permute-start.4 = (bf16[192,1024]{1,0:T(8,128)(2,1)S(1)}, bf16[192,1024]{1,0:T(8,128)(2,1)S(1)}, u32[]{:S(2)}, u32[]{:S(2)}) collective-permute-start(bf16[192,1024]{1,0:T(8,128)(2,1)S(1)} %merge.4), channel_id=1, source_target_pairs={{0,2},{1,3},{2,0},{3,1},{4,6},{5,7},{6,4},{7,5},{8,10},{9,11},{10,... | collective-permute-start | bytes 1179656 | tf_op jit(solution)/shard_map/ppermute | solution.py:637
  36.5 3.2 %late_share.1 = (bf16[192,1024]{1,0:T(8,128)(2,1)S(1)}, f32[192,1024]{1,0:T(8,128)S(1)}) custom-call(s32[1]{0:T(128)} %bitcast.lane_position._, bf16[192,1024]{1,0:T(8,128)(2,1)S(1)} %get-tuple-element.56.gated_ref, bf16[1024,8192]{1,0:T(8,128)(2,1)} %out_ref.7), custom_call_target="tpu_custom_call" | custom-call | flops 805306368 | bytes 4194304 | tf_op jit(solution)/shard_map/late_share/pallas_call | solution.py:523
  39.8 0.3 collective-permute-start.2
  40.0 0.0 collective-permute-done.5.other_ref
  40.0 0.1 halves.1
  40.1 0.5 collective-permute-start.8
  40.6 0.0 collective-permute-done.10.rest_1_
  40.6 0.1 merge.6.rest_0_
  40.7 6.2 %collective-permute-done.4.near_ref.rest_1_ = bf16[192,1024]{1,0:T(8,128)(2,1)S(1)} collective-permute-done((bf16[192,1024]{1,0:T(8,128)(2,1)S(1)}, bf16[192,1024]{1,0:T(8,128)(2,1)S(1)}, u32[]{:S(2)}, u32[]{:S(2)}) %collective-permute-start.4) | collective-permute-done | bytes 393248 | tf_op jit(solution)/shard_map/ppermute | solution.py:637
  46.9 0.1 merge.7
  47.0 0.1 collective-permute-start.11
  47.1 1.3 %collective-permute-start.7 = (bf16[96,1024]{1,0:T(8,128)(2,1)S(1)}, bf16[96,1024]{1,0:T(8,128)(2,1)S(1)}, u32[]{:S(2)}, u32[]{:S(2)}) collective-permute-start(bf16[96,1024]{1,0:T(8,128)(2,1)S(1)} %get-tuple-element.64), channel_id=1, source_target_pairs={{0,4},{1,5},{6,2},{7,3},{8,12},{9,13},{14,10},{15,11},{16,20},{17,... | collective-permute-start | bytes 589832 | tf_op jit(solution)/shard_map/ppermute | solution.py:642
  48.4 4.9 %collective-permute-start.6 = (bf16[96,1024]{1,0:T(8,128)(2,1)S(1)}, bf16[96,1024]{1,0:T(8,128)(2,1)S(1)}, u32[]{:S(2)}, u32[]{:S(2)}) collective-permute-start(bf16[96,1024]{1,0:T(8,128)(2,1)S(1)} %get-tuple-element.64), channel_id=1, source_target_pairs={{2,4},{3,5},{4,2},{5,3},{10,12},{11,13},{12,10},{13,11},{18,20},{1... | collective-permute-start | bytes 589832 | tf_op jit(solution)/shard_map/ppermute | solution.py:641
  53.3 3.8 %collective-permute-done.8.rest_1_ = bf16[96,1024]{1,0:T(8,128)(2,1)S(1)} collective-permute-done((bf16[96,1024]{1,0:T(8,128)(2,1)S(1)}, bf16[96,1024]{1,0:T(8,128)(2,1)S(1)}, u32[]{:S(2)}, u32[]{:S(2)}) %collective-permute-start.8) | collective-permute-done | bytes 196640 | tf_op jit(solution)/shard_map/ppermute | solution.py:640
  57.2 1.9 %collective-permute-start.9 = (bf16[96,1024]{1,0:T(8,128)(2,1)S(1)}, bf16[96,1024]{1,0:T(8,128)(2,1)S(1)}, u32[]{:S(2)}, u32[]{:S(2)}) collective-permute-start(bf16[96,1024]{1,0:T(8,128)(2,1)S(1)} %merge.5), channel_id=1, source_target_pairs={{2,4},{3,5},{4,2},{5,3},{10,12},{11,13},{12,10},{13,11},{18,20},{1... | collective-permute-start | bytes 589832 | tf_op jit(solution)/shard_map/ppermute | solution.py:649
  59.1 0.0 collective-permute-done.2.other_ref
  59.1 4.1 %collective-permute-done.7.end_ref = bf16[96,1024]{1,0:T(8,128)(2,1)S(1)} collective-permute-done((bf16[96,1024]{1,0:T(8,128)(2,1)S(1)}, bf16[96,1024]{1,0:T(8,128)(2,1)S(1)}, u32[]{:S(2)}, u32[]{:S(2)}) %collective-permute-start.7) | collective-permute-done | bytes 196640 | tf_op jit(solution)/shard_map/ppermute | solution.py:642
  63.3 5.2 %collective-permute-done.6.middle_ref = bf16[96,1024]{1,0:T(8,128)(2,1)S(1)} collective-permute-done((bf16[96,1024]{1,0:T(8,128)(2,1)S(1)}, bf16[96,1024]{1,0:T(8,128)(2,1)S(1)}, u32[]{:S(2)}, u32[]{:S(2)}) %collective-permute-start.6) | collective-permute-done | bytes 196640 | tf_op jit(solution)/shard_map/ppermute | solution.py:641
  68.5 2.4 %collective-permute-done.9.again_ref = bf16[96,1024]{1,0:T(8,128)(2,1)S(1)} collective-permute-done((bf16[96,1024]{1,0:T(8,128)(2,1)S(1)}, bf16[96,1024]{1,0:T(8,128)(2,1)S(1)}, u32[]{:S(2)}, u32[]{:S(2)}) %collective-permute-start.9) | collective-permute-done | bytes 196640 | tf_op jit(solution)/shard_map/ppermute | solution.py:649
  70.9 0.2 gather_own.1
  71.2 0.0 collective-permute-done.11
  71.2 0.8 %add_convert_fusion = bf16[192,1024]{1,0:T(8,128)(2,1)} fusion(f32[192,1024]{1,0:T(8,128)S(1)} %gather_own.1, bf16[192,1024]{1,0:T(8,128)(2,1)S(1)} %collective-permute-done.11), kind=kLoop, calls=%fused_computation | loop fusion | flops 589824 | bytes 1572864 | tf_op jit(solution)/shard_map/convert_element_type | solution.py:559
  (1 shorter events, 0.0 us)
Async XLA Ops:
  19.4 4.3 %collective-permute-start = (bf16[32,1024]{1,0:T(8,128)(2,1)S(1)}, bf16[32,1024]{1,0:T(8,128)(2,1)S(1)}, u32[]{:S(2)}, u32[]{:S(2)}) collective-permute-start(bf16[32,1024]{1,0:T(8,128)(2,1)S(1)} %get-tuple-element.37._.mine_ref.block_ref), channel_id=1, source_target_pairs={{0,8},{8,0},{16,24},{24,16},{1,9},{9,1},{17,25},{25,17},{2,10},{10... | collective-permute-start | bytes 196616 | tf_op jit(solution)/shard_map/ppermute | solution.py:751
  20.9 2.8 %copy-start = (s32[768]{0:T(1024)S(1)}, s32[768]{0:T(1024)}, u32[]{:S(2)}) copy-start(s32[768]{0:T(1024)} %ids_ref.3) | copy-start | bytes 9220
  24.4 4.3 %collective-permute-start.1 = (bf16[32,1024]{1,0:T(8,128)(2,1)S(1)}, bf16[32,1024]{1,0:T(8,128)(2,1)S(1)}, u32[]{:S(2)}, u32[]{:S(2)}) collective-permute-start(bf16[32,1024]{1,0:T(8,128)(2,1)S(1)} %join.1._), channel_id=1, source_target_pairs={{0,16},{8,24},{16,0},{24,8},{1,17},{9,25},{17,1},{25,9},{2,18},{10... | collective-permute-start | bytes 196616 | tf_op jit(solution)/shard_map/ppermute | solution.py:751
  31.6 3.2 %collective-permute-start.3 = (bf16[192,1024]{1,0:T(8,128)(2,1)S(1)}, bf16[192,1024]{1,0:T(8,128)(2,1)S(1)}, u32[]{:S(2)}, u32[]{:S(2)}) collective-permute-start(bf16[192,1024]{1,0:T(8,128)(2,1)S(1)} %get-tuple-element.61), channel_id=1, source_target_pairs={{0,1},{1,0},{2,3},{3,2},{4,5},{5,4},{6,7},{7,6},{8,9},{9,8},{10,11... | collective-permute-start | bytes 1179656 | tf_op jit(solution)/shard_map/ppermute | solution.py:634
  33.1 6.9 %collective-permute-start.5 = (bf16[192,1024]{1,0:T(8,128)(2,1)S(1)}, bf16[192,1024]{1,0:T(8,128)(2,1)S(1)}, u32[]{:S(2)}, u32[]{:S(2)}) collective-permute-start(bf16[192,1024]{1,0:T(8,128)(2,1)S(1)} %get-tuple-element.63), channel_id=1, source_target_pairs={{0,1},{1,0},{2,3},{3,2},{4,5},{5,4},{6,7},{7,6},{8,9},{9,8},{10,11... | collective-permute-start | bytes 1179656 | tf_op jit(solution)/shard_map/ppermute | solution.py:638
  34.7 5.9 %collective-permute-start.10 = (bf16[192,1024]{1,0:T(8,128)(2,1)S(1)}, bf16[192,1024]{1,0:T(8,128)(2,1)S(1)}, u32[]{:S(2)}, u32[]{:S(2)}) collective-permute-start(bf16[192,1024]{1,0:T(8,128)(2,1)S(1)} %get-tuple-element.68), channel_id=1, source_target_pairs={{0,1},{1,0},{2,3},{3,2},{4,5},{5,4},{6,7},{7,6},{8,9},{9,8},{10,11... | collective-permute-start | bytes 1179656 | tf_op jit(solution)/shard_map/ppermute | solution.py:644
  34.9 12.1 %collective-permute-start.4 = (bf16[192,1024]{1,0:T(8,128)(2,1)S(1)}, bf16[192,1024]{1,0:T(8,128)(2,1)S(1)}, u32[]{:S(2)}, u32[]{:S(2)}) collective-permute-start(bf16[192,1024]{1,0:T(8,128)(2,1)S(1)} %merge.4), channel_id=1, source_target_pairs={{0,2},{1,3},{2,0},{3,1},{4,6},{5,7},{6,4},{7,5},{8,10},{9,11},{10,... | collective-permute-start | bytes 1179656 | tf_op jit(solution)/shard_map/ppermute | solution.py:637
  39.8 19.4 %collective-permute-start.2 = (bf16[192,1024]{1,0:T(8,128)(2,1)S(1)}, bf16[192,1024]{1,0:T(8,128)(2,1)S(1)}, u32[]{:S(2)}, u32[]{:S(2)}) collective-permute-start(bf16[192,1024]{1,0:T(8,128)(2,1)S(1)} %get-tuple-element.58), channel_id=1, source_target_pairs={{0,1},{1,0},{2,3},{3,2},{4,5},{5,4},{6,7},{7,6},{8,9},{9,8},{10,11... | collective-permute-start | bytes 1179656 | tf_op jit(solution)/shard_map/ppermute | solution.py:650
  40.1 17.0 %collective-permute-start.8 = (bf16[96,1024]{1,0:T(8,128)(2,1)S(1)}, bf16[96,1024]{1,0:T(8,128)(2,1)S(1)}, u32[]{:S(2)}, u32[]{:S(2)}) collective-permute-start(bf16[96,1024]{1,0:T(8,128)(2,1)S(1)} %get-tuple-element.65.rest_0_), channel_id=1, source_target_pairs={{0,2},{1,3},{2,0},{3,1},{4,6},{5,7},{6,4},{7,5},{8,10},{9,11},{10,... | collective-permute-start | bytes 589832 | tf_op jit(solution)/shard_map/ppermute | solution.py:640
  47.0 24.1 %collective-permute-start.11 = (bf16[192,1024]{1,0:T(8,128)(2,1)S(1)}, bf16[192,1024]{1,0:T(8,128)(2,1)S(1)}, u32[]{:S(2)}, u32[]{:S(2)}) collective-permute-start(bf16[192,1024]{1,0:T(8,128)(2,1)S(1)} %merge.7), channel_id=1, source_target_pairs={{0,2},{1,3},{2,6},{3,7},{6,4},{7,5},{4,0},{5,1},{8,10},{9,11},{10,... | collective-permute-start | bytes 1179656 | tf_op jit(solution)/shard_map/ppermute | solution.py:646
  47.1 16.2 %collective-permute-start.7 = (bf16[96,1024]{1,0:T(8,128)(2,1)S(1)}, bf16[96,1024]{1,0:T(8,128)(2,1)S(1)}, u32[]{:S(2)}, u32[]{:S(2)}) collective-permute-start(bf16[96,1024]{1,0:T(8,128)(2,1)S(1)} %get-tuple-element.64), channel_id=1, source_target_pairs={{0,4},{1,5},{6,2},{7,3},{8,12},{9,13},{14,10},{15,11},{16,20},{17,... | collective-permute-start | bytes 589832 | tf_op jit(solution)/shard_map/ppermute | solution.py:642
  48.4 20.1 %collective-permute-start.6 = (bf16[96,1024]{1,0:T(8,128)(2,1)S(1)}, bf16[96,1024]{1,0:T(8,128)(2,1)S(1)}, u32[]{:S(2)}, u32[]{:S(2)}) collective-permute-start(bf16[96,1024]{1,0:T(8,128)(2,1)S(1)} %get-tuple-element.64), channel_id=1, source_target_pairs={{2,4},{3,5},{4,2},{5,3},{10,12},{11,13},{12,10},{13,11},{18,20},{1... | collective-permute-start | bytes 589832 | tf_op jit(solution)/shard_map/ppermute | solution.py:641
  57.2 13.7 %collective-permute-start.9 = (bf16[96,1024]{1,0:T(8,128)(2,1)S(1)}, bf16[96,1024]{1,0:T(8,128)(2,1)S(1)}, u32[]{:S(2)}, u32[]{:S(2)}) collective-permute-start(bf16[96,1024]{1,0:T(8,128)(2,1)S(1)} %merge.5), channel_id=1, source_target_pairs={{2,4},{3,5},{4,2},{5,3},{10,12},{11,13},{12,10},{13,11},{18,20},{1... | collective-permute-start | bytes 589832 | tf_op jit(solution)/shard_map/ppermute | solution.py:649
